TPU v7x, 32 devices: a whole 2x2x4 slice. The times are simulated.
32 devices in a mesh: seq: 4 (over y, x), tp: 8 (over z, core).
Axes of the slice: x: 2, y: 2, z: 4, core: 2. Of those that a mesh axis runs over, the one named last changes fastest.
Arguments:
- tokens: bfloat16 [4096, 4096], P('seq'), may hold values from -32 to 32
- w_query: bfloat16 [4096, 2048], P(None, 'tp'), may hold values from -0.109375 to 0.109375
- w_key: bfloat16 [4096, 512], P(None, 'tp'), may hold values from -0.078125 to 0.078125
- w_value: bfloat16 [4096, 512], P(None, 'tp'), may hold values from -0.09375 to 0.09375
- w_out: bfloat16 [2048, 4096], P('tp'), may hold values from -0.1875 to 0.1875
- seg_ids: int32 [4096], replicated, may hold values from 0 to 31, as said below
- owner_counts: int32 [8], replicated, may hold values from 1 to 8, 32 in all
- centroids: bfloat16 [16384, 4096], P('seq', 'tp'), may hold values from -1.5 to 1.5
- pool_gain: float32 [4096], P('tp'), may hold values from 0.1 to 1.9
- assign: int32 [32], replicated, may hold values from 0 to 16383
Outputs:
- distances: float32 [64, 16384], P('tp', 'seq')
- updated: float32 [16384, 4096], P('seq', 'tp')
Inputs may be any that keep to these rules, and one draw needn't show every extreme that they name: `seg_ids`: ids never fall along the sequence; every id occurs; one instruction spans exactly 4065 tokens. `owner_counts`: the counts sum to 32; one owner holds exactly 8 rows.
All inputs are finite; a program needn't handle non-finite values.
Results may differ from a plain program's by a relative error of at most 0.0007.
Values may be sent and summed in bfloat16 or wider, within the bound.
No kernel may reach another device: no remote copies, remote signals or barrier semaphores. Data moves between devices by JAX's collectives and lax.ppermute only.
A program may use at most 192 MiB of HBM per device.

v0:
```python
import math

import jax
import jax.numpy as jnp
from jax import lax
from jax.sharding import PartitionSpec as P

HD = 128
WINDOW = 4096
QBLOCK = 512


rope_theta = 10000.0
norm_eps = 1e-06


def from_partner(x, axis, apart):
    return lax.ppermute(x, axis, [(i, i ^ 1 << apart) for i in range(lax.axis_size(axis))])


def from_behind(value, axis, steps):
    count = lax.axis_size(axis)
    leading, last = (max(0, -steps), min(count, count - steps))
    return lax.ppermute(value, axis, [(source, source + steps) for source in range(leading, last)])


def rotate_pairs(vectors, positions, first_pair, head_size):
    cols = vectors.shape[-1]
    pair_index = (first_pair + jnp.arange(cols // 2)).astype(jnp.float32)
    inverse = jnp.exp(-(2.0 * pair_index / head_size) * math.log(rope_theta))
    angles = positions.astype(jnp.float32)[:, None] * inverse[None, :]
    cosine = jnp.cos(angles)[:, None, :]
    sine = jnp.sin(angles)[:, None, :]
    paired = vectors.reshape(vectors.shape[:-1] + (cols // 2, 2))
    even_part = paired[..., 0]
    odd_part = paired[..., 1]
    turned = jnp.stack(
        [even_part * cosine - odd_part * sine, even_part * sine + odd_part * cosine], -1
    )
    return turned.reshape(vectors.shape)


def shards(
    tokens, w_query, w_key, w_value, w_out, seg_ids, owner_counts, centroids, pool_gain, assign
):
    tok_rows, model_width = tokens.shape
    half_cols = w_key.shape[1]
    heads_here = w_query.shape[1] // HD
    rank_seq = lax.axis_index("seq")
    rank_tp = lax.axis_index("tp")
    tp_total = lax.axis_size("tp")
    positions = rank_seq * tok_rows + jnp.arange(tok_rows, dtype=jnp.int32)
    queries = rotate_pairs(
        jnp.dot(tokens, w_query, preferred_element_type=jnp.float32).reshape(
            tok_rows, heads_here, HD
        ),
        positions,
        0,
        HD,
    ).astype(jnp.bfloat16)
    lower_first = rank_tp % 2 == 0
    key_half = jnp.dot(tokens, w_key, preferred_element_type=jnp.float32).reshape(
        tok_rows, 1, half_cols
    )
    key_half = rotate_pairs(key_half, positions, rank_tp % 2 * (half_cols // 2), HD).reshape(
        tok_rows, half_cols
    )
    value_half = jnp.dot(tokens, w_value, preferred_element_type=jnp.float32)
    own_pair = jnp.concatenate([key_half.astype(jnp.bfloat16), value_half.astype(jnp.bfloat16)], -1)
    partner = from_partner(own_pair, "tp", 0)
    front = jnp.where(lower_first, own_pair, partner)
    back = jnp.where(lower_first, partner, own_pair)
    key_rows = jnp.concatenate([front[:, :half_cols], back[:, :half_cols]], -1)
    value_rows = jnp.concatenate([front[:, half_cols:], back[:, half_cols:]], -1)
    kv_local = jnp.concatenate([key_rows, value_rows], -1)
    halo_shards = WINDOW // tok_rows
    reach = min(halo_shards, lax.axis_size("seq") - 1)
    pieces = [kv_local]
    for back_step in range(1, reach + 1):
        pieces.insert(0, from_behind(kv_local, "seq", back_step))
    if halo_shards > reach:
        pieces.insert(0, jnp.zeros(((halo_shards - reach) * tok_rows, 2 * HD), jnp.bfloat16))
    kv_window = jnp.concatenate(pieces, 0)
    pad_ids = jnp.concatenate([jnp.full((WINDOW,), -1, jnp.int32), seg_ids], 0)
    distance_grid = jnp.arange(QBLOCK)[:, None] + WINDOW - jnp.arange(WINDOW + QBLOCK)[None, :]
    outputs = []
    for block_index in range(tok_rows // QBLOCK):
        q_start = block_index * QBLOCK
        q_block = queries[q_start : q_start + QBLOCK]
        kv_block = kv_window[q_start : q_start + WINDOW + QBLOCK]
        q_ids = lax.dynamic_slice_in_dim(seg_ids, rank_seq * tok_rows + q_start, QBLOCK, 0)
        k_ids = lax.dynamic_slice_in_dim(pad_ids, rank_seq * tok_rows + q_start, WINDOW + QBLOCK, 0)
        allowed = (
            (distance_grid >= 0) & (distance_grid < WINDOW) & (q_ids[:, None] == k_ids[None, :])
        )
        scores = jnp.einsum(
            "qhd,kd->hqk", q_block, kv_block[:, :HD], preferred_element_type=jnp.float32
        ) * HD ** (-0.5)
        scores = jnp.where(allowed[None], scores, -1e30)
        highest = jnp.max(scores, axis=-1, keepdims=True)
        weights = jnp.exp(scores - highest)
        soft_weights = (weights / jnp.sum(weights, axis=-1, keepdims=True)).astype(jnp.bfloat16)
        head_out = jnp.einsum(
            "hqk,kd->qhd", soft_weights, kv_block[:, HD:], preferred_element_type=jnp.float32
        ).astype(jnp.bfloat16)
        outputs.append(head_out.reshape(QBLOCK, heads_here * HD))
    attention = jnp.concatenate(outputs, 0)
    seg_total = assign.shape[0]
    member = (
        lax.dynamic_slice_in_dim(seg_ids, rank_seq * tok_rows, tok_rows, 0)[:, None]
        == jnp.arange(seg_total, dtype=jnp.int32)[None, :]
    )
    member_float = member.astype(jnp.float32)
    member_half = member.astype(jnp.bfloat16)
    feat_cols = model_width // tp_total
    token_cols = lax.dynamic_slice_in_dim(tokens, rank_tp * feat_cols, feat_cols, 1)
    pooled_tokens = lax.dot_general(
        member_half, token_cols, (((0,), (0,)), ((), ())), preferred_element_type=jnp.float32
    )
    mixed_cols = lax.psum_scatter(
        lax.dot_general(
            w_out, attention, (((0,), (1,)), ((), ())), preferred_element_type=jnp.float32
        ),
        "tp",
        scatter_dimension=0,
        tiled=True,
    )
    pooled_mixed = lax.dot_general(
        member_float, mixed_cols, (((0,), (1,)), ((), ())), precision=lax.Precision.HIGHEST
    )
    seg_sums = lax.psum(pooled_tokens + pooled_mixed, "seq")
    counts = jnp.sum(
        (seg_ids[:, None] == jnp.arange(seg_total, dtype=jnp.int32)[None, :]).astype(jnp.float32),
        axis=0,
    )
    pooled = seg_sums / counts[:, None]
    square_sums = lax.psum(jnp.sum(pooled * pooled, axis=1), "tp")
    mean_square = square_sums / model_width
    embedding = pooled * lax.rsqrt(mean_square + norm_eps)[:, None] * pool_gain[None, :]
    cross_term = lax.dot_general(
        embedding.astype(jnp.bfloat16),
        centroids,
        (((1,), (1,)), ((), ())),
        preferred_element_type=jnp.float32,
    )
    cent_float = centroids.astype(jnp.float32)
    cent_norm = jnp.sum(cent_float * cent_float, axis=1)
    row_terms = (cent_norm[None, :] - 2.0 * cross_term) / model_width**0.5
    owners = owner_counts.shape[0]
    capacity = 2 * seg_total // owners
    starts = jnp.cumsum(owner_counts) - owner_counts
    slot_index = jnp.arange(capacity, dtype=jnp.int32)
    slot_rows = (starts[:, None] + slot_index[None, :]).reshape(-1)
    slot_valid = (slot_index[None, :] < owner_counts[:, None]).reshape(-1)
    selector = (
        (slot_rows[:, None] == jnp.arange(seg_total, dtype=jnp.int32)[None, :])
        & slot_valid[:, None]
    ).astype(jnp.float32)
    slot_terms = jnp.dot(selector, row_terms, precision=lax.Precision.HIGHEST)
    distances = lax.psum_scatter(slot_terms, "tp", scatter_dimension=0, tiled=True)
    cent_rows = centroids.shape[0]
    cent_ids = rank_seq * cent_rows + jnp.arange(cent_rows, dtype=jnp.int32)
    chosen = (assign[None, :] == cent_ids[:, None]).astype(jnp.float32)
    cent_sums = jnp.dot(chosen, embedding, precision=lax.Precision.HIGHEST)
    cent_counts = jnp.sum(chosen, axis=1)
    updated = (cent_float + cent_sums) / (1.0 + cent_counts)[:, None]
    return (distances, updated)


def solution(mesh):
    in_specs = (
        P("seq", None),
        P(None, "tp"),
        P(None, "tp"),
        P(None, "tp"),
        P("tp", None),
        P(),
        P(),
        P("seq", "tp"),
        P("tp"),
        P(),
    )
    out_specs = (P("tp", "seq"), P("seq", "tp"))
    return jax.shard_map(shards, mesh=mesh, in_specs=in_specs, out_specs=out_specs, check_vma=False)
```

profile of v0, /device:TPU:0, one launch (start us, length us, event | category | flops | bytes accessed | tf_op | source)
XLA Modules:
  0.0 416.3 jit_solution(12850956107057330214)
XLA Ops:
  7.2 0.0 copy-start
  7.2 0.0 reduce-scatter.3.cloned.1.call-start
  7.3 6.3 %fusion.69 = f32[1024,64]{0,1:T(8,128)S(1)} fusion(bf16[1024,4096]{1,0:T(8,128)(2,1)} %param.10, bf16[4096,64]{0,1:T(8,128)(2,1)} %param.12), kind=kOutput, calls=%fused_computation.125 | convolution fusion | flops 536870912 | bytes 9175040 | tf_op jit(solution)/shard_map/dot_general | solution.py:62
  13.6 0.1 reshape_reshape.7
  13.7 0.2 fusion.65
  13.9 0.6 fusion.42
  14.5 0.1 copy.44
  14.7 0.1 convert_element_type.67
  14.8 6.0 %convolution_convert_fusion = bf16[1024,64]{0,1:T(8,128)(2,1)S(1)} fusion(bf16[1024,4096]{1,0:T(8,128)(2,1)} %param.10, bf16[4096,64]{0,1:T(8,128)(2,1)S(1)} %copy-done.4), kind=kOutput, calls=%fused_computation.40 | convolution fusion | flops 536936448 | bytes 9043968 | tf_op jit(solution)/shard_map/dot_general | solution.py:68
  20.8 0.7 pad_maximum_fusion.2
  21.5 0.5 collective-permute-start
  22.0 1.8 multiply_cosine_fusion
  23.8 7.3 %fusion.70 = f32[1024,256]{0,1:T(8,128)} fusion(bf16[1024,4096]{1,0:T(8,128)(2,1)} %param.10, bf16[4096,256]{1,0:T(8,128)(2,1)} %param.11), kind=kOutput, calls=%fused_computation.126 | convolution fusion | flops 2147483648 | bytes 11534336 | tf_op jit(solution)/shard_map/dot_general | solution.py:54
  31.1 1.8 reshape_reshape.8
  33.0 0.1 fusion.66
  33.1 0.1 pad_dynamic-slice_fusion.1
  33.2 7.0 %compare_and_fusion.1 = (pred[512,4608]{0,1:T(8,128)(4,1)}, pred[512,4608]{0,1:T(8,128)(4,1)}) fusion(s32[512]{0:T(512)S(1)} %get-tuple-element.20, s32[512]{0:T(512)S(1)} %get-tuple-element.32, s32[4608]{0:T(1024)S(1)} %get-tuple-element.18, s32[4608]{0:T(1024)S(1)} %get-tuple-element.19, s32[512]{0:T(512)S(1)} %get-tuple-element.21), kind=kLoop, calls=%fused_computation.23 | loop fusion | flops 18874368 | bytes 4761600 | tf_op jit(solution)/shard_map/and | solution.py:94
  40.2 0.8 fusion.62
  41.0 0.0 collective-permute-done
  41.0 1.1 broadcast_select_fusion.1
  42.2 5.4 %collective-permute-start.1 = (bf16[1024,256]{0,1:T(8,128)(2,1)S(1)}, bf16[1024,256]{0,1:T(8,128)(2,1)S(1)}, u32[]{:S(2)}, u32[]{:S(2)}) collective-permute-start(bf16[1024,256]{0,1:T(8,128)(2,1)S(1)} %pad_maximum_fusion), channel_id=1, source_target_pairs={{0,24},{1,25},{2,26},{3,27},{4,28},{5,29},{6,30},{7,31}} | collective-permute-start | bytes 1572872 | tf_op jit(solution)/shard_map/ppermute | solution.py:24
  47.6 1.3 collective-permute-start.2
  48.9 2.7 collective-permute-start.3
  51.6 1.1 subtract_convert_fusion
  52.7 0.5 fusion.30
  53.2 6.6 %collective-permute-done.1 = bf16[1024,256]{0,1:T(8,128)(2,1)S(1)} collective-permute-done((bf16[1024,256]{0,1:T(8,128)(2,1)S(1)}, bf16[1024,256]{0,1:T(8,128)(2,1)S(1)}, u32[]{:S(2)}, u32[]{:S(2)}) %collective-permute-start.1) | collective-permute-done | bytes 524320 | tf_op jit(solution)/shard_map/ppermute | solution.py:24
  59.8 12.1 %collective-permute-done.2 = bf16[1024,256]{0,1:T(8,128)(2,1)S(1)} collective-permute-done((bf16[1024,256]{0,1:T(8,128)(2,1)S(1)}, bf16[1024,256]{0,1:T(8,128)(2,1)S(1)}, u32[]{:S(2)}, u32[]{:S(2)}) %collective-permute-start.2) | collective-permute-done | bytes 524320 | tf_op jit(solution)/shard_map/ppermute | solution.py:24
  72.0 0.0 collective-permute-done.3
  72.1 0.0 copy-start.1
  72.1 8.3 %fusion.22 = f32[4608,512,2]{1,0,2:T(8,128)} fusion(bf16[5120,256]{0,1:T(8,128)(2,1)S(1)} %constant_dynamic-update-slice_fusion, bf16[512,2,128]{0,1,2:T(2,128)(2,1)S(1)} %bitcast.64), kind=kOutput, calls=%fused_computation.38 | convolution fusion | flops 1207959552 | bytes 20316160 | tf_op jit(solution)/shard_map/qhd,kd->hqk/dot_general | solution.py:96
  80.4 2.6 fusion.21
  83.0 21.7 %fusion.68 = (f32[2,512]{1,0:T(2,128)S(1)}, f32[2,512,4608]{1,2,0:T(8,128)}) fusion(f32[4608,512,2]{1,0,2:T(8,128)} %fusion.22, pred[512,4608]{0,1:T(8,128)(4,1)} %get-tuple-element.24), kind=kOutput, calls=%fused_computation.124 | output fusion | flops 28316160 | bytes 40112128 | tf_op jit(solution)/shard_map/sub | solution.py:101
  104.8 8.9 %fusion.20 = bf16[128,2,512]{2,0,1:T(8,128)(2,1)} fusion(f32[2,512,4608]{1,2,0:T(8,128)} %get-tuple-element.29, f32[2,512]{1,0:T(2,128)S(1)} %get-tuple-element.28, bf16[5120,256]{0,1:T(8,128)(2,1)} %copy-done.1), kind=kOutput, calls=%fused_computation.33 | convolution fusion | flops 1217527808 | bytes 20320256 | tf_op jit(solution)/shard_map/hqk,kd->qhd/dot_general | solution.py:103
  113.6 13.4 %fusion.67 = (f32[2,512]{1,0:T(2,128)S(1)}, f32[2,512,4608]{1,2,0:T(8,128)}) fusion(f32[4608,512,2]{1,0,2:T(8,128)S(1)} %fusion.21, pred[512,4608]{0,1:T(8,128)(4,1)} %get-tuple-element.25), kind=kOutput, calls=%fused_computation.123 | output fusion | flops 28316160 | bytes 40112128 | tf_op jit(solution)/shard_map/sub | solution.py:101
  127.0 8.2 %fusion.19 = bf16[128,2,512]{2,0,1:T(8,128)(2,1)S(1)} fusion(f32[2,512,4608]{1,2,0:T(8,128)} %get-tuple-element.27, f32[2,512]{1,0:T(2,128)S(1)} %get-tuple-element.26, bf16[5120,256]{0,1:T(8,128)(2,1)} %copy-done.1), kind=kOutput, calls=%fused_computation.32 | convolution fusion | flops 1217527808 | bytes 20320256 | tf_op jit(solution)/shard_map/hqk,kd->qhd/dot_general | solution.py:103
  135.2 0.0 copy-done
  135.2 0.0 copy-done.5
  135.2 8.1 %convolution_bitcast_fusion = f32[4096,1024]{0,1:T(8,128)} fusion(bf16[256,4096]{1,0:T(8,128)(2,1)S(1)} %copy-done, bf16[512,256]{0,1:T(8,128)(2,1)S(1)} %bitcast.66, bf16[512,256]{0,1:T(8,128)(2,1)S(1)} %bitcast.65), kind=kOutput, calls=%fused_computation.26 | convolution fusion | flops 2148532224 | bytes 19398656 | tf_op jit(solution)/shard_map/dot_general | solution.py:121
  143.3 0.0 reduce-scatter.3.cloned.1.call-update
  143.4 0.0 copy-start.8
  143.4 0.0 all-reduce.3.cloned.1.call-start
  143.4 0.5 copy-done.9
  144.0 0.2 reduce-window.9
  144.2 0.1 iota_add_fusion.1
  144.2 0.1 add.139
  144.3 0.1 iota_compare_fusion.5
  144.4 0.1 lt.53
  144.5 3.1 fusion.15
  147.6 165.5 %reduce-scatter.3.cloned.1.call-done = f32[512,1024]{0,1:T(8,128)} async-done(((f32[4096,1024]{0,1:T(8,128)}), f32[512,1024]{0,1:T(8,128)}) %reduce-scatter.3.cloned.1.call-update) | async-done | bytes 2097168 | tf_op jit(solution)/shard_map/reduce_scatter | solution.py:120
  313.1 2.6 fusion.29
  315.6 2.3 convolution_add_fusion
  318.0 0.0 all-reduce.3.cloned.1.call-update
  318.0 0.0 reduce-scatter.5.cloned.1.call-start
  318.0 0.2 convert_reduce_fusion
  318.2 39.8 %all-reduce.3.cloned.1.call-done = f32[32,512]{1,0:T(8,128)} async-done(((f32[32,512]{1,0:T(8,128)}), f32[32,512]{1,0:T(8,128)}) %all-reduce.3.cloned.1.call-update) | async-done | bytes 65552 | tf_op jit(solution)/shard_map/psum | solution.py:131
  358.0 1.0 multiply_reduce_fusion
  359.0 16.0 %psum.15 = f32[32]{0:T(128)S(1)} all-reduce(f32[32]{0:T(128)S(1)} %multiply_reduce_fusion), channel_id=1, replica_groups=mesh['seq'=4,'tp'=8] {'tp'}, use_global_device_ids=true, to_apply=%region_10.11 | all-reduce | flops 32 | bytes 256 | tf_op jit(solution)/shard_map/psum | solution.py:137
  375.0 3.6 fusion.18
  378.6 1.6 fusion.52
  380.2 0.0 reduce-scatter.5.cloned.1.call-update
  380.2 0.0 copy-done.8
  380.2 0.1 fusion.25
  380.4 8.0 %fusion.16 = f32[4096,512]{1,0:T(8,128)} fusion(bf16[4096,512]{1,0:T(8,128)(2,1)} %param.17, f32[4096]{0:T(1024)S(1)} %broadcast_add_fusion, s32[4096]{0:T(1024)S(1)} %iota_add_fusion, s32[32]{0:T(128)S(1)} %copy-done.8, f32[512]{0:T(512)S(1)} %copy-done.7, f32[32]{0:T(128)S(1)} %add_rsqrt_fusion, f32[32,512]{1,0:T(8,128)} %all-reduce.3.cloned.1.call-done, ...), kind=kOutput, calls=%fused_computation.28 | convolution fusion | flops 811778048 | bytes 12683648 | tf_op jit(solution)/shard_map/dot_general | solution.py:164
  388.4 21.4 %reduce-scatter.5.cloned.1.call-done = f32[8,4096]{1,0:T(8,128)} async-done(((f32[64,4096]{1,0:T(8,128)}), f32[8,4096]{1,0:T(8,128)}) %reduce-scatter.5.cloned.1.call-update) | async-done | bytes 131088 | tf_op jit(solution)/shard_map/reduce_scatter | solution.py:160
  (29 shorter events, 0.4 us)
Async XLA Ops:
  7.2 128.0 %copy-start = (bf16[256,4096]{1,0:T(8,128)(2,1)S(1)}, bf16[256,4096]{1,0:T(8,128)(2,1)}, u32[]{:S(2)}) copy-start(bf16[256,4096]{1,0:T(8,128)(2,1)} %param.14) | copy-start | bytes 6291460
  7.2 7.6 %copy-start.4 = (bf16[4096,64]{0,1:T(8,128)(2,1)S(1)}, bf16[4096,64]{0,1:T(8,128)(2,1)}, u32[]{:S(2)}) copy-start(bf16[4096,64]{0,1:T(8,128)(2,1)} %param.13) | copy-start | bytes 1572868
  7.2 305.9 %reduce-scatter.3.cloned.1.call-start = ((), (), s32[]{:S(2)}) async-start(), calls=%async_computation.2 | async-start | bytes 18874368 | tf_op jit(solution)/shard_map/reduce_scatter | solution.py:120
  21.5 19.5 %collective-permute-start = (bf16[1024,128]{0,1:T(8,128)(2,1)}, bf16[1024,128]{0,1:T(8,128)(2,1)}, u32[]{:S(2)}, u32[]{:S(2)}) collective-permute-start(bf16[1024,128]{0,1:T(8,128)(2,1)} %pad_maximum_fusion.2), channel_id=1, source_target_pairs={{0,1},{1,0},{2,3},{3,2},{4,5},{5,4},{6,7},{7,6},{8,9},{9,8},{10,11... | collective-permute-start | bytes 786440 | tf_op jit(solution)/shard_map/ppermute | solution.py:18
  23.8 9.2 %copy-start.6 = (s32[4096]{0:T(1024)S(1)}, s32[4096]{0:T(1024)}, u32[]{:S(2)}) copy-start(s32[4096]{0:T(1024)} %param.15) | copy-start | bytes 49156
  33.0 18.6 %copy-start.2 = (f32[1024,64]{0,1:T(8,128)S(1)}, f32[1024,64]{0,1:T(8,128)}, u32[]{:S(2)}) copy-start(f32[1024,64]{0,1:T(8,128)} %get-tuple-element.22) | copy-start | bytes 786436
  33.0 18.6 %copy-start.3 = (f32[1024,64]{0,1:T(8,128)S(1)}, f32[1024,64]{0,1:T(8,128)}, u32[]{:S(2)}) copy-start(f32[1024,64]{0,1:T(8,128)} %get-tuple-element.23) | copy-start | bytes 786436
  42.2 17.6 %collective-permute-start.1 = (bf16[1024,256]{0,1:T(8,128)(2,1)S(1)}, bf16[1024,256]{0,1:T(8,128)(2,1)S(1)}, u32[]{:S(2)}, u32[]{:S(2)}) collective-permute-start(bf16[1024,256]{0,1:T(8,128)(2,1)S(1)} %pad_maximum_fusion), channel_id=1, source_target_pairs={{0,24},{1,25},{2,26},{3,27},{4,28},{5,29},{6,30},{7,31}} | collective-permute-start | bytes 1572872 | tf_op jit(solution)/shard_map/ppermute | solution.py:24
  47.6 24.4 %collective-permute-start.2 = (bf16[1024,256]{0,1:T(8,128)(2,1)S(1)}, bf16[1024,256]{0,1:T(8,128)(2,1)S(1)}, u32[]{:S(2)}, u32[]{:S(2)}) collective-permute-start(bf16[1024,256]{0,1:T(8,128)(2,1)S(1)} %pad_maximum_fusion), channel_id=1, source_target_pairs={{0,16},{8,24},{1,17},{9,25},{2,18},{10,26},{3,19},{11,27},{4,20},{... | collective-permute-start | bytes 1572872 | tf_op jit(solution)/shard_map/ppermute | solution.py:24
  48.9 23.1 %collective-permute-start.3 = (bf16[1024,256]{0,1:T(8,128)(2,1)S(1)}, bf16[1024,256]{0,1:T(8,128)(2,1)S(1)}, u32[]{:S(2)}, u32[]{:S(2)}) collective-permute-start(bf16[1024,256]{0,1:T(8,128)(2,1)S(1)} %pad_maximum_fusion), channel_id=1, source_target_pairs={{0,8},{8,16},{16,24},{1,9},{9,17},{17,25},{2,10},{10,18},{18,26},{... | collective-permute-start | bytes 1572872 | tf_op jit(solution)/shard_map/ppermute | solution.py:24
  72.1 8.3 %copy-start.1 = (bf16[5120,256]{0,1:T(8,128)(2,1)}, bf16[5120,256]{0,1:T(8,128)(2,1)S(1)}, u32[]{:S(2)}) copy-start(bf16[5120,256]{0,1:T(8,128)(2,1)S(1)} %constant_dynamic-update-slice_fusion) | copy-start | bytes 7864324
  127.0 8.2 %copy-start.5 = (bf16[128,2,512]{2,0,1:T(8,128)(2,1)S(1)}, bf16[128,2,512]{2,0,1:T(8,128)(2,1)}, u32[]{:S(2)}) copy-start(bf16[128,2,512]{2,0,1:T(8,128)(2,1)} %fusion.20) | copy-start | bytes 786436
  143.3 0.7 copy-start.9
  143.3 231.7 %copy-start.7 = (f32[512]{0:T(512)S(1)}, f32[512]{0:T(512)}, u32[]{:S(2)}) copy-start(f32[512]{0:T(512)} %param.18) | copy-start | bytes 6148
  143.4 236.9 %copy-start.8 = (s32[32]{0:T(128)S(1)}, s32[32]{0:T(128)}, u32[]{:S(2)}) copy-start(s32[32]{0:T(128)} %param.19) | copy-start | bytes 388
  143.4 214.6 %all-reduce.3.cloned.1.call-start = ((), (), s32[]{:S(2)}) async-start(), calls=%async_computation.3 | async-start | bytes 131072 | tf_op jit(solution)/shard_map/psum | solution.py:131
  318.0 91.7 %reduce-scatter.5.cloned.1.call-start = ((), (), s32[]{:S(2)}) async-start(), calls=%async_computation.4 | async-start | bytes 1179648 | tf_op jit(solution)/shard_map/reduce_scatter | solution.py:160
Sparse Core Ops, SparseCore 0:
  143.5 169.5 reduce-scatter.2
  318.1 39.8 all-reduce.2
  380.3 29.3 reduce-scatter.4
where the time goes:
time: 417 us; the launch traced here: 416 us
  waiting for transfers between devices  245 us (59%)
  matrix products  73.8 us (18%)
  other arithmetic  52.9 us (13%)
  blocking collectives  16 us (4%)
  between operations  14.1 us (3%)
  starting transfers between devices  9.94 us (2%)
  local copies, waits for them, and re-layouts  4.25 us (1%)
    reduce_scatter x1, waiting for transfers between devices, shards(): lax.psum_scatter(lax.dot_general(w_out, attention, (((0,), (1,)), ((), ()...  165 us
    psum x1, waiting for transfers between devices, shards(): seg_sums = lax.psum(pooled_tokens + pooled_mixed, 'seq')  39.8 us
    sub x2, other arithmetic, shards(): weights = jnp.exp(scores - highest)  35.1 us
    reduce_scatter x1, waiting for transfers between devices, shards(): lax.psum_scatter(slot_terms, 'tp', scatter_dimension=0, tiled=True)  21.4 us
    ppermute x3, waiting for transfers between devices, from_behind(): lax.ppermute(value, axis, [(source, source + steps) for source in range(l...  18.7 us
    dot_general x2, matrix products, shards(): jnp.einsum('hqk,kd->qhd', soft_weights, kv_block[:, HD:], preferred_eleme...  17 us
    psum x1, blocking collectives, shards(): square_sums = lax.psum(jnp.sum(pooled * pooled, axis=1), 'tp')  16 us
    dot_general x2, matrix products, shards(): jnp.einsum('qhd,kd->hqk', q_block, kv_block[:, :HD], preferred_element_ty...  11 us
  transfers between devices with their start and end apart: 7, of which 5 were waited for; matrix products, arithmetic and copies ran while one was open for 8% of the time, Pallas kernels for 0%

commit v1 on v0

v1 whole, which is shorter than its diff:
```python
import math

import jax
import jax.numpy as jnp
import numpy as np
from jax import lax
from jax.experimental import pallas as pl
from jax.experimental.pallas import tpu as pltpu
from jax.sharding import PartitionSpec as P

HD = 128
WINDOW = 4096
QB = 256
KB = 512
LANES = 128
GROUP = 16

rope_theta = 10000.0
norm_eps = 1e-06
VMEM_LIMIT = 56 * 1024 * 1024

f32 = jnp.float32
bf16 = jnp.bfloat16
i32 = jnp.int32


def swapped(x, axis, mask):
    count = lax.axis_size(axis)
    return lax.ppermute(x, axis, [(i, i ^ mask) for i in range(count)])


def angle_tables(seq_len):
    inverse = np.exp(-(2.0 * np.arange(HD // 2) / HD) * math.log(rope_theta))
    inverse = np.repeat(inverse, 2)[None, :]
    fine = np.arange(LANES)[:, None] * inverse
    coarse = LANES * np.arange(seq_len // LANES)[:, None] * inverse
    fine_tab = np.stack([np.cos(fine), np.sin(fine)]).astype(np.float32)
    coarse_tab = np.stack([np.cos(coarse), np.sin(coarse)]).astype(np.float32)
    return fine_tab, coarse_tab


def turn(fine, coarse, which):
    ca = coarse[0, pl.ds(which, 1), :]
    sa = coarse[1, pl.ds(which, 1), :]
    cb = fine[0]
    sb = fine[1]
    return ca * cb - sa * sb, sa * cb + ca * sb


def pair_swap(x, even):
    up = pltpu.roll(x, x.shape[1] - 1, 1)
    down = pltpu.roll(x, 1, 1)
    return jnp.where(even, up, down)


def kv_body(tok, wk, wv, fine, coarse, k_out, v_out, w_both):
    step = pl.program_id(0)
    half = wk.shape[1]
    rows = tok.shape[0]
    subs = rows // LANES

    @pl.when(step == 0)
    def _():
        w_both[:, :half] = wk[...]
        w_both[:, half:] = wv[...]

    both = jnp.dot(tok[...], w_both[...], preferred_element_type=f32)
    lane = lax.broadcasted_iota(i32, (LANES, LANES), 1)
    even = lane % 2 == 0
    upper = lax.axis_index("tp") % 2 == 1
    first = lax.axis_index("seq") * (pl.num_programs(0) * subs) + step * subs
    for sub in range(subs):
        cos, sin = turn(fine, coarse, first + sub)
        cos = jnp.where(upper, pltpu.roll(cos, half, 1), cos)
        sin = jnp.where(upper, pltpu.roll(sin, half, 1), sin)
        cos = jnp.where(lane < half, cos, 1.0)
        sin = jnp.where(lane < half, jnp.where(even, -sin, sin), 0.0)
        x = both[sub * LANES : (sub + 1) * LANES]
        x = x * cos + pair_swap(x, even) * sin
        x = x.T
        k_out[:, sub * LANES : (sub + 1) * LANES] = x[:half].astype(bf16)
        v_out[:, sub * LANES : (sub + 1) * LANES] = x[half:].astype(bf16)


def project_kv(tokens, w_key, w_value, fine, coarse):
    rows, width = tokens.shape
    half = w_key.shape[1]
    block = 256
    whole = lambda a: pl.BlockSpec(a.shape, lambda i: (0,) * a.ndim)
    out = jax.ShapeDtypeStruct((half, rows), bf16)
    return pl.pallas_call(
        kv_body,
        grid=(rows // block,),
        in_specs=[
            pl.BlockSpec((block, width), lambda i: (i, 0)),
            whole(w_key),
            whole(w_value),
            whole(fine),
            whole(coarse),
        ],
        out_specs=[pl.BlockSpec((half, block), lambda i: (0, i))] * 2,
        out_shape=[out, out],
        scratch_shapes=[pltpu.VMEM((width, 2 * half), bf16)],
        compiler_params=pltpu.CompilerParams(vmem_limit_bytes=VMEM_LIMIT),
        name="project_kv",
    )(tokens, w_key, w_value, fine, coarse)


def q_body(tok, wq, fine, coarse, q_out):
    step = pl.program_id(0)
    rows = tok.shape[0]
    subs = rows // LANES
    heads = wq.shape[1] // HD
    x_all = jnp.dot(tok[...], wq[...], preferred_element_type=f32)
    lane = lax.broadcasted_iota(i32, (LANES, LANES), 1)
    even = lane % 2 == 0
    first = lax.axis_index("seq") * (pl.num_programs(0) * subs) + step * subs
    scale = HD ** (-0.5) * math.log2(math.e)
    for sub in range(subs):
        cos, sin = turn(fine, coarse, first + sub)
        cos = cos * scale
        sin = jnp.where(even, -sin, sin) * scale
        for h in range(heads):
            x = x_all[sub * LANES : (sub + 1) * LANES, h * HD : (h + 1) * HD]
            x = x * cos + pair_swap(x, even) * sin
            q_out[sub * LANES : (sub + 1) * LANES, h * HD : (h + 1) * HD] = x.astype(bf16)


def project_q(tokens, w_query, fine, coarse):
    rows, width = tokens.shape
    cols = w_query.shape[1]
    block = 256
    whole = lambda a: pl.BlockSpec(a.shape, lambda i: (0,) * a.ndim)
    return pl.pallas_call(
        q_body,
        grid=(rows // block,),
        in_specs=[
            pl.BlockSpec((block, width), lambda i: (i, 0)),
            whole(w_query),
            whole(fine),
            whole(coarse),
        ],
        out_specs=pl.BlockSpec((block, cols), lambda i: (i, 0)),
        out_shape=jax.ShapeDtypeStruct((rows, cols), bf16),
        compiler_params=pltpu.CompilerParams(vmem_limit_bytes=VMEM_LIMIT),
        name="project_q",
    )(tokens, w_query, fine, coarse)


def cent_body(base, cent, cent_any, wide, norms, picked, sems):
    step = pl.program_id(0)
    count = base.shape[0]

    def fetch(r):
        start = pl.multiple_of(base[r], GROUP)
        return pltpu.make_async_copy(
            cent_any.at[pl.ds(start, GROUP), :], picked.at[pl.ds(r * GROUP, GROUP), :], sems.at[r]
        )

    @pl.when(step == 0)
    def _():
        for r in range(count):
            fetch(r).start()

    c = cent[...].astype(f32)
    wide[...] = c
    square = c * c
    high = square.astype(bf16)
    low = (square - high.astype(f32)).astype(bf16)
    ones = jnp.ones((8, c.shape[1]), bf16)
    contract = (((1,), (1,)), ((), ()))
    total = lax.dot_general(ones, high, contract, preferred_element_type=f32)
    total = total + lax.dot_general(ones, low, contract, preferred_element_type=f32)
    norms[pl.ds(step, 1), :] = total[:1]

    @pl.when(step == pl.num_programs(0) - 1)
    def _():
        for r in range(count):
            fetch(r).wait()


def widen_centroids(base, centroids):
    rows, feat = centroids.shape
    count = base.shape[0]
    block = rows // 8
    spec = pltpu.PrefetchScalarGridSpec(
        num_scalar_prefetch=1,
        grid=(8,),
        in_specs=[
            pl.BlockSpec((block, feat), lambda i, b: (i, 0)),
            pl.BlockSpec(memory_space=pl.ANY),
        ],
        out_specs=[
            pl.BlockSpec((block, feat), lambda i, b: (i, 0)),
            pl.BlockSpec((8, block), lambda i, b: (0, 0)),
            pl.BlockSpec((count * GROUP, feat), lambda i, b: (0, 0)),
        ],
        scratch_shapes=[pltpu.SemaphoreType.DMA((count,))],
    )
    return pl.pallas_call(
        cent_body,
        grid_spec=spec,
        out_shape=[
            jax.ShapeDtypeStruct((rows, feat), f32),
            jax.ShapeDtypeStruct((8, block), f32),
            jax.ShapeDtypeStruct((count * GROUP, feat), bf16),
        ],
        compiler_params=pltpu.CompilerParams(vmem_limit_bytes=VMEM_LIMIT),
        name="widen_centroids",
    )(base, centroids, centroids)


def attend_body(pieces, seg_total, seg, q_ref, seg_row, *refs):
    keys_in = refs[: 2 * pieces]
    values_in = refs[2 * pieces : 4 * pieces]
    out, counts, kt, vt, sc, col, lhs, sems = refs[4 * pieces :]
    rows = q_ref.shape[0]
    heads = q_ref.shape[1] // HD
    half = HD // 2
    seq_len = kt.shape[1]
    rank = lax.axis_index("seq")
    parity = lax.axis_index("tp") % 2

    def copies(sources, target, first):
        result = []
        for k in range(2):
            for m in range(pieces):
                row0 = pl.multiple_of((parity ^ k) * half, half)
                col0 = pl.multiple_of((rank ^ m) * rows, rows)
                index = k * pieces + m
                result.append(
                    pltpu.make_async_copy(
                        sources[index],
                        target.at[pl.ds(row0, half), pl.ds(col0, rows)],
                        sems.at[first + index],
                    )
                )
        return result

    key_copies = copies(keys_in, kt, 0)
    value_copies = copies(values_in, vt, 2 * pieces)
    for c in key_copies:
        c.start()
    for c in value_copies:
        c.start()
    col[...] = jnp.zeros(col.shape, f32)
    for c in key_copies:
        c.wait()

    def q_step(b, carry):
        base = rank * rows + b * QB
        last_seg = seg[base + QB - 1]
        first_seg = seg[base]
        end = (base + QB - 1) // KB + 1
        clear_end = base // KB
        begin = jnp.int32(0)
        clear = jnp.int32(0)
        for t in range(seq_len // KB):
            begin = begin + (seg[t * KB + KB - 1] < first_seg).astype(i32)
            outside = (seg[t * KB] != last_seg) | (base + QB - 1 - t * KB >= WINDOW)
            clear = clear + (outside & (t < clear_end)).astype(i32)
        begin = jnp.maximum(begin, jnp.maximum(base - (WINDOW - 1), 0) // KB)
        begin = jnp.minimum(begin, clear_end)
        clear = jnp.clip(clear, begin, clear_end)
        own = jnp.broadcast_to(seg_row[:, pl.ds(base, QB)].astype(f32), (LANES, QB)).T
        i_pos = base + lax.broadcasted_iota(i32, (QB, LANES), 0)

        for h in range(heads):
            q = q_ref[pl.ds(b * QB, QB), h * HD : (h + 1) * HD]

            def score(masked, kb, top):
                start = pl.multiple_of(kb * KB, KB)
                s = jnp.dot(q, kt[:, pl.ds(start, KB)], preferred_element_type=f32)
                for g in range(KB // LANES):
                    part = s[:, g * LANES : (g + 1) * LANES]
                    at = pl.multiple_of(start + g * LANES, LANES)
                    if masked:
                        j_pos = at + lax.broadcasted_iota(i32, (QB, LANES), 1)
                        ids = seg_row[:, pl.ds(at, LANES)].astype(f32)
                        allowed = (j_pos <= i_pos) & (own == ids)
                        if seq_len > WINDOW:
                            allowed = allowed & (i_pos - j_pos < WINDOW)
                        part = jnp.where(allowed, part, -1e30)
                    sc[:, pl.ds(at, LANES)] = part
                    top = jnp.maximum(top, part)
                return top

            top = jnp.full((QB, LANES), -1e30, f32)
            top = lax.fori_loop(begin, clear, lambda kb, t: score(True, kb, t), top)
            top = lax.fori_loop(clear, clear_end, lambda kb, t: score(False, kb, t), top)
            top = lax.fori_loop(clear_end, end, lambda kb, t: score(True, kb, t), top)
            top = jnp.max(top, axis=1, keepdims=True)

            def weigh(kb, total):
                start = pl.multiple_of(kb * KB, KB)
                for g in range(KB // LANES):
                    at = pl.multiple_of(start + g * LANES, LANES)
                    p = jnp.exp2(sc[:, pl.ds(at, LANES)] - top)
                    sc[:, pl.ds(at, LANES)] = p
                    total = total + p
                return total

            total = lax.fori_loop(begin, end, weigh, jnp.zeros((QB, LANES), f32))
            share = 1.0 / jnp.sum(total, axis=1, keepdims=True)
            share = jnp.broadcast_to(share, (QB, LANES))

            def gather(kb, carry):
                start = pl.multiple_of(kb * KB, KB)
                for g in range(KB // LANES):
                    at = pl.multiple_of(start + g * LANES, LANES)
                    p = sc[:, pl.ds(at, LANES)] * share
                    p = jnp.sum(p.reshape(QB // 8, 8, LANES), axis=0)
                    col[h, :, pl.ds(at, LANES)] = col[h, :, pl.ds(at, LANES)] + p
                return carry

            lax.fori_loop(begin, end, gather, 0)
        return carry

    lax.fori_loop(0, rows // QB, q_step, 0)

    number = jnp.zeros((seg_total, LANES), f32)
    for g in range(seq_len // LANES):
        at = slice(g * LANES, (g + 1) * LANES)
        ids = seg_row[:, at]
        member = ids == lax.broadcasted_iota(i32, (seg_total, LANES), 0)
        number = number + member.astype(f32)
        for h in range(heads):
            w = jnp.sum(col[h, :, at], axis=0, keepdims=True)
            w = jnp.where(member, w, 0.0)
            high = w.astype(bf16)
            lhs[h * seg_total : (h + 1) * seg_total, at] = high
            low = (w - high.astype(f32)).astype(bf16)
            lhs[(heads + h) * seg_total : (heads + h + 1) * seg_total, at] = low
    counts[...] = jnp.broadcast_to(jnp.sum(number, axis=1, keepdims=True), counts.shape)
    for c in value_copies:
        c.wait()
    pooled = lax.dot_general(
        lhs[...], vt[...], (((1,), (1,)), ((), ())), preferred_element_type=f32
    )
    for h in range(heads):
        high = pooled[h * seg_total : (h + 1) * seg_total]
        low = pooled[(heads + h) * seg_total : (heads + h + 1) * seg_total]
        out[:, h * HD : (h + 1) * HD] = high + low


def attend(seg_ids, queries, keys, values, seg_total):
    rows, cols = queries.shape
    seq_len = seg_ids.shape[0]
    pieces = len(keys) // 2
    heads = cols // HD
    whole = pl.BlockSpec(memory_space=pltpu.VMEM)
    anywhere = pl.BlockSpec(memory_space=pl.ANY)

    def body(*refs):
        attend_body(pieces, seg_total, *refs)

    return pl.pallas_call(
        body,
        in_specs=[pl.BlockSpec(memory_space=pltpu.SMEM), whole, whole] + [anywhere] * (4 * pieces),
        out_specs=[whole, whole],
        out_shape=[
            jax.ShapeDtypeStruct((seg_total, cols), f32),
            jax.ShapeDtypeStruct((seg_total, LANES), f32),
        ],
        scratch_shapes=[
            pltpu.VMEM((HD, seq_len), bf16),
            pltpu.VMEM((HD, seq_len), bf16),
            pltpu.VMEM((QB, seq_len), f32),
            pltpu.VMEM((heads, 8, seq_len), f32),
            pltpu.VMEM((2 * heads * seg_total, seq_len), bf16),
            pltpu.SemaphoreType.DMA((4 * pieces,)),
        ],
        compiler_params=pltpu.CompilerParams(vmem_limit_bytes=VMEM_LIMIT),
        name="attend",
    )(seg_ids, queries, seg_ids.reshape(1, seq_len), *keys, *values)


def mix_body(pieces, *refs):
    parts = refs[:pieces]
    norms, w_out, keep, send = refs[pieces:]
    groups, _, feat = keep.shape
    seg_total = parts[0].shape[0]
    mixed = parts[0][...]
    for p in parts[1:]:
        mixed = mixed + p[...]
    high = mixed.astype(bf16)
    low = (mixed - high.astype(f32)).astype(bf16)
    lhs = jnp.concatenate([high, low], 0)
    rank = lax.axis_index("tp")
    for k, target in enumerate((keep, send)):
        for m in range(groups):
            owner = rank ^ (2 * m + k)
            cols = pl.ds(pl.multiple_of(owner * feat, feat), feat)
            y = jnp.dot(lhs, w_out[:, cols], preferred_element_type=f32)
            target[m, :seg_total, :] = y[:seg_total] + y[seg_total:]
            target[m, seg_total:, :] = norms[...]


def mix(parts, norms, w_out, feat, groups):
    seg_total = parts[0].shape[0]
    whole = pl.BlockSpec(memory_space=pltpu.VMEM)
    out = jax.ShapeDtypeStruct((groups, seg_total + 8, feat), f32)

    def body(*refs):
        mix_body(len(parts), *refs)

    return pl.pallas_call(
        body,
        in_specs=[whole] * (len(parts) + 2),
        out_specs=[whole, whole],
        out_shape=[out, out],
        compiler_params=pltpu.CompilerParams(vmem_limit_bytes=VMEM_LIMIT),
        name="mix",
    )(*parts, norms, w_out)


def owner_span(owner_counts, owner):
    start = jnp.int32(0)
    for o in range(owner_counts.shape[0]):
        start = start + jnp.where(o < owner, owner_counts[o], 0)
    return start, owner_counts[owner]


def cross_body(groups, pieces, model_width, owner_counts, *refs):
    mixed = refs[:groups]
    pooled_in = refs[groups : groups + pieces]
    counts, gain, cent = refs[groups + pieces : groups + pieces + 3]
    keep, send, emb, norms, lhs = refs[groups + pieces + 3 :]
    step = pl.program_id(0)
    seg_total, feat = emb.shape
    block = cent.shape[0]
    slots = keep.shape[1]
    per_side = groups * slots
    rank = lax.axis_index("tp")

    @pl.when(step == 0)
    def _():
        total = mixed[0][...]
        for p in mixed[1:]:
            total = total + p[...]
        norms[...] = total[seg_total:]
        sums = total[:seg_total]
        for p in pooled_in:
            sums = sums + p[...]
        pooled = sums / counts[:, :1]
        square = jnp.sum(pooled * pooled, axis=1, keepdims=True)
        row = lax.broadcasted_iota(i32, (seg_total, LANES), 0)
        lane = lax.broadcasted_iota(i32, (seg_total, LANES), 1)
        square = jnp.sum(jnp.where(row == lane, square, 0.0), axis=0, keepdims=True)
        square = jnp.broadcast_to(square, (slots, LANES))
        scaled = pooled * gain[...]
        emb[...] = scaled
        high = scaled.astype(bf16)
        low = (scaled - high.astype(f32)).astype(bf16)
        slot = lax.broadcasted_iota(i32, (slots, seg_total), 0)
        column = lax.broadcasted_iota(i32, (slots, seg_total), 1)
        chosen = []
        for k, target in enumerate((keep, send)):
            for m in range(groups):
                start, number = owner_span(owner_counts, rank ^ (2 * m + k))
                hit = (slot + start == column) & (slot < number)
                chosen.append(jnp.where(hit, 1.0, 0.0))
                target[m, :, block * pl.num_programs(0) :] = square
        chosen = jnp.concatenate(chosen, 0).astype(bf16)
        factor = -2.0 / model_width**0.5
        lhs[: 2 * per_side] = (
            jnp.dot(chosen, high, preferred_element_type=f32) * factor
        ).astype(bf16)
        lhs[2 * per_side :] = (
            jnp.dot(chosen, low, preferred_element_type=f32) * factor
        ).astype(bf16)

    y = lax.dot_general(
        lhs[...], cent[...], (((1,), (1,)), ((), ())), preferred_element_type=f32
    )
    y = y[: 2 * per_side] + y[2 * per_side :]
    cols = pl.ds(pl.multiple_of(step * block, block), block)
    for k, target in enumerate((keep, send)):
        for m in range(groups):
            first = k * per_side + m * slots
            target[m, :, cols] = y[first : first + slots]


def cross(owner_counts, mixed, pooled_in, counts, gain, centroids, slots, model_width):
    rows, feat = centroids.shape
    groups = len(mixed)
    pieces = len(pooled_in)
    seg_total = counts.shape[0]
    block = rows // 8
    fixed = lambda shape: pl.BlockSpec(shape, lambda i, o: (0,) * len(shape))
    side = (groups, slots, rows + LANES)
    spec = pltpu.PrefetchScalarGridSpec(
        num_scalar_prefetch=1,
        grid=(8,),
        in_specs=[fixed(a.shape) for a in mixed]
        + [fixed(a.shape) for a in pooled_in]
        + [
            fixed(counts.shape),
            fixed(gain.shape),
            pl.BlockSpec((block, feat), lambda i, o: (i, 0)),
        ],
        out_specs=[fixed(side), fixed(side), fixed((seg_total, feat)), fixed((8, block))],
        scratch_shapes=[pltpu.VMEM((4 * groups * slots, feat), bf16)],
    )

    def body(*refs):
        cross_body(groups, pieces, model_width, *refs)

    return pl.pallas_call(
        body,
        grid_spec=spec,
        out_shape=[
            jax.ShapeDtypeStruct(side, f32),
            jax.ShapeDtypeStruct(side, f32),
            jax.ShapeDtypeStruct((seg_total, feat), f32),
            jax.ShapeDtypeStruct((8, block), f32),
        ],
        compiler_params=pltpu.CompilerParams(vmem_limit_bytes=VMEM_LIMIT),
        name="cross",
    )(owner_counts, *mixed, *pooled_in, counts, gain, centroids)


def finish_body(groups, model_width, owner_counts, place, *refs):
    terms = refs[:groups]
    norms, emb, assign_row, picked, wide_in, dist, wide, moved, sems = refs[groups:]
    seg_total, feat = emb.shape
    block = norms.shape[1]
    slots = dist.shape[0]
    rows = dist.shape[1]
    total = terms[0][:, rows:]
    for t in terms[1:]:
        total = total + t[:, rows:]
    scale = lax.rsqrt(total / model_width + norm_eps)
    slot = lax.broadcasted_iota(i32, (slots, LANES), 0)
    lane = lax.broadcasted_iota(i32, (slots, LANES), 1)
    start, number = owner_span(owner_counts, lax.axis_index("tp"))
    hit = (slot + start == lane) & (slot < number)
    own_scale = jnp.sum(jnp.where(hit, scale, 0.0), axis=1, keepdims=True)

    spread = jnp.broadcast_to(scale[:1], (seg_total, LANES))
    r_row = lax.broadcasted_iota(i32, (seg_total, LANES), 0)
    r_lane = lax.broadcasted_iota(i32, (seg_total, LANES), 1)
    row_scale = jnp.sum(jnp.where(r_row == r_lane, spread, 0.0), axis=1, keepdims=True)
    value = emb[...] * row_scale
    high = value.astype(bf16)
    rest = value - high.astype(f32)
    middle = rest.astype(bf16)
    low = (rest - middle.astype(f32)).astype(bf16)
    stacked = jnp.concatenate([high, middle, low], 0)
    member = lax.broadcasted_iota(i32, (GROUP, 3 * seg_total), 0)
    once = lax.broadcasted_iota(i32, (GROUP, 3 * seg_total), 1) < seg_total
    for r in range(seg_total):
        match = assign_row[...] == member + place[1, r]
        match = jnp.where(match, 1.0, 0.0)
        number_r = jnp.sum(jnp.where(once, match, 0.0), axis=1, keepdims=True)
        added = jnp.dot(match.astype(bf16), stacked, preferred_element_type=f32)
        at = slice(r * GROUP, (r + 1) * GROUP)
        moved[at, :] = (picked[at, :].astype(f32) + added) / (1.0 + number_r)

    def write(r):
        first = pl.multiple_of(place[0, r], GROUP)
        return pltpu.make_async_copy(
            moved.at[pl.ds(r * GROUP, GROUP), :], wide.at[pl.ds(first, GROUP), :], sems.at[r]
        )

    for r in range(seg_total):
        pl.when(place[2, r] == 1)(lambda r=r: write(r).start())

    valid = lax.broadcasted_iota(i32, (slots, block), 0) < number
    for g in range(rows // block):
        at = slice(g * block, (g + 1) * block)
        y = terms[0][:, at]
        for t in terms[1:]:
            y = y + t[:, at]
        y = norms[g : g + 1, :] * (1.0 / model_width**0.5) + y * own_scale
        dist[:, at] = jnp.where(valid, y, 0.0)

    for r in range(seg_total):
        pl.when(place[2, r] == 1)(lambda r=r: write(r).wait())


def finish(owner_counts, place, terms, norms, emb, assign_row, picked, wide, model_width):
    groups = len(terms)
    seg_total = emb.shape[0]
    slots, rows = terms[0].shape
    rows = rows - LANES
    whole = pl.BlockSpec(memory_space=pltpu.VMEM)
    anywhere = pl.BlockSpec(memory_space=pl.ANY)
    scalar = pl.BlockSpec(memory_space=pltpu.SMEM)

    def body(*refs):
        finish_body(groups, model_width, *refs)

    return pl.pallas_call(
        body,
        in_specs=[scalar, scalar] + [whole] * (groups + 4) + [anywhere],
        out_specs=[whole, anywhere],
        out_shape=[
            jax.ShapeDtypeStruct((slots, rows), f32),
            jax.ShapeDtypeStruct(wide.shape, f32),
        ],
        scratch_shapes=[
            pltpu.VMEM((seg_total * GROUP, emb.shape[1]), f32),
            pltpu.SemaphoreType.DMA((seg_total,)),
        ],
        input_output_aliases={2 + groups + 4: 1},
        compiler_params=pltpu.CompilerParams(vmem_limit_bytes=VMEM_LIMIT),
        name="finish",
    )(owner_counts, place, *terms, norms, emb, assign_row, picked, wide)


def shards(
    tokens, w_query, w_key, w_value, w_out, seg_ids, owner_counts, centroids, pool_gain, assign
):
    tok_rows, model_width = tokens.shape
    seq_len = seg_ids.shape[0]
    seg_total = assign.shape[0]
    rank_seq = lax.axis_index("seq")
    rank_tp = lax.axis_index("tp")
    seq_total = lax.axis_size("seq")
    tp_total = lax.axis_size("tp")
    groups = tp_total // 2
    feat = model_width // tp_total
    cent_rows = centroids.shape[0]
    slots = 2 * seg_total // owner_counts.shape[0]
    fine_np, coarse_np = angle_tables(seq_len)
    fine = jnp.asarray(fine_np)
    coarse = jnp.asarray(coarse_np)

    key_half, value_half = project_kv(tokens, w_key, w_value, fine, coarse)
    masks = range(1, seq_total)
    keys = [key_half] + [swapped(key_half, "seq", m) for m in masks]
    keys = keys + [swapped(k, "tp", 1) for k in keys]
    values = [value_half] + [swapped(value_half, "seq", m) for m in masks]
    values = values + [swapped(v, "tp", 1) for v in values]

    queries = project_q(tokens, w_query, fine, coarse)

    local = assign - rank_seq * cent_rows
    mine = (local >= 0) & (local < cent_rows)
    first_row = jnp.where(mine, local // GROUP * GROUP, 0)
    line = assign // GROUP
    order = jnp.arange(seg_total, dtype=i32)
    repeat = jnp.any((line[:, None] == line[None, :]) & (order[None, :] < order[:, None]), axis=1)
    place = jnp.stack([first_row, line * GROUP, (mine & ~repeat).astype(i32)])
    wide, norms, picked = widen_centroids(first_row, centroids)

    member = (
        lax.dynamic_slice_in_dim(seg_ids, rank_seq * tok_rows, tok_rows, 0)[:, None]
        == jnp.arange(seg_total, dtype=i32)[None, :]
    ).astype(bf16)
    token_cols = lax.dynamic_slice_in_dim(tokens, rank_tp * feat, feat, 1)
    pooled_tokens = lax.dot_general(
        member, token_cols, (((0,), (0,)), ((), ())), preferred_element_type=f32
    )
    pooled_tokens = [pooled_tokens] + [swapped(pooled_tokens, "seq", m) for m in masks]

    attended, counts = attend(seg_ids, queries, keys, values, seg_total)
    attended = [attended] + [swapped(attended, "seq", m) for m in masks]

    keep, send = mix(attended, norms, w_out, feat, groups)
    both = keep + swapped(send, "tp", 1)
    mixed = [both[0]] + [swapped(both[m], "tp", 2 * m) for m in range(1, groups)]

    keep, send, emb, norms = cross(
        owner_counts,
        mixed,
        pooled_tokens,
        counts,
        pool_gain.reshape(1, feat),
        centroids,
        slots,
        model_width,
    )
    both = keep + swapped(send, "tp", 1)
    terms = [both[0]] + [swapped(both[m], "tp", 2 * m) for m in range(1, groups)]
    assign_row = jnp.tile(assign, 3).reshape(1, 3 * seg_total)
    distances, updated = finish(
        owner_counts, place, terms, norms, emb, assign_row, picked, wide, model_width
    )
    return (distances, updated)


def solution(mesh):
    in_specs = (
        P("seq", None),
        P(None, "tp"),
        P(None, "tp"),
        P(None, "tp"),
        P("tp", None),
        P(),
        P(),
        P("seq", "tp"),
        P("tp"),
        P(),
    )
    out_specs = (P("tp", "seq"), P("seq", "tp"))
    return jax.shard_map(shards, mesh=mesh, in_specs=in_specs, out_specs=out_specs, check_vma=False)
```

time: 417 us -> 142 us (0.34)
  waiting for transfers between devices: 245 us -> 23.1 us
  matrix products: 73.8 us -> 1.68 us
  Pallas kernels: 0 us -> 52.2 us
  other arithmetic: 52.9 us -> 3.49 us
  starting transfers between devices: 9.94 us -> 49.4 us
  blocking collectives: 16 us -> 0 us
  between operations: 14.1 us -> 0.97 us
  local copies, waits for them, and re-layouts: 4.25 us -> 10.1 us
    reduce_scatter x2 -> x0, waiting for transfers between devices: 187 us -> none  [the longest x1 165 us: shards(): lax.psum_scatter(lax.dot_general(w_out, attention, (((0,), (1,)), ((), ()...]
    dot_general x13 -> x1, matrix products: 73.8 us -> 1.68 us  [shards(): lax.dot_general(member, token_cols, (((0,), (0,)), ((), ())), preferred_e...]
    pallas_call x0 -> x7, Pallas kernels: none -> 52.2 us  [the longest x1 12.2 us: attend(): pl.pallas_call(body, in_specs=[pl.BlockSpec(memory_space=pltpu.SMEM), who...]
    psum x1 -> x0, waiting for transfers between devices: 39.8 us -> none  [shards(): seg_sums = lax.psum(pooled_tokens + pooled_mixed, 'seq')]
    ppermute x4 -> x28, starting transfers between devices: 9.82 us -> 49.4 us  [swapped(): return lax.ppermute(x, axis, [(i, i ^ mask) for i in range(count)])]
    sub x3 -> x0, other arithmetic: 35.1 us -> none  [the longest x2 35.1 us: shards(): weights = jnp.exp(scores - highest)]
    psum x1 -> x0, blocking collectives: 16 us -> none  [shards(): square_sums = lax.psum(jnp.sum(pooled * pooled, axis=1), 'tp')]
    and x1 -> x0, other arithmetic: 7.01 us -> none  [shards(): (distance_grid >= 0) & (distance_grid < WINDOW)]
  transfers between devices with their start and end apart: 7 -> 28, of which waited for: 5 -> 11; matrix products, arithmetic and copies ran while one was open for 8% -> 4% of each run, Pallas kernels for 0% -> 13%
where the time goes in v1:
time: 142 us; the launch traced here: 141 us
  Pallas kernels  52.2 us (37%)
  starting transfers between devices  49.4 us (35%)
  waiting for transfers between devices  23.1 us (16%)
  local copies, waits for them, and re-layouts  10.1 us (7%)
  other arithmetic  3.49 us (2%)
  matrix products  1.68 us (1%)
    ppermute x28, starting transfers between devices, swapped(): return lax.ppermute(x, axis, [(i, i ^ mask) for i in range(count)])  49.4 us
    ppermute x28, waiting for transfers between devices, swapped(): return lax.ppermute(x, axis, [(i, i ^ mask) for i in range(count)])  23.1 us
    pallas_call x1, Pallas kernels, attend(): pl.pallas_call(body, in_specs=[pl.BlockSpec(memory_space=pltpu.SMEM), who...  12.2 us
    pallas_call x1, Pallas kernels, widen_centroids(): pl.pallas_call(cent_body, grid_spec=spec, out_shape=[jax.ShapeDtypeStruct...  10.3 us
    pallas_call x1, Pallas kernels, cross(): pl.pallas_call(body, grid_spec=spec, out_shape=[jax.ShapeDtypeStruct(side...  8.06 us
    pallas_call x1, Pallas kernels, project_kv(): pl.pallas_call(kv_body, grid=(rows // block,), in_specs=[pl.BlockSpec((bl...  7.78 us
    unnamed x60, local copies, waits for them, and re-layouts  7.46 us
    pallas_call x1, Pallas kernels, project_q(): pl.pallas_call(q_body, grid=(rows // block,), in_specs=[pl.BlockSpec((blo...  7.3 us
  transfers between devices with their start and end apart: 28, of which 11 were waited for; matrix products, arithmetic and copies ran while one was open for 4% of the time, Pallas kernels for 13%

profile of v1, /device:TPU:0, one launch (start us, length us, event | category | flops | bytes accessed | tf_op | source)
XLA Modules:
  0.0 140.9 jit_solution(13951827308838756017)
XLA Ops:
  0.6 2.4 %copy.17.wk = bf16[4096,64]{1,0:T(8,128)(2,1)} copy(bf16[4096,64]{0,1:T(8,128)(2,1)} %param.14) | data formatting | bytes 1048576 | tf_op args[2]
  3.0 2.4 %copy.18.wv = bf16[4096,64]{1,0:T(8,128)(2,1)} copy(bf16[4096,64]{0,1:T(8,128)(2,1)} %param.15) | data formatting | bytes 1048576 | tf_op args[3]
  5.4 7.8 %project_kv.1 = (bf16[64,1024]{1,0:T(8,128)(2,1)}, bf16[64,1024]{1,0:T(8,128)(2,1)}) custom-call(bf16[1024,4096]{1,0:T(8,128)(2,1)} %tok.3, bf16[4096,64]{1,0:T(8,128)(2,1)} %copy.17.wk, bf16[4096,64]{1,0:T(8,128)(2,1)} %copy.18.wv, f32[2,128,128]{2,1,0:T(8,128)} %constant.48.clone.fine, f32[2,32,128]{2,1,0:T(8,128)} %constant.49.clone.coarse), custom_call_target="tpu_custom_call" | custom-call | tf_op jit(solution)/shard_map/project_kv/pallas_call | solution.py:91
  13.2 0.5 collective-permute-start.3
  13.6 3.5 %collective-permute-start.2 = (bf16[64,1024]{1,0:T(8,128)(2,1)}, bf16[64,1024]{1,0:T(8,128)(2,1)S(1)}, u32[]{:S(2)}, u32[]{:S(2)}) collective-permute-start(bf16[64,1024]{1,0:T(8,128)(2,1)} %get-tuple-element.15.refs_3_), channel_id=1, source_target_pairs={{0,24},{8,16},{16,8},{24,0},{1,25},{9,17},{17,9},{25,1},{2,26},{10... | collective-permute-start | bytes 393224 | tf_op jit(solution)/shard_map/ppermute | solution.py:29
  17.2 0.5 collective-permute-start.1
  17.7 0.1 collective-permute-start
  17.8 0.0 collective-permute-start.10
  17.8 0.0 collective-permute-done.3.refs_7_
  17.8 2.9 %collective-permute-start.9 = (bf16[64,1024]{1,0:T(8,128)(2,1)}, bf16[64,1024]{1,0:T(8,128)(2,1)S(1)}, u32[]{:S(2)}, u32[]{:S(2)}) collective-permute-start(bf16[64,1024]{1,0:T(8,128)(2,1)} %get-tuple-element.16.refs_11_), channel_id=1, source_target_pairs={{0,24},{8,16},{16,8},{24,0},{1,25},{9,17},{17,9},{25,1},{2,26},{10... | collective-permute-start | bytes 393224 | tf_op jit(solution)/shard_map/ppermute | solution.py:29
  20.7 0.8 collective-permute-done.2.refs_6_
  21.6 2.1 %collective-permute-start.8 = (bf16[64,1024]{1,0:T(8,128)(2,1)}, bf16[64,1024]{1,0:T(8,128)(2,1)S(1)}, u32[]{:S(2)}, u32[]{:S(2)}) collective-permute-start(bf16[64,1024]{1,0:T(8,128)(2,1)} %get-tuple-element.16.refs_11_), channel_id=1, source_target_pairs={{0,16},{8,24},{16,0},{24,8},{1,17},{9,25},{17,1},{25,9},{2,18},{10... | collective-permute-start | bytes 393224 | tf_op jit(solution)/shard_map/ppermute | solution.py:29
  23.7 1.6 %collective-permute-done.1.refs_5_ = bf16[64,1024]{1,0:T(8,128)(2,1)S(1)} collective-permute-done((bf16[64,1024]{1,0:T(8,128)(2,1)}, bf16[64,1024]{1,0:T(8,128)(2,1)S(1)}, u32[]{:S(2)}, u32[]{:S(2)}) %collective-permute-start.1) | collective-permute-done | bytes 131104 | tf_op jit(solution)/shard_map/ppermute | solution.py:29
  25.3 1.2 collective-permute-start.7
  26.5 0.0 collective-permute-start.6
  26.5 0.0 collective-permute-done.10.refs_15_
  26.5 0.5 collective-permute-start.5
  27.0 0.2 collective-permute-done.9.refs_14_
  27.2 2.7 %collective-permute-done.8.refs_13_ = bf16[64,1024]{1,0:T(8,128)(2,1)S(1)} collective-permute-done((bf16[64,1024]{1,0:T(8,128)(2,1)}, bf16[64,1024]{1,0:T(8,128)(2,1)S(1)}, u32[]{:S(2)}, u32[]{:S(2)}) %collective-permute-start.8) | collective-permute-done | bytes 131104 | tf_op jit(solution)/shard_map/ppermute | solution.py:29
  29.9 0.9 collective-permute-done.7.refs_12_
  30.8 0.5 collective-permute-start.11
  31.3 7.3 %project_q.1.refs_1_ = bf16[1024,256]{1,0:T(8,128)(2,1)} custom-call(bf16[1024,4096]{1,0:T(8,128)(2,1)} %tok.3, bf16[4096,256]{1,0:T(8,128)(2,1)} %wq.1, f32[2,128,128]{2,1,0:T(8,128)} %constant.48.clone.fine, f32[2,32,128]{2,1,0:T(8,128)} %constant.49.clone.coarse), custom_call_target="tpu_custom_call" | custom-call | tf_op jit(solution)/shard_map/project_q/pallas_call | solution.py:134
  38.8 0.5 copy-done.13
  39.3 0.1 copy-done.14
  39.3 0.1 copy-done.15
  39.4 0.0 copy-done.16
  39.4 0.0 copy-done.17
  39.5 12.2 %attend.1 = (f32[32,256]{1,0:T(8,128)}, f32[32,128]{1,0:T(8,128)}) custom-call(s32[4096]{0:T(1024)} %refs_0_.3, bf16[1024,256]{1,0:T(8,128)(2,1)} %project_q.1.refs_1_, s32[1,4096]{1,0:T(1,128)} %bitcast.23, bf16[64,1024]{1,0:T(8,128)(2,1)} %get-tuple-element.15.refs_3_, bf16[64,1024]{1,0:T(8,128)(2,1)} %copy-done.7, bf16[64,1024]{1,0:T(8,128)(2,1)} %copy-done.6, ...), custom_call_target="tpu_custom_call" | custom-call | tf_op jit(solution)/shard_map/attend/pallas_call | solution.py:357
  51.6 24.6 %collective-permute-start.16 = (f32[32,256]{1,0:T(8,128)}, f32[32,256]{1,0:T(8,128)S(1)}, u32[]{:S(2)}, u32[]{:S(2)}) collective-permute-start(f32[32,256]{1,0:T(8,128)} %get-tuple-element.17.refs_0_), channel_id=1, source_target_pairs={{0,24},{8,16},{16,8},{24,0},{1,25},{9,17},{17,9},{25,1},{2,26},{10... | collective-permute-start | bytes 98312 | tf_op jit(solution)/shard_map/ppermute | solution.py:29
  76.2 0.6 collective-permute-start.14
  76.8 0.6 multiply_bitcast_fusion
  77.4 10.3 %widen_centroids.1 = (f32[4096,512]{1,0:T(8,128)}, f32[8,512]{1,0:T(8,128)}, bf16[512,512]{1,0:T(8,128)(2,1)}) custom-call(s32[32]{0:T(128)} %get-tuple-element.38.base, bf16[4096,512]{1,0:T(8,128)(2,1)} %refs_11_.1, bf16[4096,512]{1,0:T(8,128)(2,1)} %refs_11_.1), custom_call_target="tpu_custom_call" | custom-call | tf_op jit(solution)/shard_map/widen_centroids/pallas_call | solution.py:200
  87.8 0.0 copy-start.26
  87.8 0.6 copy-done.24
  88.4 0.0 copy-done.25
  88.4 0.0 copy-done.26
  88.4 2.9 %mix.1 = (f32[4,40,512]{2,1,0:T(8,128)}, f32[4,40,512]{2,1,0:T(8,128)}) custom-call(f32[32,256]{1,0:T(8,128)} %get-tuple-element.17.refs_0_, f32[32,256]{1,0:T(8,128)} %copy-done.26, f32[32,256]{1,0:T(8,128)} %copy-done.25, f32[32,256]{1,0:T(8,128)} %copy-done.24, f32[8,512]{1,0:T(8,128)} %get-tuple-element.18.refs_4_, bf16[256,4096]{1,0:T(8,128)(2,1)} %refs_5_.1), custom_call_target="tpu_custom_call" | custom-call | tf_op jit(solution)/shard_map/mix/pallas_call | solution.py:407
  91.4 0.7 dynamic_slice.6
  92.0 1.7 %fusion.refs_5_ = f32[32,512]{1,0:T(8,128)S(1)} fusion(bf16[1024,4096]{1,0:T(8,128)(2,1)} %tok.3, s32[]{:T(128)S(6)} %select_n.22, s32[1024]{0:T(1024)S(1)} %dynamic_slice.6), kind=kOutput, calls=%fused_computation | convolution fusion | flops 33587200 | bytes 1118212 | tf_op jit(solution)/shard_map/dot_general | solution.py:653
  93.7 3.0 %collective-permute-start.23 = (f32[32,512]{1,0:T(8,128)S(1)}, f32[32,512]{1,0:T(8,128)S(1)}, u32[]{:S(2)}, u32[]{:S(2)}) collective-permute-start(f32[32,512]{1,0:T(8,128)S(1)} %fusion.refs_5_), channel_id=1, source_target_pairs={{0,24},{8,16},{16,8},{24,0},{1,25},{9,17},{17,9},{25,1},{2,26},{10... | collective-permute-start | bytes 196616 | tf_op jit(solution)/shard_map/ppermute | solution.py:29
  96.8 1.0 add.14
  97.8 0.7 slice_bitcast_fusion.4
  98.4 3.6 %collective-permute-start.20 = (f32[40,512]{1,0:T(8,128)S(1)}, f32[40,512]{1,0:T(8,128)S(1)}, u32[]{:S(2)}, u32[]{:S(2)}) collective-permute-start(f32[40,512]{1,0:T(8,128)S(1)} %get-tuple-element.34), channel_id=1, source_target_pairs={{0,6},{1,7},{2,4},{3,5},{4,2},{5,3},{6,0},{7,1},{8,14},{9,15},{10,... | collective-permute-start | bytes 245768 | tf_op jit(solution)/shard_map/ppermute | solution.py:29
  102.0 0.8 collective-permute-start.18
  102.8 0.6 collective-permute-start.21
  103.4 3.7 %collective-permute-done.22.refs_7_ = f32[32,512]{1,0:T(8,128)S(1)} collective-permute-done((f32[32,512]{1,0:T(8,128)S(1)}, f32[32,512]{1,0:T(8,128)S(1)}, u32[]{:S(2)}, u32[]{:S(2)}) %collective-permute-start.22) | collective-permute-done | bytes 65568 | tf_op jit(solution)/shard_map/ppermute | solution.py:29
  107.1 0.1 collective-permute-done.21.refs_6_
  107.2 2.1 %collective-permute-done.19.refs_3_ = f32[40,512]{1,0:T(8,128)S(1)} collective-permute-done((f32[40,512]{1,0:T(8,128)S(1)}, f32[40,512]{1,0:T(8,128)S(1)}, u32[]{:S(2)}, u32[]{:S(2)}) %collective-permute-start.19) | collective-permute-done | bytes 81952 | tf_op jit(solution)/shard_map/ppermute | solution.py:29
  109.3 0.6 copy-done.19
  109.9 0.0 copy-done.20
  110.0 8.1 %cross.1 = (f32[4,8,4224]{2,1,0:T(8,128)}, f32[4,8,4224]{2,1,0:T(8,128)}, f32[32,512]{1,0:T(8,128)}, f32[8,512]{1,0:T(8,128)}) custom-call(s32[8]{0:T(128)} %refs_0_.5, f32[40,512]{1,0:T(8,128)} %get-tuple-element.37.refs_1_, f32[40,512]{1,0:T(8,128)} %copy-done.20, f32[40,512]{1,0:T(8,128)} %copy-done.19, f32[40,512]{1,0:T(8,128)} %copy-done.18, ...), custom_call_target="tpu_custom_call" | custom-call | tf_op jit(solution)/shard_map/cross/pallas_call | solution.py:509
  118.0 0.2 fusion.4
  118.2 2.0 %collective-permute-done.24 = f32[4,8,4224]{2,1,0:T(8,128)S(1)} collective-permute-done((f32[4,8,4224]{2,1,0:T(8,128)}, f32[4,8,4224]{2,1,0:T(8,128)S(1)}, u32[]{:S(2)}, u32[]{:S(2)}) %collective-permute-start.24) | collective-permute-done | bytes 540704 | tf_op jit(solution)/shard_map/ppermute | solution.py:29
  120.2 1.1 add.17
  121.3 0.7 slice_bitcast_fusion
  122.0 2.5 %collective-permute-start.27 = (f32[8,4224]{1,0:T(8,128)S(1)}, f32[8,4224]{1,0:T(8,128)S(1)}, u32[]{:S(2)}, u32[]{:S(2)}) collective-permute-start(f32[8,4224]{1,0:T(8,128)S(1)} %get-tuple-element.30), channel_id=1, source_target_pairs={{0,6},{1,7},{2,4},{3,5},{4,2},{5,3},{6,0},{7,1},{8,14},{9,15},{10,... | collective-permute-start | bytes 405512 | tf_op jit(solution)/shard_map/ppermute | solution.py:29
  124.4 1.9 %collective-permute-start.25 = (f32[8,4224]{1,0:T(8,128)S(1)}, f32[8,4224]{1,0:T(8,128)S(1)}, u32[]{:S(2)}, u32[]{:S(2)}) collective-permute-start(f32[8,4224]{1,0:T(8,128)S(1)} %get-tuple-element.32), channel_id=1, source_target_pairs={{0,2},{1,3},{2,0},{3,1},{4,6},{5,7},{6,4},{7,5},{8,10},{9,11},{10,... | collective-permute-start | bytes 405512 | tf_op jit(solution)/shard_map/ppermute | solution.py:29
  126.3 0.6 reshape_tile.3.refs_8_
  126.9 0.6 pad_add_fusion.refs_1_
  127.5 2.8 %collective-permute-done.27.refs_5_ = f32[8,4224]{1,0:T(8,128)S(1)} collective-permute-done((f32[8,4224]{1,0:T(8,128)S(1)}, f32[8,4224]{1,0:T(8,128)S(1)}, u32[]{:S(2)}, u32[]{:S(2)}) %collective-permute-start.27) | collective-permute-done | bytes 135200 | tf_op jit(solution)/shard_map/ppermute | solution.py:29
  130.3 6.2 %collective-permute-done.26.refs_4_ = f32[8,4224]{1,0:T(8,128)S(1)} collective-permute-done((f32[8,4224]{1,0:T(8,128)S(1)}, f32[8,4224]{1,0:T(8,128)S(1)}, u32[]{:S(2)}, u32[]{:S(2)}) %collective-permute-start.26) | collective-permute-done | bytes 135200 | tf_op jit(solution)/shard_map/ppermute | solution.py:29
  136.6 0.6 copy-done.2
  137.2 0.1 copy-done.3
  137.3 3.7 %finish.1 = (f32[8,4096]{1,0:T(8,128)}, f32[4096,512]{1,0:T(8,128)}) custom-call(s32[8]{0:T(128)} %refs_0_.5, s32[3,32]{1,0:T(4,128)} %pad_add_fusion.refs_1_, f32[8,4224]{1,0:T(8,128)} %get-tuple-element.33.refs_2_, f32[8,4224]{1,0:T(8,128)} %copy-done.3, f32[8,4224]{1,0:T(8,128)} %copy-done.2, ...), custom_call_target="tpu_custom_call", output_to_operand_aliasing={{1}: (10, {})} | custom-call | tf_op jit(solution)/shard_map/finish/pallas_call | solution.py:594
  (71 shorter events, 0.2 us)
Async XLA Ops:
  13.2 63.7 %copy-start.28 = (s32[32]{0:T(128)S(1)}, s32[32]{0:T(128)}, u32[]{:S(2)}) copy-start(s32[32]{0:T(128)} %param.21) | copy-start | bytes 388
  13.2 4.6 %collective-permute-start.3 = (bf16[64,1024]{1,0:T(8,128)(2,1)}, bf16[64,1024]{1,0:T(8,128)(2,1)S(1)}, u32[]{:S(2)}, u32[]{:S(2)}) collective-permute-start(bf16[64,1024]{1,0:T(8,128)(2,1)} %get-tuple-element.15.refs_3_), channel_id=1, source_target_pairs={{0,1},{1,0},{2,3},{3,2},{4,5},{5,4},{6,7},{7,6},{8,9},{9,8},{10,11... | collective-permute-start | bytes 393224 | tf_op jit(solution)/shard_map/ppermute | solution.py:29
  13.6 7.9 %collective-permute-start.2 = (bf16[64,1024]{1,0:T(8,128)(2,1)}, bf16[64,1024]{1,0:T(8,128)(2,1)S(1)}, u32[]{:S(2)}, u32[]{:S(2)}) collective-permute-start(bf16[64,1024]{1,0:T(8,128)(2,1)} %get-tuple-element.15.refs_3_), channel_id=1, source_target_pairs={{0,24},{8,16},{16,8},{24,0},{1,25},{9,17},{17,9},{25,1},{2,26},{10... | collective-permute-start | bytes 393224 | tf_op jit(solution)/shard_map/ppermute | solution.py:29
  17.2 8.1 %collective-permute-start.1 = (bf16[64,1024]{1,0:T(8,128)(2,1)}, bf16[64,1024]{1,0:T(8,128)(2,1)S(1)}, u32[]{:S(2)}, u32[]{:S(2)}) collective-permute-start(bf16[64,1024]{1,0:T(8,128)(2,1)} %get-tuple-element.15.refs_3_), channel_id=1, source_target_pairs={{0,16},{8,24},{16,0},{24,8},{1,17},{9,25},{17,1},{25,9},{2,18},{10... | collective-permute-start | bytes 393224 | tf_op jit(solution)/shard_map/ppermute | solution.py:29
  17.7 8.8 %collective-permute-start = (bf16[64,1024]{1,0:T(8,128)(2,1)}, bf16[64,1024]{1,0:T(8,128)(2,1)S(1)}, u32[]{:S(2)}, u32[]{:S(2)}) collective-permute-start(bf16[64,1024]{1,0:T(8,128)(2,1)} %get-tuple-element.15.refs_3_), channel_id=1, source_target_pairs={{0,8},{8,0},{16,24},{24,16},{1,9},{9,1},{17,25},{25,17},{2,10},{10... | collective-permute-start | bytes 393224 | tf_op jit(solution)/shard_map/ppermute | solution.py:29
  17.8 8.7 %collective-permute-start.10 = (bf16[64,1024]{1,0:T(8,128)(2,1)}, bf16[64,1024]{1,0:T(8,128)(2,1)S(1)}, u32[]{:S(2)}, u32[]{:S(2)}) collective-permute-start(bf16[64,1024]{1,0:T(8,128)(2,1)} %get-tuple-element.16.refs_11_), channel_id=1, source_target_pairs={{0,1},{1,0},{2,3},{3,2},{4,5},{5,4},{6,7},{7,6},{8,9},{9,8},{10,11... | collective-permute-start | bytes 393224 | tf_op jit(solution)/shard_map/ppermute | solution.py:29
  17.8 20.9 %copy-start.4 = (bf16[64,1024]{1,0:T(8,128)(2,1)}, bf16[64,1024]{1,0:T(8,128)(2,1)S(1)}, u32[]{:S(2)}) copy-start(bf16[64,1024]{1,0:T(8,128)(2,1)S(1)} %collective-permute-done.3.refs_7_) | copy-start | bytes 393220
  17.8 9.4 %collective-permute-start.9 = (bf16[64,1024]{1,0:T(8,128)(2,1)}, bf16[64,1024]{1,0:T(8,128)(2,1)S(1)}, u32[]{:S(2)}, u32[]{:S(2)}) collective-permute-start(bf16[64,1024]{1,0:T(8,128)(2,1)} %get-tuple-element.16.refs_11_), channel_id=1, source_target_pairs={{0,24},{8,16},{16,8},{24,0},{1,25},{9,17},{17,9},{25,1},{2,26},{10... | collective-permute-start | bytes 393224 | tf_op jit(solution)/shard_map/ppermute | solution.py:29
  21.6 17.1 %copy-start.5 = (bf16[64,1024]{1,0:T(8,128)(2,1)}, bf16[64,1024]{1,0:T(8,128)(2,1)S(1)}, u32[]{:S(2)}) copy-start(bf16[64,1024]{1,0:T(8,128)(2,1)S(1)} %collective-permute-done.2.refs_6_) | copy-start | bytes 393220
  21.6 8.3 %collective-permute-start.8 = (bf16[64,1024]{1,0:T(8,128)(2,1)}, bf16[64,1024]{1,0:T(8,128)(2,1)S(1)}, u32[]{:S(2)}, u32[]{:S(2)}) collective-permute-start(bf16[64,1024]{1,0:T(8,128)(2,1)} %get-tuple-element.16.refs_11_), channel_id=1, source_target_pairs={{0,16},{8,24},{16,0},{24,8},{1,17},{9,25},{17,1},{25,9},{2,18},{10... | collective-permute-start | bytes 393224 | tf_op jit(solution)/shard_map/ppermute | solution.py:29
  25.3 13.4 %copy-start.6 = (bf16[64,1024]{1,0:T(8,128)(2,1)}, bf16[64,1024]{1,0:T(8,128)(2,1)S(1)}, u32[]{:S(2)}) copy-start(bf16[64,1024]{1,0:T(8,128)(2,1)S(1)} %collective-permute-done.1.refs_5_) | copy-start | bytes 393220
  25.3 5.5 %collective-permute-start.7 = (bf16[64,1024]{1,0:T(8,128)(2,1)}, bf16[64,1024]{1,0:T(8,128)(2,1)S(1)}, u32[]{:S(2)}, u32[]{:S(2)}) collective-permute-start(bf16[64,1024]{1,0:T(8,128)(2,1)} %get-tuple-element.16.refs_11_), channel_id=1, source_target_pairs={{0,8},{8,0},{16,24},{24,16},{1,9},{9,1},{17,25},{25,17},{2,10},{10... | collective-permute-start | bytes 393224 | tf_op jit(solution)/shard_map/ppermute | solution.py:29
  26.5 12.2 %copy-start.7 = (bf16[64,1024]{1,0:T(8,128)(2,1)}, bf16[64,1024]{1,0:T(8,128)(2,1)S(1)}, u32[]{:S(2)}) copy-start(bf16[64,1024]{1,0:T(8,128)(2,1)S(1)} %collective-permute-done.refs_4_) | copy-start | bytes 393220
  26.5 4.3 %collective-permute-start.6 = (bf16[64,1024]{1,0:T(8,128)(2,1)S(1)}, bf16[64,1024]{1,0:T(8,128)(2,1)S(1)}, u32[]{:S(2)}, u32[]{:S(2)}) collective-permute-start(bf16[64,1024]{1,0:T(8,128)(2,1)S(1)} %collective-permute-done.2.refs_6_), channel_id=1, source_target_pairs={{0,1},{1,0},{2,3},{3,2},{4,5},{5,4},{6,7},{7,6},{8,9},{9,8},{10,11... | collective-permute-start | bytes 393224 | tf_op jit(solution)/shard_map/ppermute | solution.py:29
  26.5 12.2 %copy-start.8 = (bf16[64,1024]{1,0:T(8,128)(2,1)}, bf16[64,1024]{1,0:T(8,128)(2,1)S(1)}, u32[]{:S(2)}) copy-start(bf16[64,1024]{1,0:T(8,128)(2,1)S(1)} %collective-permute-done.10.refs_15_) | copy-start | bytes 393220
  26.5 12.1 %collective-permute-start.5 = (bf16[64,1024]{1,0:T(8,128)(2,1)S(1)}, bf16[64,1024]{1,0:T(8,128)(2,1)S(1)}, u32[]{:S(2)}, u32[]{:S(2)}) collective-permute-start(bf16[64,1024]{1,0:T(8,128)(2,1)S(1)} %collective-permute-done.1.refs_5_), channel_id=1, source_target_pairs={{0,1},{1,0},{2,3},{3,2},{4,5},{5,4},{6,7},{7,6},{8,9},{9,8},{10,11... | collective-permute-start | bytes 393224 | tf_op jit(solution)/shard_map/ppermute | solution.py:29
  27.2 11.6 %copy-start.9 = (bf16[64,1024]{1,0:T(8,128)(2,1)}, bf16[64,1024]{1,0:T(8,128)(2,1)S(1)}, u32[]{:S(2)}) copy-start(bf16[64,1024]{1,0:T(8,128)(2,1)S(1)} %collective-permute-done.9.refs_14_) | copy-start | bytes 393220
  27.2 11.4 %collective-permute-start.4 = (bf16[64,1024]{1,0:T(8,128)(2,1)S(1)}, bf16[64,1024]{1,0:T(8,128)(2,1)S(1)}, u32[]{:S(2)}, u32[]{:S(2)}) collective-permute-start(bf16[64,1024]{1,0:T(8,128)(2,1)S(1)} %collective-permute-done.refs_4_), channel_id=1, source_target_pairs={{0,1},{1,0},{2,3},{3,2},{4,5},{5,4},{6,7},{7,6},{8,9},{9,8},{10,11... | collective-permute-start | bytes 393224 | tf_op jit(solution)/shard_map/ppermute | solution.py:29
  29.9 8.9 %copy-start.10 = (bf16[64,1024]{1,0:T(8,128)(2,1)}, bf16[64,1024]{1,0:T(8,128)(2,1)S(1)}, u32[]{:S(2)}) copy-start(bf16[64,1024]{1,0:T(8,128)(2,1)S(1)} %collective-permute-done.8.refs_13_) | copy-start | bytes 393220
  29.9 8.7 %collective-permute-start.13 = (bf16[64,1024]{1,0:T(8,128)(2,1)S(1)}, bf16[64,1024]{1,0:T(8,128)(2,1)S(1)}, u32[]{:S(2)}, u32[]{:S(2)}) collective-permute-start(bf16[64,1024]{1,0:T(8,128)(2,1)S(1)} %collective-permute-done.9.refs_14_), channel_id=1, source_target_pairs={{0,1},{1,0},{2,3},{3,2},{4,5},{5,4},{6,7},{7,6},{8,9},{9,8},{10,11... | collective-permute-start | bytes 393224 | tf_op jit(solution)/shard_map/ppermute | solution.py:29
  30.8 8.0 %copy-start.11 = (bf16[64,1024]{1,0:T(8,128)(2,1)}, bf16[64,1024]{1,0:T(8,128)(2,1)S(1)}, u32[]{:S(2)}) copy-start(bf16[64,1024]{1,0:T(8,128)(2,1)S(1)} %collective-permute-done.7.refs_12_) | copy-start | bytes 393220
  30.8 7.9 %collective-permute-start.12 = (bf16[64,1024]{1,0:T(8,128)(2,1)S(1)}, bf16[64,1024]{1,0:T(8,128)(2,1)S(1)}, u32[]{:S(2)}, u32[]{:S(2)}) collective-permute-start(bf16[64,1024]{1,0:T(8,128)(2,1)S(1)} %collective-permute-done.8.refs_13_), channel_id=1, source_target_pairs={{0,1},{1,0},{2,3},{3,2},{4,5},{5,4},{6,7},{7,6},{8,9},{9,8},{10,11... | collective-permute-start | bytes 393224 | tf_op jit(solution)/shard_map/ppermute | solution.py:29
  30.8 8.0 %copy-start.12 = (bf16[64,1024]{1,0:T(8,128)(2,1)}, bf16[64,1024]{1,0:T(8,128)(2,1)S(1)}, u32[]{:S(2)}) copy-start(bf16[64,1024]{1,0:T(8,128)(2,1)S(1)} %collective-permute-done.6.refs_10_) | copy-start | bytes 393220
  30.8 7.9 %collective-permute-start.11 = (bf16[64,1024]{1,0:T(8,128)(2,1)S(1)}, bf16[64,1024]{1,0:T(8,128)(2,1)S(1)}, u32[]{:S(2)}, u32[]{:S(2)}) collective-permute-start(bf16[64,1024]{1,0:T(8,128)(2,1)S(1)} %collective-permute-done.7.refs_12_), channel_id=1, source_target_pairs={{0,1},{1,0},{2,3},{3,2},{4,5},{5,4},{6,7},{7,6},{8,9},{9,8},{10,11... | collective-permute-start | bytes 393224 | tf_op jit(solution)/shard_map/ppermute | solution.py:29
  38.6 0.7 copy-start.13
  38.6 0.7 copy-start.14
  38.6 0.7 copy-start.15
  38.7 0.8 copy-start.16
  38.7 0.8 copy-start.17
  51.6 36.2 %collective-permute-start.16 = (f32[32,256]{1,0:T(8,128)}, f32[32,256]{1,0:T(8,128)S(1)}, u32[]{:S(2)}, u32[]{:S(2)}) collective-permute-start(f32[32,256]{1,0:T(8,128)} %get-tuple-element.17.refs_0_), channel_id=1, source_target_pairs={{0,24},{8,16},{16,8},{24,0},{1,25},{9,17},{17,9},{25,1},{2,26},{10... | collective-permute-start | bytes 98312 | tf_op jit(solution)/shard_map/ppermute | solution.py:29
  76.2 11.6 %collective-permute-start.15 = (f32[32,256]{1,0:T(8,128)}, f32[32,256]{1,0:T(8,128)S(1)}, u32[]{:S(2)}, u32[]{:S(2)}) collective-permute-start(f32[32,256]{1,0:T(8,128)} %get-tuple-element.17.refs_0_), channel_id=1, source_target_pairs={{0,16},{8,24},{16,0},{24,8},{1,17},{9,25},{17,1},{25,9},{2,18},{10... | collective-permute-start | bytes 98312 | tf_op jit(solution)/shard_map/ppermute | solution.py:29
  76.2 11.6 %collective-permute-start.14 = (f32[32,256]{1,0:T(8,128)}, f32[32,256]{1,0:T(8,128)S(1)}, u32[]{:S(2)}, u32[]{:S(2)}) collective-permute-start(f32[32,256]{1,0:T(8,128)} %get-tuple-element.17.refs_0_), channel_id=1, source_target_pairs={{0,8},{8,0},{16,24},{24,16},{1,9},{9,1},{17,25},{25,17},{2,10},{10... | collective-permute-start | bytes 98312 | tf_op jit(solution)/shard_map/ppermute | solution.py:29
  77.4 49.5 %copy-start.27 = (s32[32]{0:T(128)S(1)}, s32[32]{0:T(128)}, u32[]{:S(2)}) copy-start(s32[32]{0:T(128)} %get-tuple-element.38.base) | copy-start | bytes 388
  87.8 0.6 copy-start.24
  87.8 0.6 copy-start.25
  87.8 0.6 copy-start.26
  91.4 5.4 %collective-permute-start.17 = (f32[4,40,512]{2,1,0:T(8,128)}, f32[4,40,512]{2,1,0:T(8,128)S(1)}, u32[]{:S(2)}, u32[]{:S(2)}) collective-permute-start(f32[4,40,512]{2,1,0:T(8,128)} %get-tuple-element.20), channel_id=1, source_target_pairs={{0,1},{1,0},{2,3},{3,2},{4,5},{5,4},{6,7},{7,6},{8,9},{9,8},{10,11... | collective-permute-start | bytes 983048 | tf_op jit(solution)/shard_map/ppermute | solution.py:29
  93.7 15.6 %copy-start = (f32[32,512]{1,0:T(8,128)}, f32[32,512]{1,0:T(8,128)S(1)}, u32[]{:S(2)}) copy-start(f32[32,512]{1,0:T(8,128)S(1)} %fusion.refs_5_) | copy-start | bytes 196612
  93.7 9.1 %collective-permute-start.23 = (f32[32,512]{1,0:T(8,128)S(1)}, f32[32,512]{1,0:T(8,128)S(1)}, u32[]{:S(2)}, u32[]{:S(2)}) collective-permute-start(f32[32,512]{1,0:T(8,128)S(1)} %fusion.refs_5_), channel_id=1, source_target_pairs={{0,24},{8,16},{16,8},{24,0},{1,25},{9,17},{17,9},{25,1},{2,26},{10... | collective-permute-start | bytes 196616 | tf_op jit(solution)/shard_map/ppermute | solution.py:29
  98.4 8.7 %collective-permute-start.20 = (f32[40,512]{1,0:T(8,128)S(1)}, f32[40,512]{1,0:T(8,128)S(1)}, u32[]{:S(2)}, u32[]{:S(2)}) collective-permute-start(f32[40,512]{1,0:T(8,128)S(1)} %get-tuple-element.34), channel_id=1, source_target_pairs={{0,6},{1,7},{2,4},{3,5},{4,2},{5,3},{6,0},{7,1},{8,14},{9,15},{10,... | collective-permute-start | bytes 245768 | tf_op jit(solution)/shard_map/ppermute | solution.py:29
  102.0 7.3 %collective-permute-start.19 = (f32[40,512]{1,0:T(8,128)S(1)}, f32[40,512]{1,0:T(8,128)S(1)}, u32[]{:S(2)}, u32[]{:S(2)}) collective-permute-start(f32[40,512]{1,0:T(8,128)S(1)} %get-tuple-element.35), channel_id=1, source_target_pairs={{0,4},{1,5},{2,6},{3,7},{4,0},{5,1},{6,2},{7,3},{8,12},{9,13},{10,... | collective-permute-start | bytes 245768 | tf_op jit(solution)/shard_map/ppermute | solution.py:29
  102.0 7.3 %collective-permute-start.18 = (f32[40,512]{1,0:T(8,128)S(1)}, f32[40,512]{1,0:T(8,128)S(1)}, u32[]{:S(2)}, u32[]{:S(2)}) collective-permute-start(f32[40,512]{1,0:T(8,128)S(1)} %get-tuple-element.36), channel_id=1, source_target_pairs={{0,2},{1,3},{2,0},{3,1},{4,6},{5,7},{6,4},{7,5},{8,10},{9,11},{10,... | collective-permute-start | bytes 245768 | tf_op jit(solution)/shard_map/ppermute | solution.py:29
  102.8 4.3 %collective-permute-start.22 = (f32[32,512]{1,0:T(8,128)S(1)}, f32[32,512]{1,0:T(8,128)S(1)}, u32[]{:S(2)}, u32[]{:S(2)}) collective-permute-start(f32[32,512]{1,0:T(8,128)S(1)} %fusion.refs_5_), channel_id=1, source_target_pairs={{0,16},{8,24},{16,0},{24,8},{1,17},{9,25},{17,1},{25,9},{2,18},{10... | collective-permute-start | bytes 196616 | tf_op jit(solution)/shard_map/ppermute | solution.py:29
  102.8 6.5 %copy-start.21 = (f32[32,512]{1,0:T(8,128)}, f32[32,512]{1,0:T(8,128)S(1)}, u32[]{:S(2)}) copy-start(f32[32,512]{1,0:T(8,128)S(1)} %collective-permute-done.23.refs_8_) | copy-start | bytes 196612
  102.8 4.3 %collective-permute-start.21 = (f32[32,512]{1,0:T(8,128)S(1)}, f32[32,512]{1,0:T(8,128)S(1)}, u32[]{:S(2)}, u32[]{:S(2)}) collective-permute-start(f32[32,512]{1,0:T(8,128)S(1)} %fusion.refs_5_), channel_id=1, source_target_pairs={{0,8},{8,0},{16,24},{24,16},{1,9},{9,1},{17,25},{25,17},{2,10},{10... | collective-permute-start | bytes 196616 | tf_op jit(solution)/shard_map/ppermute | solution.py:29
  107.1 2.2 %copy-start.22 = (f32[32,512]{1,0:T(8,128)}, f32[32,512]{1,0:T(8,128)S(1)}, u32[]{:S(2)}) copy-start(f32[32,512]{1,0:T(8,128)S(1)} %collective-permute-done.22.refs_7_) | copy-start | bytes 196612
  107.2 2.2 %copy-start.23 = (f32[32,512]{1,0:T(8,128)}, f32[32,512]{1,0:T(8,128)S(1)}, u32[]{:S(2)}) copy-start(f32[32,512]{1,0:T(8,128)S(1)} %collective-permute-done.21.refs_6_) | copy-start | bytes 196612
  107.2 2.2 %copy-start.18 = (f32[40,512]{1,0:T(8,128)}, f32[40,512]{1,0:T(8,128)S(1)}, u32[]{:S(2)}) copy-start(f32[40,512]{1,0:T(8,128)S(1)} %collective-permute-done.20.refs_4_) | copy-start | bytes 245764
  109.3 0.6 copy-start.19
  109.3 0.7 copy-start.20
  118.0 2.1 %collective-permute-start.24 = (f32[4,8,4224]{2,1,0:T(8,128)}, f32[4,8,4224]{2,1,0:T(8,128)S(1)}, u32[]{:S(2)}, u32[]{:S(2)}) collective-permute-start(f32[4,8,4224]{2,1,0:T(8,128)} %get-tuple-element.23), channel_id=1, source_target_pairs={{0,1},{1,0},{2,3},{3,2},{4,5},{5,4},{6,7},{7,6},{8,9},{9,8},{10,11... | collective-permute-start | bytes 1622024 | tf_op jit(solution)/shard_map/ppermute | solution.py:29
  122.0 8.4 %collective-permute-start.27 = (f32[8,4224]{1,0:T(8,128)S(1)}, f32[8,4224]{1,0:T(8,128)S(1)}, u32[]{:S(2)}, u32[]{:S(2)}) collective-permute-start(f32[8,4224]{1,0:T(8,128)S(1)} %get-tuple-element.30), channel_id=1, source_target_pairs={{0,6},{1,7},{2,4},{3,5},{4,2},{5,3},{6,0},{7,1},{8,14},{9,15},{10,... | collective-permute-start | bytes 405512 | tf_op jit(solution)/shard_map/ppermute | solution.py:29
  124.4 12.1 %collective-permute-start.26 = (f32[8,4224]{1,0:T(8,128)S(1)}, f32[8,4224]{1,0:T(8,128)S(1)}, u32[]{:S(2)}, u32[]{:S(2)}) collective-permute-start(f32[8,4224]{1,0:T(8,128)S(1)} %get-tuple-element.31), channel_id=1, source_target_pairs={{0,4},{1,5},{2,6},{3,7},{4,0},{5,1},{6,2},{7,3},{8,12},{9,13},{10,... | collective-permute-start | bytes 405512 | tf_op jit(solution)/shard_map/ppermute | solution.py:29
  124.4 12.1 %collective-permute-start.25 = (f32[8,4224]{1,0:T(8,128)S(1)}, f32[8,4224]{1,0:T(8,128)S(1)}, u32[]{:S(2)}, u32[]{:S(2)}) collective-permute-start(f32[8,4224]{1,0:T(8,128)S(1)} %get-tuple-element.32), channel_id=1, source_target_pairs={{0,2},{1,3},{2,0},{3,1},{4,6},{5,7},{6,4},{7,5},{8,10},{9,11},{10,... | collective-permute-start | bytes 405512 | tf_op jit(solution)/shard_map/ppermute | solution.py:29
  130.3 6.3 %copy-start.1 = (f32[8,4224]{1,0:T(8,128)}, f32[8,4224]{1,0:T(8,128)S(1)}, u32[]{:S(2)}) copy-start(f32[8,4224]{1,0:T(8,128)S(1)} %collective-permute-done.27.refs_5_) | copy-start | bytes 405508
  136.6 0.7 copy-start.2
  136.6 0.7 copy-start.3

commit v2 on v1

--- a/solution.py
+++ b/solution.py
@@ -14,6 +14,7 @@
 KB = 512
 LANES = 128
 GROUP = 16
+PROJECT_STEPS = 4
 
 rope_theta = 10000.0
 norm_eps = 1e-06
@@ -53,95 +54,118 @@
     return jnp.where(even, up, down)
 
 
-def kv_body(tok, wk, wv, fine, coarse, k_out, v_out, w_both):
+def kv_body(tok, wk, wv, fine, coarse, out, acc):
     step = pl.program_id(0)
-    half = wk.shape[1]
-    rows = tok.shape[0]
-    subs = rows // LANES
+    half = wk.shape[0]
+    subs = out.shape[0] // LANES
+    weight = jnp.concatenate([wk[...], wv[...]], 0)
+    part = lax.dot_general(
+        tok[...], weight, (((1,), (1,)), ((), ())), preferred_element_type=f32
+    )
 
     @pl.when(step == 0)
     def _():
-        w_both[:, :half] = wk[...]
-        w_both[:, half:] = wv[...]
-
-    both = jnp.dot(tok[...], w_both[...], preferred_element_type=f32)
-    lane = lax.broadcasted_iota(i32, (LANES, LANES), 1)
-    even = lane % 2 == 0
-    upper = lax.axis_index("tp") % 2 == 1
-    first = lax.axis_index("seq") * (pl.num_programs(0) * subs) + step * subs
-    for sub in range(subs):
-        cos, sin = turn(fine, coarse, first + sub)
-        cos = jnp.where(upper, pltpu.roll(cos, half, 1), cos)
-        sin = jnp.where(upper, pltpu.roll(sin, half, 1), sin)
-        cos = jnp.where(lane < half, cos, 1.0)
-        sin = jnp.where(lane < half, jnp.where(even, -sin, sin), 0.0)
-        x = both[sub * LANES : (sub + 1) * LANES]
-        x = x * cos + pair_swap(x, even) * sin
-        x = x.T
-        k_out[:, sub * LANES : (sub + 1) * LANES] = x[:half].astype(bf16)
-        v_out[:, sub * LANES : (sub + 1) * LANES] = x[half:].astype(bf16)
+        acc[...] = part
+
+    @pl.when(step > 0)
+    def _():
+        acc[...] = acc[...] + part
+
+    @pl.when(step == pl.num_programs(0) - 1)
+    def _():
+        lane = lax.broadcasted_iota(i32, (LANES, LANES), 1)
+        even = lane % 2 == 0
+        upper = lax.axis_index("tp") % 2 == 1
+        first = lax.axis_index("seq") * subs
+        for sub in range(subs):
+            at = slice(sub * LANES, (sub + 1) * LANES)
+            cos, sin = turn(fine, coarse, first + sub)
+            cos = jnp.where(upper, pltpu.roll(cos, half, 1), cos)
+            sin = jnp.where(upper, pltpu.roll(sin, half, 1), sin)
+            cos = jnp.where(lane < half, cos, 1.0)
+            sin = jnp.where(lane < half, jnp.where(even, -sin, sin), 0.0)
+            x = acc[at]
+            out[at, :] = (x * cos + pair_swap(x, even) * sin).astype(bf16)
 
 
 def project_kv(tokens, w_key, w_value, fine, coarse):
     rows, width = tokens.shape
     half = w_key.shape[1]
-    block = 256
+    block = width // PROJECT_STEPS
     whole = lambda a: pl.BlockSpec(a.shape, lambda i: (0,) * a.ndim)
-    out = jax.ShapeDtypeStruct((half, rows), bf16)
     return pl.pallas_call(
         kv_body,
-        grid=(rows // block,),
+        grid=(PROJECT_STEPS,),
         in_specs=[
-            pl.BlockSpec((block, width), lambda i: (i, 0)),
-            whole(w_key),
-            whole(w_value),
+            pl.BlockSpec((rows, block), lambda i: (0, i)),
+            pl.BlockSpec((half, block), lambda i: (0, i)),
+            pl.BlockSpec((half, block), lambda i: (0, i)),
             whole(fine),
             whole(coarse),
         ],
-        out_specs=[pl.BlockSpec((half, block), lambda i: (0, i))] * 2,
-        out_shape=[out, out],
-        scratch_shapes=[pltpu.VMEM((width, 2 * half), bf16)],
+        out_specs=pl.BlockSpec((rows, 2 * half), lambda i: (0, 0)),
+        out_shape=jax.ShapeDtypeStruct((rows, 2 * half), bf16),
+        scratch_shapes=[pltpu.VMEM((rows, 2 * half), f32)],
         compiler_params=pltpu.CompilerParams(vmem_limit_bytes=VMEM_LIMIT),
         name="project_kv",
-    )(tokens, w_key, w_value, fine, coarse)
-
-
-def q_body(tok, wq, fine, coarse, q_out):
+    )(tokens, w_key.T, w_value.T, fine, coarse)
+
+
+def q_body(tok, wq, fine, coarse, *refs):
+    outs = refs[:-1]
+    acc = refs[-1]
     step = pl.program_id(0)
-    rows = tok.shape[0]
-    subs = rows // LANES
+    subs = acc.shape[0] // LANES
+    per_out = subs // len(outs)
     heads = wq.shape[1] // HD
-    x_all = jnp.dot(tok[...], wq[...], preferred_element_type=f32)
-    lane = lax.broadcasted_iota(i32, (LANES, LANES), 1)
-    even = lane % 2 == 0
-    first = lax.axis_index("seq") * (pl.num_programs(0) * subs) + step * subs
-    scale = HD ** (-0.5) * math.log2(math.e)
-    for sub in range(subs):
-        cos, sin = turn(fine, coarse, first + sub)
-        cos = cos * scale
-        sin = jnp.where(even, -sin, sin) * scale
-        for h in range(heads):
-            x = x_all[sub * LANES : (sub + 1) * LANES, h * HD : (h + 1) * HD]
-            x = x * cos + pair_swap(x, even) * sin
-            q_out[sub * LANES : (sub + 1) * LANES, h * HD : (h + 1) * HD] = x.astype(bf16)
+    part = jnp.dot(tok[...], wq[...], preferred_element_type=f32)
+
+    @pl.when(step == 0)
+    def _():
+        acc[...] = part
+
+    @pl.when(step > 0)
+    def _():
+        acc[...] = acc[...] + part
+
+    @pl.when(step == pl.num_programs(0) - 1)
+    def _():
+        lane = lax.broadcasted_iota(i32, (LANES, LANES), 1)
+        even = lane % 2 == 0
+        upper = lax.axis_index("tp") % 2 == 1
+        first = lax.axis_index("seq") * subs
+        scale = HD ** (-0.5) * math.log2(math.e)
+        for sub in range(subs):
+            cos, sin = turn(fine, coarse, first + sub)
+            cos = cos * scale
+            sin = jnp.where(even, -sin, sin) * scale
+            out = outs[sub // per_out]
+            row = (sub % per_out) * LANES
+            for h in range(heads):
+                x = acc[sub * LANES : (sub + 1) * LANES, h * HD : (h + 1) * HD]
+                x = x * cos + pair_swap(x, even) * sin
+                x = jnp.where(upper, pltpu.roll(x, HD // 2, 1), x)
+                out[row : row + LANES, h * HD : (h + 1) * HD] = x.astype(bf16)
 
 
 def project_q(tokens, w_query, fine, coarse):
     rows, width = tokens.shape
     cols = w_query.shape[1]
-    block = 256
+    block = width // PROJECT_STEPS
     whole = lambda a: pl.BlockSpec(a.shape, lambda i: (0,) * a.ndim)
+    out = jax.ShapeDtypeStruct((rows // 2, cols), bf16)
     return pl.pallas_call(
         q_body,
-        grid=(rows // block,),
+        grid=(PROJECT_STEPS,),
         in_specs=[
-            pl.BlockSpec((block, width), lambda i: (i, 0)),
-            whole(w_query),
+            pl.BlockSpec((rows, block), lambda i: (0, i)),
+            pl.BlockSpec((block, cols), lambda i: (i, 0)),
             whole(fine),
             whole(coarse),
         ],
-        out_specs=pl.BlockSpec((block, cols), lambda i: (i, 0)),
-        out_shape=jax.ShapeDtypeStruct((rows, cols), bf16),
+        out_specs=[pl.BlockSpec((rows // 2, cols), lambda i: (0, 0))] * 2,
+        out_shape=[out, out],
+        scratch_shapes=[pltpu.VMEM((rows, cols), f32)],
         compiler_params=pltpu.CompilerParams(vmem_limit_bytes=VMEM_LIMIT),
         name="project_q",
     )(tokens, w_query, fine, coarse)
@@ -165,13 +189,10 @@
     c = cent[...].astype(f32)
     wide[...] = c
     square = c * c
-    high = square.astype(bf16)
-    low = (square - high.astype(f32)).astype(bf16)
-    ones = jnp.ones((8, c.shape[1]), bf16)
-    contract = (((1,), (1,)), ((), ()))
-    total = lax.dot_general(ones, high, contract, preferred_element_type=f32)
-    total = total + lax.dot_general(ones, low, contract, preferred_element_type=f32)
-    norms[pl.ds(step, 1), :] = total[:1]
+    part = square[:, :LANES]
+    for g in range(1, c.shape[1] // LANES):
+        part = part + square[:, g * LANES : (g + 1) * LANES]
+    norms[pl.ds(step, 1), :] = jnp.sum(part.T, axis=0, keepdims=True)
 
     @pl.when(step == pl.num_programs(0) - 1)
     def _():
@@ -210,45 +231,75 @@
     )(base, centroids, centroids)
 
 
-def attend_body(pieces, seg_total, seg, q_ref, seg_row, *refs):
-    keys_in = refs[: 2 * pieces]
-    values_in = refs[2 * pieces : 4 * pieces]
-    out, counts, kt, vt, sc, col, lhs, sems = refs[4 * pieces :]
-    rows = q_ref.shape[0]
-    heads = q_ref.shape[1] // HD
+def segment_starts(ids):
+    rows = ids.shape[0]
+    row = lax.broadcasted_iota(i32, ids.shape, 0)
+    lane = lax.broadcasted_iota(i32, ids.shape, 1)
+    left = pltpu.roll(ids, 1, 1)
+    left = jnp.where(lane == 0, pltpu.roll(left, 1, 0), left)
+    token = row * LANES + lane
+    first = jnp.where((ids != left) & (token > 0), token, 0)
+    shift = 1
+    while shift < LANES:
+        first = jnp.maximum(first, jnp.where(lane >= shift, pltpu.roll(first, shift, 1), 0))
+        shift = shift * 2
+    above = jnp.broadcast_to(jnp.max(first, axis=1, keepdims=True), ids.shape)
+    above = jnp.where(row >= 1, pltpu.roll(above, 1, 0), 0)
+    shift = 1
+    while shift < rows:
+        above = jnp.maximum(above, jnp.where(row >= shift, pltpu.roll(above, shift, 0), 0))
+        shift = shift * 2
+    return jnp.maximum(first, above)
+
+
+def attend_body(pieces, seg_total, balanced, seg, ids, *refs):
+    queries = refs[: 3 if balanced else 2]
+    refs = refs[len(queries) :]
+    own_in = refs[:pieces]
+    other_in = refs[pieces : 2 * pieces]
+    out, counts, q_all, own, other, kn, vn, starts, weights, tops, col, lhs, sems = refs[
+        2 * pieces :
+    ]
+    q_rows, q_cols = queries[0].shape
+    rows = own_in[0].shape[0]
+    heads = q_cols // HD
     half = HD // 2
-    seq_len = kt.shape[1]
+    seq_len = own.shape[0]
+    wide = heads * QB
+    own_blocks = rows // QB
     rank = lax.axis_index("seq")
-    parity = lax.axis_index("tp") % 2
-
-    def copies(sources, target, first):
-        result = []
-        for k in range(2):
-            for m in range(pieces):
-                row0 = pl.multiple_of((parity ^ k) * half, half)
-                col0 = pl.multiple_of((rank ^ m) * rows, rows)
-                index = k * pieces + m
-                result.append(
-                    pltpu.make_async_copy(
-                        sources[index],
-                        target.at[pl.ds(row0, half), pl.ds(col0, rows)],
-                        sems.at[first + index],
-                    )
-                )
-        return result
-
-    key_copies = copies(keys_in, kt, 0)
-    value_copies = copies(values_in, vt, 2 * pieces)
-    for c in key_copies:
-        c.start()
-    for c in value_copies:
+    upper = lax.axis_index("tp") % 2 == 1
+
+    copies = []
+    for k, source in enumerate(queries):
+        target = q_all.at[pl.ds(k * q_rows, q_rows), :]
+        copies.append(pltpu.make_async_copy(source, target, sems.at[len(copies)]))
+    for sources, target in ((own_in, own), (other_in, other)):
+        for m in range(pieces):
+            row0 = pl.multiple_of((rank ^ m) * rows, rows)
+            place = target.at[pl.ds(row0, rows), :]
+            copies.append(pltpu.make_async_copy(sources[m], place, sems.at[len(copies)]))
+    for c in copies:
         c.start()
     col[...] = jnp.zeros(col.shape, f32)
-    for c in key_copies:
+    starts[...] = segment_starts(ids[...])
+    for c in copies:
         c.wait()
 
-    def q_step(b, carry):
-        base = rank * rows + b * QB
+    def join(t, carry):
+        at = pl.ds(pl.multiple_of(t * KB, KB), KB)
+        a = own[at, :]
+        b = other[at, :]
+        kn[at, :] = jnp.concatenate([a[:, :half], b[:, :half]], 1)
+        vn[at, :] = jnp.concatenate([a[:, half:], b[:, half:]], 1)
+        return carry
+
+    lax.fori_loop(0, seq_len // KB, join, 0)
+
+    def q_step(n, carry):
+        home = n < own_blocks
+        base = jnp.where(home, rank, rank ^ 3) * rows + jnp.where(home, n, n - own_blocks) * QB
+        base = pl.multiple_of(base, QB)
         last_seg = seg[base + QB - 1]
         first_seg = seg[base]
         end = (base + QB - 1) // KB + 1
@@ -262,117 +313,126 @@
         begin = jnp.maximum(begin, jnp.maximum(base - (WINDOW - 1), 0) // KB)
         begin = jnp.minimum(begin, clear_end)
         clear = jnp.clip(clear, begin, clear_end)
-        own = jnp.broadcast_to(seg_row[:, pl.ds(base, QB)].astype(f32), (LANES, QB)).T
-        i_pos = base + lax.broadcasted_iota(i32, (QB, LANES), 0)
-
-        for h in range(heads):
-            q = q_ref[pl.ds(b * QB, QB), h * HD : (h + 1) * HD]
-
-            def score(masked, kb, top):
-                start = pl.multiple_of(kb * KB, KB)
-                s = jnp.dot(q, kt[:, pl.ds(start, KB)], preferred_element_type=f32)
-                for g in range(KB // LANES):
-                    part = s[:, g * LANES : (g + 1) * LANES]
-                    at = pl.multiple_of(start + g * LANES, LANES)
-                    if masked:
-                        j_pos = at + lax.broadcasted_iota(i32, (QB, LANES), 1)
-                        ids = seg_row[:, pl.ds(at, LANES)].astype(f32)
-                        allowed = (j_pos <= i_pos) & (own == ids)
-                        if seq_len > WINDOW:
-                            allowed = allowed & (i_pos - j_pos < WINDOW)
-                        part = jnp.where(allowed, part, -1e30)
-                    sc[:, pl.ds(at, LANES)] = part
-                    top = jnp.maximum(top, part)
-                return top
-
-            top = jnp.full((QB, LANES), -1e30, f32)
-            top = lax.fori_loop(begin, clear, lambda kb, t: score(True, kb, t), top)
-            top = lax.fori_loop(clear, clear_end, lambda kb, t: score(False, kb, t), top)
-            top = lax.fori_loop(clear_end, end, lambda kb, t: score(True, kb, t), top)
-            top = jnp.max(top, axis=1, keepdims=True)
-
-            def weigh(kb, total):
-                start = pl.multiple_of(kb * KB, KB)
-                for g in range(KB // LANES):
-                    at = pl.multiple_of(start + g * LANES, LANES)
-                    p = jnp.exp2(sc[:, pl.ds(at, LANES)] - top)
-                    sc[:, pl.ds(at, LANES)] = p
-                    total = total + p
-                return total
-
-            total = lax.fori_loop(begin, end, weigh, jnp.zeros((QB, LANES), f32))
-            share = 1.0 / jnp.sum(total, axis=1, keepdims=True)
-            share = jnp.broadcast_to(share, (QB, LANES))
-
-            def gather(kb, carry):
-                start = pl.multiple_of(kb * KB, KB)
-                for g in range(KB // LANES):
-                    at = pl.multiple_of(start + g * LANES, LANES)
-                    p = sc[:, pl.ds(at, LANES)] * share
-                    p = jnp.sum(p.reshape(QB // 8, 8, LANES), axis=0)
-                    col[h, :, pl.ds(at, LANES)] = col[h, :, pl.ds(at, LANES)] + p
-                return carry
-
-            lax.fori_loop(begin, end, gather, 0)
+
+        q_at = pl.ds(pl.multiple_of(n * QB, QB), QB)
+        q = jnp.concatenate([q_all[q_at, h * HD : (h + 1) * HD] for h in range(heads)], 0)
+        low = [starts[pl.ds(base // LANES + g, 1), :] for g in range(QB // LANES)]
+        low = jnp.concatenate(low * heads, 1)
+        i_pos = base + lax.broadcasted_iota(i32, (1, wide), 1) % QB
+        if seq_len > WINDOW:
+            low = jnp.maximum(low, i_pos - (WINDOW - 1))
+
+        def score(masked, kb, carry):
+            top, total = carry
+            start = pl.multiple_of(kb * KB, KB)
+            s = lax.dot_general(
+                kn[pl.ds(start, KB), :],
+                q,
+                (((1,), (1,)), ((), ())),
+                preferred_element_type=f32,
+            )
+            if masked:
+                j_pos = start + lax.broadcasted_iota(i32, (KB, wide), 0)
+                s = jnp.where((j_pos <= i_pos) & (j_pos >= low), s, -1e30)
+            new_top = jnp.maximum(top, jnp.max(s, axis=0, keepdims=True))
+            p = jnp.exp2(s - new_top)
+            weights[pl.ds(start, KB), :] = p.astype(bf16)
+            tops[pl.ds(kb, 1), :] = new_top
+            p = jnp.sum(p.reshape(KB // 8, 8, wide), axis=0)
+            return new_top, total * jnp.exp2(top - new_top) + p
+
+        state = (jnp.full((1, wide), -1e30, f32), jnp.zeros((8, wide), f32))
+        state = lax.fori_loop(begin, clear, lambda kb, c: score(True, kb, c), state)
+        state = lax.fori_loop(clear, clear_end, lambda kb, c: score(False, kb, c), state)
+        top, total = lax.fori_loop(clear_end, end, lambda kb, c: score(True, kb, c), state)
+        share = 1.0 / jnp.sum(total, axis=0, keepdims=True)
+        row = lax.broadcasted_iota(i32, (16, wide), 0)
+        head = lax.broadcasted_iota(i32, (16, wide), 1) // QB
+
+        def gather(kb, carry):
+            start = pl.multiple_of(kb * KB, KB)
+            r = share * jnp.exp2(tops[pl.ds(kb, 1), :] - top)
+            high = r.astype(bf16).astype(f32)
+            r = jnp.where(row == head, high, jnp.where(row == heads + head, r - high, 0.0))
+            add = lax.dot_general(
+                weights[pl.ds(start, KB), :],
+                r.astype(bf16),
+                (((1,), (1,)), ((), ())),
+                preferred_element_type=f32,
+            )
+            at = pl.ds(start, KB)
+            col[at, :16] = col[at, :16] + add
+            return carry
+
+        lax.fori_loop(begin, end, gather, 0)
         return carry
 
-    lax.fori_loop(0, rows // QB, q_step, 0)
+    if balanced:
+        low_n = jnp.where(rank == 3, 2, jnp.where(rank == 2, 1, 0))
+        high_n = own_blocks + jnp.where(rank == 0, 2, jnp.where(rank == 1, 1, 0))
+    else:
+        low_n = 0
+        high_n = own_blocks
+    lax.fori_loop(low_n, high_n, q_step, 0)
 
     number = jnp.zeros((seg_total, LANES), f32)
     for g in range(seq_len // LANES):
         at = slice(g * LANES, (g + 1) * LANES)
-        ids = seg_row[:, at]
-        member = ids == lax.broadcasted_iota(i32, (seg_total, LANES), 0)
+        member = ids[g : g + 1, :] == lax.broadcasted_iota(i32, (seg_total, LANES), 0)
         number = number + member.astype(f32)
+        turned = col[at, :].T
         for h in range(heads):
-            w = jnp.sum(col[h, :, at], axis=0, keepdims=True)
+            w = turned[h : h + 1] + turned[heads + h : heads + h + 1]
             w = jnp.where(member, w, 0.0)
             high = w.astype(bf16)
             lhs[h * seg_total : (h + 1) * seg_total, at] = high
-            low = (w - high.astype(f32)).astype(bf16)
-            lhs[(heads + h) * seg_total : (heads + h + 1) * seg_total, at] = low
+            rest = (w - high.astype(f32)).astype(bf16)
+            lhs[(heads + h) * seg_total : (heads + h + 1) * seg_total, at] = rest
     counts[...] = jnp.broadcast_to(jnp.sum(number, axis=1, keepdims=True), counts.shape)
-    for c in value_copies:
-        c.wait()
-    pooled = lax.dot_general(
-        lhs[...], vt[...], (((1,), (1,)), ((), ())), preferred_element_type=f32
-    )
+    pooled = jnp.dot(lhs[...], vn[...], preferred_element_type=f32)
     for h in range(heads):
-        high = pooled[h * seg_total : (h + 1) * seg_total]
-        low = pooled[(heads + h) * seg_total : (heads + h + 1) * seg_total]
-        out[:, h * HD : (h + 1) * HD] = high + low
-
-
-def attend(seg_ids, queries, keys, values, seg_total):
-    rows, cols = queries.shape
+        x = pooled[h * seg_total : (h + 1) * seg_total]
+        x = x + pooled[(heads + h) * seg_total : (heads + h + 1) * seg_total]
+        out[:, h * HD : (h + 1) * HD] = jnp.where(upper, pltpu.roll(x, half, 1), x)
+
+
+def attend(seg_ids, queries, own, other, seg_total, balanced):
+    q_rows, cols = queries[0].shape
+    rows = own[0].shape[0]
     seq_len = seg_ids.shape[0]
-    pieces = len(keys) // 2
+    pieces = len(own)
     heads = cols // HD
     whole = pl.BlockSpec(memory_space=pltpu.VMEM)
     anywhere = pl.BlockSpec(memory_space=pl.ANY)
+    inputs = len(queries) + 2 * pieces
 
     def body(*refs):
-        attend_body(pieces, seg_total, *refs)
+        attend_body(pieces, seg_total, balanced, *refs)
 
     return pl.pallas_call(
         body,
-        in_specs=[pl.BlockSpec(memory_space=pltpu.SMEM), whole, whole] + [anywhere] * (4 * pieces),
+        in_specs=[pl.BlockSpec(memory_space=pltpu.SMEM), whole] + [anywhere] * inputs,
         out_specs=[whole, whole],
         out_shape=[
             jax.ShapeDtypeStruct((seg_total, cols), f32),
             jax.ShapeDtypeStruct((seg_total, LANES), f32),
         ],
         scratch_shapes=[
-            pltpu.VMEM((HD, seq_len), bf16),
-            pltpu.VMEM((HD, seq_len), bf16),
-            pltpu.VMEM((QB, seq_len), f32),
-            pltpu.VMEM((heads, 8, seq_len), f32),
+            pltpu.VMEM((len(queries) * q_rows, cols), bf16),
+            pltpu.VMEM((seq_len, HD), bf16),
+            pltpu.VMEM((seq_len, HD), bf16),
+            pltpu.VMEM((seq_len, HD), bf16),
+            pltpu.VMEM((seq_len, HD), bf16),
+            pltpu.VMEM((seq_len // LANES, LANES), i32),
+            pltpu.VMEM((seq_len, heads * QB), bf16),
+            pltpu.VMEM((max(8, seq_len // KB), heads * QB), f32),
+            pltpu.VMEM((seq_len, LANES), f32),
             pltpu.VMEM((2 * heads * seg_total, seq_len), bf16),
-            pltpu.SemaphoreType.DMA((4 * pieces,)),
+            pltpu.SemaphoreType.DMA((inputs,)),
         ],
         compiler_params=pltpu.CompilerParams(vmem_limit_bytes=VMEM_LIMIT),
         name="attend",
-    )(seg_ids, queries, seg_ids.reshape(1, seq_len), *keys, *values)
+    )(seg_ids, seg_ids.reshape(seq_len // LANES, LANES), *queries, *own, *other)
 
 
 def mix_body(pieces, *refs):
@@ -471,8 +531,8 @@
         ).astype(bf16)
 
     y = lax.dot_general(
-        lhs[...], cent[...], (((1,), (1,)), ((), ())), preferred_element_type=f32
-    )
+        cent[...], lhs[...], (((1,), (1,)), ((), ())), preferred_element_type=f32
+    ).T
     y = y[: 2 * per_side] + y[2 * per_side :]
     cols = pl.ds(pl.multiple_of(step * block, block), block)
     for k, target in enumerate((keep, send)):
@@ -627,14 +687,15 @@
     fine = jnp.asarray(fine_np)
     coarse = jnp.asarray(coarse_np)
 
-    key_half, value_half = project_kv(tokens, w_key, w_value, fine, coarse)
+    own = project_kv(tokens, w_key, w_value, fine, coarse)
     masks = range(1, seq_total)
-    keys = [key_half] + [swapped(key_half, "seq", m) for m in masks]
-    keys = keys + [swapped(k, "tp", 1) for k in keys]
-    values = [value_half] + [swapped(value_half, "seq", m) for m in masks]
-    values = values + [swapped(v, "tp", 1) for v in values]
-
-    queries = project_q(tokens, w_query, fine, coarse)
+    own = [own] + [swapped(own, "seq", m) for m in masks]
+    other = [swapped(x, "tp", 1) for x in own]
+
+    queries = list(project_q(tokens, w_query, fine, coarse))
+    balanced = seq_total == 4 and seq_len <= WINDOW and tok_rows == 4 * QB
+    if balanced:
+        queries = queries + [lax.ppermute(queries[0], "seq", [(3, 0), (2, 1)])]
 
     local = assign - rank_seq * cent_rows
     mine = (local >= 0) & (local < cent_rows)
@@ -655,7 +716,11 @@
     )
     pooled_tokens = [pooled_tokens] + [swapped(pooled_tokens, "seq", m) for m in masks]
 
-    attended, counts = attend(seg_ids, queries, keys, values, seg_total)
+    queries, wide, norms, picked, pooled_first = lax.optimization_barrier(
+        (queries, wide, norms, picked, pooled_tokens[0])
+    )
+    pooled_tokens[0] = pooled_first
+    attended, counts = attend(seg_ids, queries, own, other, seg_total, balanced)
     attended = [attended] + [swapped(attended, "seq", m) for m in masks]
 
     keep, send = mix(attended, norms, w_out, feat, groups)

time: 142 us -> 117 us (0.82)
  starting transfers between devices: 49.4 us -> 21.9 us
  Pallas kernels: 52.2 us -> 62.5 us
  local copies, waits for them, and re-layouts: 10.1 us -> 4.86 us
  waiting for transfers between devices: 23.1 us -> 20.5 us
    ppermute x28 -> x21, starting transfers between devices: 49.4 us -> 20.7 us  [swapped(): return lax.ppermute(x, axis, [(i, i ^ mask) for i in range(count)])]
    pallas_call x1, Pallas kernels: 12.2 us -> 22.1 us  [attend(): pl.pallas_call(body, in_specs=[pl.BlockSpec(memory_space=pltpu.SMEM), who...]
    unnamed x60 -> x46, local copies, waits for them, and re-layouts: 7.46 us -> 2.94 us
    ppermute x28 -> x21, waiting for transfers between devices: 23.1 us -> 20.5 us  [swapped(): return lax.ppermute(x, axis, [(i, i ^ mask) for i in range(count)])]
  transfers between devices with their start and end apart: 28 -> 22, of which waited for: 11 -> 11; matrix products, arithmetic and copies ran while one was open for 4% -> 5% of each run, Pallas kernels for 13% -> 16%
where the time goes in v2:
time: 117 us; the launch traced here: 116 us
  Pallas kernels  62.5 us (53%)
  starting transfers between devices  21.9 us (19%)
  waiting for transfers between devices  20.5 us (18%)
  local copies, waits for them, and re-layouts  4.86 us (4%)
  other arithmetic  3.49 us (3%)
  matrix products  1.69 us (1%)
    pallas_call x1, Pallas kernels, attend(): pl.pallas_call(body, in_specs=[pl.BlockSpec(memory_space=pltpu.SMEM), who...  22.1 us
    ppermute x21, starting transfers between devices, swapped(): return lax.ppermute(x, axis, [(i, i ^ mask) for i in range(count)])  20.7 us
    ppermute x21, waiting for transfers between devices, swapped(): return lax.ppermute(x, axis, [(i, i ^ mask) for i in range(count)])  20.5 us
    pallas_call x1, Pallas kernels, widen_centroids(): pl.pallas_call(cent_body, grid_spec=spec, out_shape=[jax.ShapeDtypeStruct...  9.86 us
    pallas_call x1, Pallas kernels, project_q(): pl.pallas_call(q_body, grid=(PROJECT_STEPS,), in_specs=[pl.BlockSpec((row...  8.49 us
    pallas_call x1, Pallas kernels, cross(): pl.pallas_call(body, grid_spec=spec, out_shape=[jax.ShapeDtypeStruct(side...  8.29 us
    pallas_call x1, Pallas kernels, project_kv(): pl.pallas_call(kv_body, grid=(PROJECT_STEPS,), in_specs=[pl.BlockSpec((ro...  7.19 us
    pallas_call x1, Pallas kernels, finish(): pl.pallas_call(body, in_specs=[scalar, scalar] + [whole] * (groups + 4) +...  3.62 us
  transfers between devices with their start and end apart: 22, of which 11 were waited for; matrix products, arithmetic and copies ran while one was open for 5% of the time, Pallas kernels for 16%

profile of v2, /device:TPU:0, one launch (start us, length us, event | category | flops | bytes accessed | tf_op | source)
XLA Modules:
  0.0 115.8 jit_solution(17211667848873776202)
XLA Ops:
  0.6 7.2 %project_kv.1.refs_5_ = bf16[1024,128]{1,0:T(8,128)(2,1)} custom-call(bf16[1024,4096]{1,0:T(8,128)(2,1)} %tok.3, bf16[64,4096]{1,0:T(8,128)(2,1)} %bitcast.25, bf16[64,4096]{1,0:T(8,128)(2,1)} %bitcast.26, f32[2,128,128]{2,1,0:T(8,128)} %constant.48.clone.fine, f32[2,32,128]{2,1,0:T(8,128)} %constant.49.clone.coarse), custom_call_target="tpu_custom_call" | custom-call | tf_op jit(solution)/shard_map/project_kv/pallas_call | solution.py:96
  7.8 3.9 %collective-permute-start.3 = (bf16[1024,128]{1,0:T(8,128)(2,1)}, bf16[1024,128]{1,0:T(8,128)(2,1)S(1)}, u32[]{:S(2)}, u32[]{:S(2)}) collective-permute-start(bf16[1024,128]{1,0:T(8,128)(2,1)} %project_kv.1.refs_5_), channel_id=1, source_target_pairs={{0,24},{8,16},{16,8},{24,0},{1,25},{9,17},{17,9},{25,1},{2,26},{10... | collective-permute-start | bytes 786440 | tf_op jit(solution)/shard_map/ppermute | solution.py:30
  11.7 0.5 collective-permute-start.2
  12.2 0.1 collective-permute-start.1
  12.3 0.0 collective-permute-start.4
  12.3 8.5 %project_q.1 = (bf16[512,256]{1,0:T(8,128)(2,1)}, bf16[512,256]{1,0:T(8,128)(2,1)}) custom-call(bf16[1024,4096]{1,0:T(8,128)(2,1)} %tok.3, bf16[4096,256]{1,0:T(8,128)(2,1)} %wq.1, f32[2,128,128]{2,1,0:T(8,128)} %constant.48.clone.fine, f32[2,32,128]{2,1,0:T(8,128)} %constant.49.clone.coarse), custom_call_target="tpu_custom_call" | custom-call | tf_op jit(solution)/shard_map/project_q/pallas_call | solution.py:157
  20.8 1.3 %collective-permute-start = (bf16[512,256]{1,0:T(8,128)(2,1)}, bf16[512,256]{1,0:T(8,128)(2,1)S(1)}, u32[]{:S(2)}, u32[]{:S(2)}) collective-permute-start(bf16[512,256]{1,0:T(8,128)(2,1)} %get-tuple-element.27.refs_2_), channel_id=1, source_target_pairs={{24,0},{16,8},{25,1},{17,9},{26,2},{18,10},{27,3},{19,11},{28,4},{... | collective-permute-start | bytes 786440 | tf_op jit(solution)/shard_map/ppermute | solution.py:698
  22.1 0.0 collective-permute-done.3.refs_8_
  22.1 0.6 collective-permute-start.7
  22.7 1.2 %collective-permute-done.2.refs_7_ = bf16[1024,128]{1,0:T(8,128)(2,1)S(1)} collective-permute-done((bf16[1024,128]{1,0:T(8,128)(2,1)}, bf16[1024,128]{1,0:T(8,128)(2,1)S(1)}, u32[]{:S(2)}, u32[]{:S(2)}) %collective-permute-start.2) | collective-permute-done | bytes 262176 | tf_op jit(solution)/shard_map/ppermute | solution.py:30
  23.8 0.0 collective-permute-start.6
  23.9 0.3 collective-permute-done.1.refs_6_
  24.1 0.2 collective-permute-start.5
  24.4 0.6 multiply_bitcast_fusion
  25.0 9.9 %widen_centroids.1 = (f32[4096,512]{1,0:T(8,128)}, f32[8,512]{1,0:T(8,128)}, bf16[512,512]{1,0:T(8,128)(2,1)}) custom-call(s32[32]{0:T(128)} %get-tuple-element.52.base, bf16[4096,512]{1,0:T(8,128)(2,1)} %refs_11_.1, bf16[4096,512]{1,0:T(8,128)(2,1)} %refs_11_.1), custom_call_target="tpu_custom_call" | custom-call | tf_op jit(solution)/shard_map/widen_centroids/pallas_call | solution.py:221
  34.9 1.7 %fusion.refs_5_ = f32[32,512]{1,0:T(8,128)S(1)} fusion(bf16[1024,4096]{1,0:T(8,128)(2,1)} %tok.3, s32[]{:T(128)S(6)} %select_n.22, s32[1024]{0:T(1024)S(1)} %dynamic-slice-done), kind=kOutput, calls=%fused_computation | convolution fusion | flops 33587200 | bytes 1118212 | tf_op jit(solution)/shard_map/dot_general | solution.py:714
  36.5 0.0 copy-start
  36.5 0.0 collective-permute-done.refs_4_
  36.6 0.0 collective-permute-done.4.refs_9_
  36.6 0.0 collective-permute-done.6.refs_11_
  36.6 0.0 collective-permute-done.5.refs_10_
  36.7 0.6 copy-done.5
  37.3 0.1 copy-done.4
  37.4 0.1 copy-done.6
  37.5 0.1 copy-done.7
  37.5 0.1 copy-done.8
  37.7 22.1 %attend.1 = (f32[32,256]{1,0:T(8,128)}, f32[32,128]{1,0:T(8,128)}) custom-call(s32[4096]{0:T(1024)} %refs_0_.3, s32[32,128]{1,0:T(8,128)} %bitcast.27, bf16[512,256]{1,0:T(8,128)(2,1)} %get-tuple-element.27.refs_2_, bf16[512,256]{1,0:T(8,128)(2,1)} %get-tuple-element.28.refs_3_, bf16[512,256]{1,0:T(8,128)(2,1)} %copy-done.5, ...), custom_call_target="tpu_custom_call" | custom-call | tf_op jit(solution)/shard_map/attend/pallas_call | solution.py:412
  59.8 0.1 collective-permute-start.10
  59.8 2.3 %collective-permute-start.9 = (f32[32,256]{1,0:T(8,128)}, f32[32,256]{1,0:T(8,128)S(1)}, u32[]{:S(2)}, u32[]{:S(2)}) collective-permute-start(f32[32,256]{1,0:T(8,128)} %get-tuple-element.30.refs_0_), channel_id=1, source_target_pairs={{0,16},{8,24},{16,0},{24,8},{1,17},{9,25},{17,1},{25,9},{2,18},{10... | collective-permute-start | bytes 98312 | tf_op jit(solution)/shard_map/ppermute | solution.py:30
  62.1 1.2 %collective-permute-start.8 = (f32[32,256]{1,0:T(8,128)}, f32[32,256]{1,0:T(8,128)S(1)}, u32[]{:S(2)}, u32[]{:S(2)}) collective-permute-start(f32[32,256]{1,0:T(8,128)} %get-tuple-element.30.refs_0_), channel_id=1, source_target_pairs={{0,8},{8,0},{16,24},{24,16},{1,9},{9,1},{17,25},{25,17},{2,10},{10... | collective-permute-start | bytes 98312 | tf_op jit(solution)/shard_map/ppermute | solution.py:30
  63.3 1.6 %collective-permute-done.10.refs_3_ = f32[32,256]{1,0:T(8,128)S(1)} collective-permute-done((f32[32,256]{1,0:T(8,128)}, f32[32,256]{1,0:T(8,128)S(1)}, u32[]{:S(2)}, u32[]{:S(2)}) %collective-permute-start.10) | collective-permute-done | bytes 32800 | tf_op jit(solution)/shard_map/ppermute | solution.py:30
  64.9 1.3 %collective-permute-done.8.refs_1_ = f32[32,256]{1,0:T(8,128)S(1)} collective-permute-done((f32[32,256]{1,0:T(8,128)}, f32[32,256]{1,0:T(8,128)S(1)}, u32[]{:S(2)}, u32[]{:S(2)}) %collective-permute-start.8) | collective-permute-done | bytes 32800 | tf_op jit(solution)/shard_map/ppermute | solution.py:30
  66.2 0.6 copy-done.20
  66.8 2.9 %mix.1 = (f32[4,40,512]{2,1,0:T(8,128)}, f32[4,40,512]{2,1,0:T(8,128)}) custom-call(f32[32,256]{1,0:T(8,128)} %get-tuple-element.30.refs_0_, f32[32,256]{1,0:T(8,128)} %copy-done.20, f32[32,256]{1,0:T(8,128)} %copy-done.19, f32[32,256]{1,0:T(8,128)} %copy-done.18, f32[8,512]{1,0:T(8,128)} %get-tuple-element.31.refs_4_, bf16[256,4096]{1,0:T(8,128)(2,1)} %refs_5_.1), custom_call_target="tpu_custom_call" | custom-call | tf_op jit(solution)/shard_map/mix/pallas_call | solution.py:467
  69.7 1.2 %collective-permute-start.17 = (f32[32,512]{1,0:T(8,128)S(1)}, f32[32,512]{1,0:T(8,128)S(1)}, u32[]{:S(2)}, u32[]{:S(2)}) collective-permute-start(f32[32,512]{1,0:T(8,128)S(1)} %fusion.refs_5_), channel_id=1, source_target_pairs={{0,24},{8,16},{16,8},{24,0},{1,25},{9,17},{17,9},{25,1},{2,26},{10... | collective-permute-start | bytes 196616 | tf_op jit(solution)/shard_map/ppermute | solution.py:30
  71.0 0.6 collective-permute-done.11
  71.6 1.0 add.16
  72.6 0.7 slice_bitcast_fusion.4
  73.3 3.6 %collective-permute-start.14 = (f32[40,512]{1,0:T(8,128)S(1)}, f32[40,512]{1,0:T(8,128)S(1)}, u32[]{:S(2)}, u32[]{:S(2)}) collective-permute-start(f32[40,512]{1,0:T(8,128)S(1)} %get-tuple-element.48), channel_id=1, source_target_pairs={{0,6},{1,7},{2,4},{3,5},{4,2},{5,3},{6,0},{7,1},{8,14},{9,15},{10,... | collective-permute-start | bytes 245768 | tf_op jit(solution)/shard_map/ppermute | solution.py:30
  76.8 0.8 collective-permute-start.12
  77.7 0.8 collective-permute-start.16
  78.5 1.0 collective-permute-start.15
  79.5 2.4 %collective-permute-done.16.refs_7_ = f32[32,512]{1,0:T(8,128)S(1)} collective-permute-done((f32[32,512]{1,0:T(8,128)S(1)}, f32[32,512]{1,0:T(8,128)S(1)}, u32[]{:S(2)}, u32[]{:S(2)}) %collective-permute-start.16) | collective-permute-done | bytes 65568 | tf_op jit(solution)/shard_map/ppermute | solution.py:30
  81.9 0.9 collective-permute-done.15.refs_6_
  82.8 0.0 collective-permute-done.14.refs_4_
  82.8 1.2 %collective-permute-done.13.refs_3_ = f32[40,512]{1,0:T(8,128)S(1)} collective-permute-done((f32[40,512]{1,0:T(8,128)S(1)}, f32[40,512]{1,0:T(8,128)S(1)}, u32[]{:S(2)}, u32[]{:S(2)}) %collective-permute-start.13) | collective-permute-done | bytes 81952 | tf_op jit(solution)/shard_map/ppermute | solution.py:30
  84.1 0.6 copy-done.13
  84.6 0.0 copy-done.14
  84.7 8.3 %cross.1 = (f32[4,8,4224]{2,1,0:T(8,128)}, f32[4,8,4224]{2,1,0:T(8,128)}, f32[32,512]{1,0:T(8,128)}, f32[8,512]{1,0:T(8,128)}) custom-call(s32[8]{0:T(128)} %refs_0_.5, f32[40,512]{1,0:T(8,128)} %get-tuple-element.51.refs_1_, f32[40,512]{1,0:T(8,128)} %copy-done.14, f32[40,512]{1,0:T(8,128)} %copy-done.13, f32[40,512]{1,0:T(8,128)} %copy-done.12, ...), custom_call_target="tpu_custom_call" | custom-call | tf_op jit(solution)/shard_map/cross/pallas_call | solution.py:569
  93.0 0.0 collective-permute-start.18
  93.0 0.2 fusion.4
  93.1 2.0 %collective-permute-done.18 = f32[4,8,4224]{2,1,0:T(8,128)S(1)} collective-permute-done((f32[4,8,4224]{2,1,0:T(8,128)}, f32[4,8,4224]{2,1,0:T(8,128)S(1)}, u32[]{:S(2)}, u32[]{:S(2)}) %collective-permute-start.18) | collective-permute-done | bytes 540704 | tf_op jit(solution)/shard_map/ppermute | solution.py:30
  95.1 1.1 add.17
  96.2 0.7 slice_bitcast_fusion
  96.9 2.6 %collective-permute-start.21 = (f32[8,4224]{1,0:T(8,128)S(1)}, f32[8,4224]{1,0:T(8,128)S(1)}, u32[]{:S(2)}, u32[]{:S(2)}) collective-permute-start(f32[8,4224]{1,0:T(8,128)S(1)} %get-tuple-element.44), channel_id=1, source_target_pairs={{0,6},{1,7},{2,4},{3,5},{4,2},{5,3},{6,0},{7,1},{8,14},{9,15},{10,... | collective-permute-start | bytes 405512 | tf_op jit(solution)/shard_map/ppermute | solution.py:30
  99.5 0.0 collective-permute-start.20
  99.5 1.7 %collective-permute-start.19 = (f32[8,4224]{1,0:T(8,128)S(1)}, f32[8,4224]{1,0:T(8,128)S(1)}, u32[]{:S(2)}, u32[]{:S(2)}) collective-permute-start(f32[8,4224]{1,0:T(8,128)S(1)} %get-tuple-element.46), channel_id=1, source_target_pairs={{0,2},{1,3},{2,0},{3,1},{4,6},{5,7},{6,4},{7,5},{8,10},{9,11},{10,... | collective-permute-start | bytes 405512 | tf_op jit(solution)/shard_map/ppermute | solution.py:30
  101.3 0.6 reshape_tile.3.refs_8_
  101.9 0.6 pad_add_fusion.refs_1_
  102.4 2.8 %collective-permute-done.21.refs_5_ = f32[8,4224]{1,0:T(8,128)S(1)} collective-permute-done((f32[8,4224]{1,0:T(8,128)S(1)}, f32[8,4224]{1,0:T(8,128)S(1)}, u32[]{:S(2)}, u32[]{:S(2)}) %collective-permute-start.21) | collective-permute-done | bytes 135200 | tf_op jit(solution)/shard_map/ppermute | solution.py:30
  105.2 6.3 %collective-permute-done.20.refs_4_ = f32[8,4224]{1,0:T(8,128)S(1)} collective-permute-done((f32[8,4224]{1,0:T(8,128)S(1)}, f32[8,4224]{1,0:T(8,128)S(1)}, u32[]{:S(2)}, u32[]{:S(2)}) %collective-permute-start.20) | collective-permute-done | bytes 135200 | tf_op jit(solution)/shard_map/ppermute | solution.py:30
  111.5 0.6 copy-done.10
  112.2 0.1 copy-done.11
  112.2 3.6 %finish.1 = (f32[8,4096]{1,0:T(8,128)}, f32[4096,512]{1,0:T(8,128)}) custom-call(s32[8]{0:T(128)} %refs_0_.5, s32[3,32]{1,0:T(4,128)} %pad_add_fusion.refs_1_, f32[8,4224]{1,0:T(8,128)} %get-tuple-element.47.refs_2_, f32[8,4224]{1,0:T(8,128)} %copy-done.11, f32[8,4224]{1,0:T(8,128)} %copy-done.10, ...), custom_call_target="tpu_custom_call", output_to_operand_aliasing={{1}: (10, {})} | custom-call | tf_op jit(solution)/shard_map/finish/pallas_call | solution.py:654
  (46 shorter events, 0.1 us)
Async XLA Ops:
  0.6 23.7 %copy-start.22 = (s32[32]{0:T(128)S(1)}, s32[32]{0:T(128)}, u32[]{:S(2)}) copy-start(s32[32]{0:T(128)} %param.21) | copy-start | bytes 388
  7.8 14.3 %collective-permute-start.3 = (bf16[1024,128]{1,0:T(8,128)(2,1)}, bf16[1024,128]{1,0:T(8,128)(2,1)S(1)}, u32[]{:S(2)}, u32[]{:S(2)}) collective-permute-start(bf16[1024,128]{1,0:T(8,128)(2,1)} %project_kv.1.refs_5_), channel_id=1, source_target_pairs={{0,24},{8,16},{16,8},{24,0},{1,25},{9,17},{17,9},{25,1},{2,26},{10... | collective-permute-start | bytes 786440 | tf_op jit(solution)/shard_map/ppermute | solution.py:30
  11.7 12.1 %collective-permute-start.2 = (bf16[1024,128]{1,0:T(8,128)(2,1)}, bf16[1024,128]{1,0:T(8,128)(2,1)S(1)}, u32[]{:S(2)}, u32[]{:S(2)}) collective-permute-start(bf16[1024,128]{1,0:T(8,128)(2,1)} %project_kv.1.refs_5_), channel_id=1, source_target_pairs={{0,16},{8,24},{16,0},{24,8},{1,17},{9,25},{17,1},{25,9},{2,18},{10... | collective-permute-start | bytes 786440 | tf_op jit(solution)/shard_map/ppermute | solution.py:30
  12.2 11.9 %collective-permute-start.1 = (bf16[1024,128]{1,0:T(8,128)(2,1)}, bf16[1024,128]{1,0:T(8,128)(2,1)S(1)}, u32[]{:S(2)}, u32[]{:S(2)}) collective-permute-start(bf16[1024,128]{1,0:T(8,128)(2,1)} %project_kv.1.refs_5_), channel_id=1, source_target_pairs={{0,8},{8,0},{16,24},{24,16},{1,9},{9,1},{17,25},{25,17},{2,10},{10... | collective-permute-start | bytes 786440 | tf_op jit(solution)/shard_map/ppermute | solution.py:30
  12.3 24.3 %collective-permute-start.4 = (bf16[1024,128]{1,0:T(8,128)(2,1)}, bf16[1024,128]{1,0:T(8,128)(2,1)S(1)}, u32[]{:S(2)}, u32[]{:S(2)}) collective-permute-start(bf16[1024,128]{1,0:T(8,128)(2,1)} %project_kv.1.refs_5_), channel_id=1, source_target_pairs={{0,1},{1,0},{2,3},{3,2},{4,5},{5,4},{6,7},{7,6},{8,9},{9,8},{10,11... | collective-permute-start | bytes 786440 | tf_op jit(solution)/shard_map/ppermute | solution.py:30
  20.8 15.8 %collective-permute-start = (bf16[512,256]{1,0:T(8,128)(2,1)}, bf16[512,256]{1,0:T(8,128)(2,1)S(1)}, u32[]{:S(2)}, u32[]{:S(2)}) collective-permute-start(bf16[512,256]{1,0:T(8,128)(2,1)} %get-tuple-element.27.refs_2_), channel_id=1, source_target_pairs={{24,0},{16,8},{25,1},{17,9},{26,2},{18,10},{27,3},{19,11},{28,4},{... | collective-permute-start | bytes 786440 | tf_op jit(solution)/shard_map/ppermute | solution.py:698
  22.1 14.6 %copy-start.1 = (bf16[1024,128]{1,0:T(8,128)(2,1)}, bf16[1024,128]{1,0:T(8,128)(2,1)S(1)}, u32[]{:S(2)}) copy-start(bf16[1024,128]{1,0:T(8,128)(2,1)S(1)} %collective-permute-done.3.refs_8_) | copy-start | bytes 786436
  22.1 14.5 %collective-permute-start.7 = (bf16[1024,128]{1,0:T(8,128)(2,1)S(1)}, bf16[1024,128]{1,0:T(8,128)(2,1)S(1)}, u32[]{:S(2)}, u32[]{:S(2)}) collective-permute-start(bf16[1024,128]{1,0:T(8,128)(2,1)S(1)} %collective-permute-done.3.refs_8_), channel_id=1, source_target_pairs={{0,1},{1,0},{2,3},{3,2},{4,5},{5,4},{6,7},{7,6},{8,9},{9,8},{10,11... | collective-permute-start | bytes 786440 | tf_op jit(solution)/shard_map/ppermute | solution.py:30
  23.8 12.8 %copy-start.2 = (bf16[1024,128]{1,0:T(8,128)(2,1)}, bf16[1024,128]{1,0:T(8,128)(2,1)S(1)}, u32[]{:S(2)}) copy-start(bf16[1024,128]{1,0:T(8,128)(2,1)S(1)} %collective-permute-done.2.refs_7_) | copy-start | bytes 786436
  23.8 12.8 %collective-permute-start.6 = (bf16[1024,128]{1,0:T(8,128)(2,1)S(1)}, bf16[1024,128]{1,0:T(8,128)(2,1)S(1)}, u32[]{:S(2)}, u32[]{:S(2)}) collective-permute-start(bf16[1024,128]{1,0:T(8,128)(2,1)S(1)} %collective-permute-done.2.refs_7_), channel_id=1, source_target_pairs={{0,1},{1,0},{2,3},{3,2},{4,5},{5,4},{6,7},{7,6},{8,9},{9,8},{10,11... | collective-permute-start | bytes 786440 | tf_op jit(solution)/shard_map/ppermute | solution.py:30
  24.1 12.5 %copy-start.3 = (bf16[1024,128]{1,0:T(8,128)(2,1)}, bf16[1024,128]{1,0:T(8,128)(2,1)S(1)}, u32[]{:S(2)}) copy-start(bf16[1024,128]{1,0:T(8,128)(2,1)S(1)} %collective-permute-done.1.refs_6_) | copy-start | bytes 786436
  24.1 12.5 %collective-permute-start.5 = (bf16[1024,128]{1,0:T(8,128)(2,1)S(1)}, bf16[1024,128]{1,0:T(8,128)(2,1)S(1)}, u32[]{:S(2)}, u32[]{:S(2)}) collective-permute-start(bf16[1024,128]{1,0:T(8,128)(2,1)S(1)} %collective-permute-done.1.refs_6_), channel_id=1, source_target_pairs={{0,1},{1,0},{2,3},{3,2},{4,5},{5,4},{6,7},{7,6},{8,9},{9,8},{10,11... | collective-permute-start | bytes 786440 | tf_op jit(solution)/shard_map/ppermute | solution.py:30
  25.0 9.9 %dynamic-slice-start = ((s32[4096]{0:T(1024)}, s32[]{:T(128)}), s32[1024]{0:T(1024)S(1)}, s32[]{:S(2)}) async-start(s32[4096]{0:T(1024)} %refs_0_.3, s32[]{:T(128)} %select_n.21), calls=%async_computation | async-start | bytes 8704 | tf_op jit(solution)/shard_map/dynamic_slice | solution.py:710
  34.8 67.0 %copy-start.21 = (s32[32]{0:T(128)S(1)}, s32[32]{0:T(128)}, u32[]{:S(2)}) copy-start(s32[32]{0:T(128)} %get-tuple-element.52.base) | copy-start | bytes 388
  36.5 47.5 %copy-start = (f32[32,512]{1,0:T(8,128)}, f32[32,512]{1,0:T(8,128)S(1)}, u32[]{:S(2)}) copy-start(f32[32,512]{1,0:T(8,128)S(1)} %fusion.refs_5_) | copy-start | bytes 196612
  36.6 0.7 copy-start.5
  36.6 0.8 copy-start.4
  36.6 0.9 copy-start.6
  36.6 0.9 copy-start.7
  36.6 1.0 copy-start.8
  59.8 5.1 %collective-permute-start.10 = (f32[32,256]{1,0:T(8,128)}, f32[32,256]{1,0:T(8,128)S(1)}, u32[]{:S(2)}, u32[]{:S(2)}) collective-permute-start(f32[32,256]{1,0:T(8,128)} %get-tuple-element.30.refs_0_), channel_id=1, source_target_pairs={{0,24},{8,16},{16,8},{24,0},{1,25},{9,17},{17,9},{25,1},{2,26},{10... | collective-permute-start | bytes 98312 | tf_op jit(solution)/shard_map/ppermute | solution.py:30
  59.8 5.0 %collective-permute-start.9 = (f32[32,256]{1,0:T(8,128)}, f32[32,256]{1,0:T(8,128)S(1)}, u32[]{:S(2)}, u32[]{:S(2)}) collective-permute-start(f32[32,256]{1,0:T(8,128)} %get-tuple-element.30.refs_0_), channel_id=1, source_target_pairs={{0,16},{8,24},{16,0},{24,8},{1,17},{9,25},{17,1},{25,9},{2,18},{10... | collective-permute-start | bytes 98312 | tf_op jit(solution)/shard_map/ppermute | solution.py:30
  62.1 4.1 %collective-permute-start.8 = (f32[32,256]{1,0:T(8,128)}, f32[32,256]{1,0:T(8,128)S(1)}, u32[]{:S(2)}, u32[]{:S(2)}) collective-permute-start(f32[32,256]{1,0:T(8,128)} %get-tuple-element.30.refs_0_), channel_id=1, source_target_pairs={{0,8},{8,0},{16,24},{24,16},{1,9},{9,1},{17,25},{25,17},{2,10},{10... | collective-permute-start | bytes 98312 | tf_op jit(solution)/shard_map/ppermute | solution.py:30
  64.9 1.3 %copy-start.18 = (f32[32,256]{1,0:T(8,128)}, f32[32,256]{1,0:T(8,128)S(1)}, u32[]{:S(2)}) copy-start(f32[32,256]{1,0:T(8,128)S(1)} %collective-permute-done.10.refs_3_) | copy-start | bytes 98308
  64.9 1.3 %copy-start.19 = (f32[32,256]{1,0:T(8,128)}, f32[32,256]{1,0:T(8,128)S(1)}, u32[]{:S(2)}) copy-start(f32[32,256]{1,0:T(8,128)S(1)} %collective-permute-done.9.refs_2_) | copy-start | bytes 98308
  66.2 0.6 copy-start.20
  69.7 1.8 %collective-permute-start.11 = (f32[4,40,512]{2,1,0:T(8,128)}, f32[4,40,512]{2,1,0:T(8,128)S(1)}, u32[]{:S(2)}, u32[]{:S(2)}) collective-permute-start(f32[4,40,512]{2,1,0:T(8,128)} %get-tuple-element.33), channel_id=1, source_target_pairs={{0,1},{1,0},{2,3},{3,2},{4,5},{5,4},{6,7},{7,6},{8,9},{9,8},{10,11... | collective-permute-start | bytes 983048 | tf_op jit(solution)/shard_map/ppermute | solution.py:30
  69.7 8.8 %collective-permute-start.17 = (f32[32,512]{1,0:T(8,128)S(1)}, f32[32,512]{1,0:T(8,128)S(1)}, u32[]{:S(2)}, u32[]{:S(2)}) collective-permute-start(f32[32,512]{1,0:T(8,128)S(1)} %fusion.refs_5_), channel_id=1, source_target_pairs={{0,24},{8,16},{16,8},{24,0},{1,25},{9,17},{17,9},{25,1},{2,26},{10... | collective-permute-start | bytes 196616 | tf_op jit(solution)/shard_map/ppermute | solution.py:30
  73.3 9.5 %collective-permute-start.14 = (f32[40,512]{1,0:T(8,128)S(1)}, f32[40,512]{1,0:T(8,128)S(1)}, u32[]{:S(2)}, u32[]{:S(2)}) collective-permute-start(f32[40,512]{1,0:T(8,128)S(1)} %get-tuple-element.48), channel_id=1, source_target_pairs={{0,6},{1,7},{2,4},{3,5},{4,2},{5,3},{6,0},{7,1},{8,14},{9,15},{10,... | collective-permute-start | bytes 245768 | tf_op jit(solution)/shard_map/ppermute | solution.py:30
  76.8 7.2 %collective-permute-start.13 = (f32[40,512]{1,0:T(8,128)S(1)}, f32[40,512]{1,0:T(8,128)S(1)}, u32[]{:S(2)}, u32[]{:S(2)}) collective-permute-start(f32[40,512]{1,0:T(8,128)S(1)} %get-tuple-element.49), channel_id=1, source_target_pairs={{0,4},{1,5},{2,6},{3,7},{4,0},{5,1},{6,2},{7,3},{8,12},{9,13},{10,... | collective-permute-start | bytes 245768 | tf_op jit(solution)/shard_map/ppermute | solution.py:30
  76.8 7.2 %collective-permute-start.12 = (f32[40,512]{1,0:T(8,128)S(1)}, f32[40,512]{1,0:T(8,128)S(1)}, u32[]{:S(2)}, u32[]{:S(2)}) collective-permute-start(f32[40,512]{1,0:T(8,128)S(1)} %get-tuple-element.50), channel_id=1, source_target_pairs={{0,2},{1,3},{2,0},{3,1},{4,6},{5,7},{6,4},{7,5},{8,10},{9,11},{10,... | collective-permute-start | bytes 245768 | tf_op jit(solution)/shard_map/ppermute | solution.py:30
  77.7 4.3 %collective-permute-start.16 = (f32[32,512]{1,0:T(8,128)S(1)}, f32[32,512]{1,0:T(8,128)S(1)}, u32[]{:S(2)}, u32[]{:S(2)}) collective-permute-start(f32[32,512]{1,0:T(8,128)S(1)} %fusion.refs_5_), channel_id=1, source_target_pairs={{0,16},{8,24},{16,0},{24,8},{1,17},{9,25},{17,1},{25,9},{2,18},{10... | collective-permute-start | bytes 196616 | tf_op jit(solution)/shard_map/ppermute | solution.py:30
  78.5 5.5 %copy-start.15 = (f32[32,512]{1,0:T(8,128)}, f32[32,512]{1,0:T(8,128)S(1)}, u32[]{:S(2)}) copy-start(f32[32,512]{1,0:T(8,128)S(1)} %collective-permute-done.17.refs_8_) | copy-start | bytes 196612
  78.5 4.3 %collective-permute-start.15 = (f32[32,512]{1,0:T(8,128)S(1)}, f32[32,512]{1,0:T(8,128)S(1)}, u32[]{:S(2)}, u32[]{:S(2)}) collective-permute-start(f32[32,512]{1,0:T(8,128)S(1)} %fusion.refs_5_), channel_id=1, source_target_pairs={{0,8},{8,0},{16,24},{24,16},{1,9},{9,1},{17,25},{25,17},{2,10},{10... | collective-permute-start | bytes 196616 | tf_op jit(solution)/shard_map/ppermute | solution.py:30
  81.9 2.1 %copy-start.16 = (f32[32,512]{1,0:T(8,128)}, f32[32,512]{1,0:T(8,128)S(1)}, u32[]{:S(2)}) copy-start(f32[32,512]{1,0:T(8,128)S(1)} %collective-permute-done.16.refs_7_) | copy-start | bytes 196612
  82.8 1.3 %copy-start.17 = (f32[32,512]{1,0:T(8,128)}, f32[32,512]{1,0:T(8,128)S(1)}, u32[]{:S(2)}) copy-start(f32[32,512]{1,0:T(8,128)S(1)} %collective-permute-done.15.refs_6_) | copy-start | bytes 196612
  82.8 1.3 %copy-start.12 = (f32[40,512]{1,0:T(8,128)}, f32[40,512]{1,0:T(8,128)S(1)}, u32[]{:S(2)}) copy-start(f32[40,512]{1,0:T(8,128)S(1)} %collective-permute-done.14.refs_4_) | copy-start | bytes 245764
  84.0 0.6 copy-start.13
  84.0 0.7 copy-start.14
  93.0 2.1 %collective-permute-start.18 = (f32[4,8,4224]{2,1,0:T(8,128)}, f32[4,8,4224]{2,1,0:T(8,128)S(1)}, u32[]{:S(2)}, u32[]{:S(2)}) collective-permute-start(f32[4,8,4224]{2,1,0:T(8,128)} %get-tuple-element.37), channel_id=1, source_target_pairs={{0,1},{1,0},{2,3},{3,2},{4,5},{5,4},{6,7},{7,6},{8,9},{9,8},{10,11... | collective-permute-start | bytes 1622024 | tf_op jit(solution)/shard_map/ppermute | solution.py:30
  96.9 8.3 %collective-permute-start.21 = (f32[8,4224]{1,0:T(8,128)S(1)}, f32[8,4224]{1,0:T(8,128)S(1)}, u32[]{:S(2)}, u32[]{:S(2)}) collective-permute-start(f32[8,4224]{1,0:T(8,128)S(1)} %get-tuple-element.44), channel_id=1, source_target_pairs={{0,6},{1,7},{2,4},{3,5},{4,2},{5,3},{6,0},{7,1},{8,14},{9,15},{10,... | collective-permute-start | bytes 405512 | tf_op jit(solution)/shard_map/ppermute | solution.py:30
  99.5 12.0 %collective-permute-start.20 = (f32[8,4224]{1,0:T(8,128)S(1)}, f32[8,4224]{1,0:T(8,128)S(1)}, u32[]{:S(2)}, u32[]{:S(2)}) collective-permute-start(f32[8,4224]{1,0:T(8,128)S(1)} %get-tuple-element.45), channel_id=1, source_target_pairs={{0,4},{1,5},{2,6},{3,7},{4,0},{5,1},{6,2},{7,3},{8,12},{9,13},{10,... | collective-permute-start | bytes 405512 | tf_op jit(solution)/shard_map/ppermute | solution.py:30
  99.5 12.0 %collective-permute-start.19 = (f32[8,4224]{1,0:T(8,128)S(1)}, f32[8,4224]{1,0:T(8,128)S(1)}, u32[]{:S(2)}, u32[]{:S(2)}) collective-permute-start(f32[8,4224]{1,0:T(8,128)S(1)} %get-tuple-element.46), channel_id=1, source_target_pairs={{0,2},{1,3},{2,0},{3,1},{4,6},{5,7},{6,4},{7,5},{8,10},{9,11},{10,... | collective-permute-start | bytes 405512 | tf_op jit(solution)/shard_map/ppermute | solution.py:30
  105.2 6.3 %copy-start.9 = (f32[8,4224]{1,0:T(8,128)}, f32[8,4224]{1,0:T(8,128)S(1)}, u32[]{:S(2)}) copy-start(f32[8,4224]{1,0:T(8,128)S(1)} %collective-permute-done.21.refs_5_) | copy-start | bytes 405508
  111.5 0.7 copy-start.10
  111.5 0.7 copy-start.11

commit v3 on v2

v3 whole, which is shorter than its diff:
```python
import math

import jax
import jax.numpy as jnp
import numpy as np
from jax import lax
from jax.experimental import pallas as pl
from jax.experimental.pallas import tpu as pltpu
from jax.sharding import PartitionSpec as P

HD = 128
WINDOW = 4096
QB = 256
KB = 512
LANES = 128
GROUP = 16
TOKEN_CHUNKS = 8
AHEAD = 3
COLUMNS_AS_ROWS = True

rope_theta = 10000.0
norm_eps = 1e-06
MIB = 1024 * 1024

f32 = jnp.float32
bf16 = jnp.bfloat16
i32 = jnp.int32


def swapped(x, axis, mask):
    count = lax.axis_size(axis)
    return lax.ppermute(x, axis, [(i, i ^ mask) for i in range(count)])


def angle_tables(seq_len):
    inverse = np.exp(-(2.0 * np.arange(HD // 2) / HD) * math.log(rope_theta))
    inverse = np.repeat(inverse, 2)[None, :]
    fine = np.arange(LANES)[:, None] * inverse
    coarse = LANES * np.arange(seq_len // LANES)[:, None] * inverse
    fine_tab = np.stack([np.cos(fine), np.sin(fine)]).astype(np.float32)
    coarse_tab = np.stack([np.cos(coarse), np.sin(coarse)]).astype(np.float32)
    return fine_tab, coarse_tab


def turn(fine, coarse, which):
    ca = coarse[0, pl.ds(which, 1), :]
    sa = coarse[1, pl.ds(which, 1), :]
    cb = fine[0]
    sb = fine[1]
    return ca * cb - sa * sb, sa * cb + ca * sb


def pair_swap(x, even):
    up = pltpu.roll(x, x.shape[1] - 1, 1)
    down = pltpu.roll(x, 1, 1)
    return jnp.where(even, up, down)


def far(x):
    return pltpu.with_memory_space_constraint(x, pltpu.HBM)


def near(x):
    return pltpu.with_memory_space_constraint(x, pltpu.VMEM)


def stream(source, buffer, sems, chunks, axis):
    size = source.shape[axis] // chunks
    result = []
    for i in range(chunks):
        part = pl.ds(i * size, size)
        at = (part, slice(None)) if axis == 0 else (slice(None), part)
        result.append(pltpu.make_async_copy(source.at[at], buffer.at[at], sems.at[i]))
    return result


def kv_body(chunks, seg_total, *refs):
    ids_in, wk_in, wv_in, fine_in, coarse_in, tok_in = refs[:6]
    out, pooled, tables, tok, key_tables, weight, ids, fine, coarse, acc, small, sems = refs[6:]
    rows, width = tok.shape
    half = wk_in.shape[0]
    subs = rows // LANES
    size = width // chunks
    rest = [
        pltpu.make_async_copy(wk_in, weight.at[pl.ds(0, half), :], small.at[0]),
        pltpu.make_async_copy(wv_in, weight.at[pl.ds(half, half), :], small.at[1]),
        pltpu.make_async_copy(fine_in, fine, small.at[2]),
        pltpu.make_async_copy(coarse_in, coarse, small.at[3]),
        pltpu.make_async_copy(ids_in, ids, small.at[4]),
    ]
    for c in rest:
        c.start()
    copies = stream(tok_in, tok, sems, chunks, 1)
    for c in copies[:AHEAD]:
        c.start()
    for c in rest:
        c.wait()
    lane = lax.broadcasted_iota(i32, (LANES, LANES), 1)
    even = lane % 2 == 0
    upper = lax.axis_index("tp") % 2 == 1
    first = lax.axis_index("seq") * subs
    members = []
    for sub in range(subs):
        at = slice(sub * LANES, (sub + 1) * LANES)
        cos, sin = turn(fine, coarse, first + sub)
        sin = jnp.where(even, -sin, sin)
        tables[0, at, :] = cos
        tables[1, at, :] = sin
        cos = jnp.where(upper, pltpu.roll(cos, half, 1), cos)
        sin = jnp.where(upper, pltpu.roll(sin, half, 1), sin)
        key_tables[0, at, :] = jnp.where(lane < half, cos, 1.0)
        key_tables[1, at, :] = jnp.where(lane < half, sin, 0.0)
        member = ids[pl.ds(first + sub, 1), :] == lax.broadcasted_iota(i32, (seg_total, LANES), 0)
        members.append(jnp.where(member, 1.0, 0.0))
    for i in range(chunks):
        at = slice(i * size, (i + 1) * size)
        copies[i].wait()
        if i + AHEAD < chunks:
            copies[i + AHEAD].start()
        part = lax.dot_general(
            tok[:, at], weight[:, at], (((1,), (1,)), ((), ())), preferred_element_type=f32
        )
        acc[...] = part if i == 0 else acc[...] + part
    for sub in range(subs):
        at = slice(sub * LANES, (sub + 1) * LANES)
        x = acc[at]
        x = x * key_tables[0, at, :] + pair_swap(x, even) * key_tables[1, at, :]
        out[at, :] = x.astype(bf16)
    feat = pooled.shape[1]
    cols = pl.ds(pl.multiple_of(lax.axis_index("tp") * feat, feat), feat)
    member = jnp.concatenate(members, 1).astype(bf16)
    pooled[...] = jnp.dot(member, tok[:, cols], preferred_element_type=f32)


def project_kv(tokens, w_key, w_value, fine, coarse, ids, seg_total, feat):
    rows, width = tokens.shape
    half = w_key.shape[1]
    whole = pl.BlockSpec(memory_space=pltpu.VMEM)

    def body(*refs):
        kv_body(TOKEN_CHUNKS, seg_total, *refs)

    return pl.pallas_call(
        body,
        in_specs=[pl.BlockSpec(memory_space=pltpu.HBM)] * 6,
        out_specs=[whole] * 3,
        out_shape=[
            jax.ShapeDtypeStruct((rows, 2 * half), bf16),
            jax.ShapeDtypeStruct((seg_total, feat), f32),
            jax.ShapeDtypeStruct((2, rows, LANES), f32),
        ],
        scratch_shapes=[
            pltpu.VMEM((rows, width), bf16),
            pltpu.VMEM((2, rows, LANES), f32),
            pltpu.VMEM((2 * half, width), bf16),
            pltpu.VMEM(ids.shape, i32),
            pltpu.VMEM(fine.shape, f32),
            pltpu.VMEM(coarse.shape, f32),
            pltpu.VMEM((rows, 2 * half), f32),
            pltpu.SemaphoreType.DMA((5,)),
            pltpu.SemaphoreType.DMA((TOKEN_CHUNKS,)),
        ],
        compiler_params=pltpu.CompilerParams(vmem_limit_bytes=20 * MIB),
        name="project_kv",
    )(*[far(x) for x in (ids, w_key.T, w_value.T, fine, coarse, tokens)])


def q_body(tok, weight, tables, *refs):
    outs = refs[:2]
    acc = refs[2]
    rows = tok.shape[0]
    subs = rows // LANES
    per_out = subs // len(outs)
    heads = weight.shape[1] // HD
    acc[...] = jnp.dot(tok[...], weight[...], preferred_element_type=f32)
    even = lax.broadcasted_iota(i32, (LANES, LANES), 1) % 2 == 0
    upper = lax.axis_index("tp") % 2 == 1
    scale = HD ** (-0.5) * math.log2(math.e)
    for sub in range(subs):
        at = slice(sub * LANES, (sub + 1) * LANES)
        cos = tables[0, at, :] * scale
        sin = tables[1, at, :] * scale
        out = outs[sub // per_out]
        row = (sub % per_out) * LANES
        for h in range(heads):
            x = acc[at, h * HD : (h + 1) * HD]
            x = x * cos + pair_swap(x, even) * sin
            x = jnp.where(upper, pltpu.roll(x, HD // 2, 1), x)
            out[row : row + LANES, h * HD : (h + 1) * HD] = x.astype(bf16)


def project_q(tokens, w_query, tables):
    rows = tokens.shape[0]
    cols = w_query.shape[1]
    whole = pl.BlockSpec(memory_space=pltpu.VMEM)
    out = jax.ShapeDtypeStruct((rows // 2, cols), bf16)
    return pl.pallas_call(
        q_body,
        in_specs=[whole] * 3,
        out_specs=[whole, whole],
        out_shape=[out, out],
        scratch_shapes=[pltpu.VMEM((rows, cols), f32)],
        compiler_params=pltpu.CompilerParams(vmem_limit_bytes=20 * MIB),
        name="project_q",
    )(near(tokens), near(w_query), near(tables))


def cent_body(chunks, groups, place, owner_counts, gain_in, cent_in, *refs):
    wide, norms, picked, gain, chosen, hit, match = refs[:7]
    cent, wide_buf, in_sems, out_sems = refs[7:]
    rows, feat = cent.shape
    size = rows // chunks
    block = norms.shape[1]
    loads = stream(cent_in, cent, in_sems, chunks, 0)
    stores = []
    for i in range(chunks):
        at = pl.ds(i * size, size)
        stores.append(pltpu.make_async_copy(wide_buf.at[at, :], wide.at[at, :], out_sems.at[i]))
    for c in loads:
        c.start()
    gain[...] = gain_in[...]
    slots = hit.shape[0]
    seg_total = chosen.shape[1]
    rank = lax.axis_index("tp")
    slot = lax.broadcasted_iota(i32, (slots, seg_total), 0)
    column = lax.broadcasted_iota(i32, (slots, seg_total), 1)
    for k in range(2):
        for m in range(groups):
            start, number = owner_span(owner_counts, rank ^ (2 * m + k))
            row = (k * groups + m) * slots
            taken = (slot + start == column) & (slot < number)
            chosen[row : row + slots, :] = jnp.where(taken, 1.0, 0.0)
    start, number = owner_span(owner_counts, rank)
    slot = lax.broadcasted_iota(i32, (slots, LANES), 0)
    column = lax.broadcasted_iota(i32, (slots, LANES), 1)
    hit[...] = jnp.where((slot + start == column) & (slot < number), 1.0, 0.0)
    third = lax.broadcasted_iota(i32, (1, match.shape[1]), 1) % seg_total
    assigned = jnp.zeros((1, match.shape[1]), i32)
    for r in range(seg_total):
        assigned = jnp.where(third == r, place[3, r], assigned)
    member = lax.broadcasted_iota(i32, (GROUP, match.shape[1]), 0)
    for r in range(seg_total):
        same = jnp.where(assigned == member + place[1, r], 1.0, 0.0)
        match[r * GROUP : (r + 1) * GROUP, :] = same.astype(bf16)

    def widen(b, carry):
        at = pl.ds(pl.multiple_of(b * block, block), block)
        c = cent[at, :].astype(f32)
        wide_buf[at, :] = c
        square = c * c
        part = square[:, :LANES]
        for g in range(1, feat // LANES):
            part = part + square[:, g * LANES : (g + 1) * LANES]
        norms[pl.ds(b, 1), :] = jnp.sum(part.T, axis=0, keepdims=True)
        return carry

    per_chunk = size // block
    for i in range(chunks):
        loads[i].wait()
        lax.fori_loop(i * per_chunk, (i + 1) * per_chunk, widen, 0)
        stores[i].start()
    for r in range(seg_total):
        first = pl.multiple_of(place[0, r], GROUP)
        picked[r * GROUP : (r + 1) * GROUP, :] = cent[pl.ds(first, GROUP), :]
    for c in stores:
        c.wait()


def widen_centroids(place, owner_counts, gain, centroids, groups, slots):
    rows, feat = centroids.shape
    count = place.shape[1]
    chunks = 4
    whole = pl.BlockSpec(memory_space=pltpu.VMEM)
    scalar = pl.BlockSpec(memory_space=pltpu.SMEM)
    in_hbm = pl.BlockSpec(memory_space=pltpu.HBM)

    def body(*refs):
        cent_body(chunks, groups, *refs)

    return pl.pallas_call(
        body,
        in_specs=[scalar, scalar, whole, in_hbm],
        out_specs=[in_hbm] + [whole] * 6,
        out_shape=[
            jax.ShapeDtypeStruct((rows, feat), f32),
            jax.ShapeDtypeStruct((8, rows // 8), f32),
            jax.ShapeDtypeStruct((count * GROUP, feat), bf16),
            jax.ShapeDtypeStruct((1, feat), f32),
            jax.ShapeDtypeStruct((2 * groups * slots, count), f32),
            jax.ShapeDtypeStruct((slots, LANES), f32),
            jax.ShapeDtypeStruct((count * GROUP, 3 * count), bf16),
        ],
        scratch_shapes=[
            pltpu.VMEM((rows, feat), bf16),
            pltpu.VMEM((rows, feat), f32),
            pltpu.SemaphoreType.DMA((chunks,)),
            pltpu.SemaphoreType.DMA((chunks,)),
        ],
        compiler_params=pltpu.CompilerParams(vmem_limit_bytes=24 * MIB),
        name="widen_centroids",
    )(place, owner_counts, gain, far(centroids))


def segment_starts(ids):
    rows = ids.shape[0]
    row = lax.broadcasted_iota(i32, ids.shape, 0)
    lane = lax.broadcasted_iota(i32, ids.shape, 1)
    left = pltpu.roll(ids, 1, 1)
    left = jnp.where(lane == 0, pltpu.roll(left, 1, 0), left)
    token = row * LANES + lane
    first = jnp.where((ids != left) & (token > 0), token, 0)
    shift = 1
    while shift < LANES:
        first = jnp.maximum(first, jnp.where(lane >= shift, pltpu.roll(first, shift, 1), 0))
        shift = shift * 2
    above = jnp.broadcast_to(jnp.max(first, axis=1, keepdims=True), ids.shape)
    above = jnp.where(row >= 1, pltpu.roll(above, 1, 0), 0)
    shift = 1
    while shift < rows:
        above = jnp.maximum(above, jnp.where(row >= shift, pltpu.roll(above, shift, 0), 0))
        shift = shift * 2
    return jnp.maximum(first, above)


def attend_body(pieces, seg_total, balanced, seg, ids, *refs):
    queries = refs[: 3 if balanced else 2]
    refs = refs[len(queries) :]
    own_in = refs[:pieces]
    other_in = refs[pieces : 2 * pieces]
    token_sums = refs[2 * pieces : 3 * pieces]
    out, counts, tokens_out, q_all, kv, starts, weights, tops, col, lhs, sems = refs[
        3 * pieces :
    ]
    q_rows, q_cols = queries[0].shape
    rows = own_in[0].shape[0]
    heads = q_cols // HD
    half = HD // 2
    seq_len = kv.shape[0]
    wide = heads * QB
    own_blocks = rows // QB
    rank = lax.axis_index("seq")
    upper = lax.axis_index("tp") % 2 == 1

    copies = []
    for k, source in enumerate(queries):
        target = q_all.at[pl.ds(k * q_rows, q_rows), :]
        copies.append(pltpu.make_async_copy(source, target, sems.at[len(copies)]))
    for k, sources in enumerate((own_in, other_in)):
        for m in range(pieces):
            row0 = pl.multiple_of((rank ^ m) * rows, rows)
            place = kv.at[pl.ds(row0, rows), pl.ds(k * HD, HD)]
            copies.append(pltpu.make_async_copy(sources[m], place, sems.at[len(copies)]))
    for c in copies:
        c.start()
    col[...] = jnp.zeros(col.shape, f32)
    starts[...] = segment_starts(ids[...])
    for c in copies:
        c.wait()

    def q_step(n, carry):
        home = n < own_blocks
        base = jnp.where(home, rank, rank ^ 3) * rows + jnp.where(home, n, n - own_blocks) * QB
        base = pl.multiple_of(base, QB)
        last_seg = seg[base + QB - 1]
        first_seg = seg[base]
        end = (base + QB - 1) // KB + 1
        clear_end = base // KB
        begin = jnp.int32(0)
        clear = jnp.int32(0)
        for t in range(seq_len // KB):
            begin = begin + (seg[t * KB + KB - 1] < first_seg).astype(i32)
            outside = (seg[t * KB] != last_seg) | (base + QB - 1 - t * KB >= WINDOW)
            clear = clear + (outside & (t < clear_end)).astype(i32)
        begin = jnp.maximum(begin, jnp.maximum(base - (WINDOW - 1), 0) // KB)
        begin = jnp.minimum(begin, clear_end)
        clear = jnp.clip(clear, begin, clear_end)

        q_at = pl.ds(pl.multiple_of(n * QB, QB), QB)
        nothing = jnp.zeros((QB, half), bf16)
        q = []
        for h in range(heads):
            x = q_all[q_at, h * HD : (h + 1) * HD]
            q.append(jnp.concatenate([x[:, :half], nothing, x[:, half:], nothing], 1))
        low = [starts[pl.ds(base // LANES + g, 1), :] for g in range(QB // LANES)]
        low = jnp.concatenate(low, 1)
        i_pos = base + lax.broadcasted_iota(i32, (1, QB), 1)
        if seq_len > WINDOW:
            low = jnp.maximum(low, i_pos - (WINDOW - 1))

        def score(masked, size, kb, carry):
            start = pl.multiple_of(kb * KB, KB)
            rows_kb = kv[pl.ds(start, size), :]
            if masked:
                j_pos = start + lax.broadcasted_iota(i32, (size, QB), 0)
                allowed = (j_pos <= i_pos) & (j_pos >= low)
            result = []
            for h in range(heads):
                top, total = carry[h]
                lanes = slice(h * QB, (h + 1) * QB)
                s = lax.dot_general(
                    rows_kb, q[h], (((1,), (1,)), ((), ())), preferred_element_type=f32
                )
                if masked:
                    s = jnp.where(allowed, s, -1e30)
                new_top = jnp.maximum(top, jnp.max(s, axis=0, keepdims=True))
                p = jnp.exp2(s - new_top)
                weights[pl.ds(start, size), lanes] = p.astype(bf16)
                tops[pl.ds(kb, 1), lanes] = new_top
                p = jnp.sum(p.reshape(size // 8, 8, QB), axis=0)
                result.append((new_top, total * jnp.exp2(top - new_top) + p))
            return tuple(result)

        state = (jnp.full((1, QB), -1e30, f32), jnp.zeros((8, QB), f32))
        state = (state,) * heads
        pairs = (clear_end - clear) // 2
        single = clear + 2 * pairs
        state = lax.fori_loop(begin, clear, lambda kb, c: score(True, KB, kb, c), state)
        state = lax.fori_loop(
            0, pairs, lambda t, c: score(False, 2 * KB, clear + 2 * t, c), state
        )
        state = lax.fori_loop(single, clear_end, lambda kb, c: score(False, KB, kb, c), state)
        state = lax.fori_loop(clear_end, end, lambda kb, c: score(True, KB, kb, c), state)
        top = jnp.concatenate([t for t, _ in state], 1)
        total = jnp.concatenate([t for _, t in state], 1)
        share = 1.0 / jnp.sum(total, axis=0, keepdims=True)
        row = lax.broadcasted_iota(i32, (16, wide), 0)
        head = lax.broadcasted_iota(i32, (16, wide), 1) // QB

        def gather(size, kb, carry):
            start = pl.multiple_of(kb * KB, KB)
            r = share * jnp.exp2(tops[pl.ds(kb, 1), :] - top)
            high = r.astype(bf16).astype(f32)
            r = jnp.where(row == head, high, jnp.where(row == heads + head, r - high, 0.0))
            at = pl.ds(start, size)
            contract = (((1,), (1,)), ((), ()))
            w = weights[at, :]
            r = r.astype(bf16)
            if COLUMNS_AS_ROWS:
                add = lax.dot_general(r, w, contract, preferred_element_type=f32)
                col[:16, at] = col[:16, at] + add
            else:
                add = lax.dot_general(w, r, contract, preferred_element_type=f32)
                col[at, :16] = col[at, :16] + add
            return carry

        lax.fori_loop(begin, clear, lambda kb, c: gather(KB, kb, c), 0)
        lax.fori_loop(0, pairs, lambda t, c: gather(2 * KB, clear + 2 * t, c), 0)
        lax.fori_loop(single, end, lambda kb, c: gather(KB, kb, c), 0)
        return carry

    if balanced:
        low_n = jnp.where(rank == 3, 2, jnp.where(rank == 2, 1, 0))
        high_n = own_blocks + jnp.where(rank == 0, 2, jnp.where(rank == 1, 1, 0))
    else:
        low_n = 0
        high_n = own_blocks
    lax.fori_loop(low_n, high_n, q_step, 0)

    number = jnp.zeros((seg_total, LANES), f32)
    for g in range(seq_len // LANES):
        at = slice(g * LANES, (g + 1) * LANES)
        member = ids[g : g + 1, :] == lax.broadcasted_iota(i32, (seg_total, LANES), 0)
        number = number + member.astype(f32)
        turned = col[:16, at] if COLUMNS_AS_ROWS else col[at, :].T
        for h in range(heads):
            w = turned[h : h + 1] + turned[heads + h : heads + h + 1]
            w = jnp.where(member, w, 0.0)
            high = w.astype(bf16)
            lhs[h * seg_total : (h + 1) * seg_total, at] = high
            rest = (w - high.astype(f32)).astype(bf16)
            lhs[(heads + h) * seg_total : (heads + h + 1) * seg_total, at] = rest
    sums = token_sums[0][...]
    for t in token_sums[1:]:
        sums = sums + t[...]
    tokens_out[...] = sums
    counts[...] = jnp.broadcast_to(jnp.sum(number, axis=1, keepdims=True), counts.shape)
    pooled = jnp.dot(lhs[...], kv[...], preferred_element_type=f32)
    pooled = jnp.concatenate([pooled[:, half:HD], pooled[:, HD + half :]], 1)
    for h in range(heads):
        x = pooled[h * seg_total : (h + 1) * seg_total]
        x = x + pooled[(heads + h) * seg_total : (heads + h + 1) * seg_total]
        out[:, h * HD : (h + 1) * HD] = jnp.where(upper, pltpu.roll(x, half, 1), x)


def attend(seg_ids, ids, queries, own, other, token_sums, seg_total, balanced):
    q_rows, cols = queries[0].shape
    rows = own[0].shape[0]
    seq_len = seg_ids.shape[0]
    pieces = len(own)
    heads = cols // HD
    whole = pl.BlockSpec(memory_space=pltpu.VMEM)
    anywhere = pl.BlockSpec(memory_space=pl.ANY)
    inputs = len(queries) + 2 * pieces

    def body(*refs):
        attend_body(pieces, seg_total, balanced, *refs)

    return pl.pallas_call(
        body,
        in_specs=[pl.BlockSpec(memory_space=pltpu.SMEM), whole]
        + [anywhere] * inputs
        + [whole] * pieces,
        out_specs=[whole, whole, whole],
        out_shape=[
            jax.ShapeDtypeStruct((seg_total, cols), f32),
            jax.ShapeDtypeStruct((seg_total, LANES), f32),
            jax.ShapeDtypeStruct(token_sums[0].shape, f32),
        ],
        scratch_shapes=[
            pltpu.VMEM((len(queries) * q_rows, cols), bf16),
            pltpu.VMEM((seq_len, 2 * HD), bf16),
            pltpu.VMEM((seq_len // LANES, LANES), i32),
            pltpu.VMEM((seq_len, heads * QB), bf16),
            pltpu.VMEM((max(8, seq_len // KB), heads * QB), f32),
            pltpu.VMEM((16, seq_len) if COLUMNS_AS_ROWS else (seq_len, LANES), f32),
            pltpu.VMEM((2 * heads * seg_total, seq_len), bf16),
            pltpu.SemaphoreType.DMA((inputs,)),
        ],
        compiler_params=pltpu.CompilerParams(vmem_limit_bytes=24 * MIB),
        name="attend",
    )(seg_ids, ids, *queries, *own, *other, *token_sums)


def mix_body(pieces, *refs):
    parts = refs[:pieces]
    norms, w_out, keep, send = refs[pieces:]
    groups, _, feat = keep.shape
    seg_total = parts[0].shape[0]
    mixed = parts[0][...]
    for p in parts[1:]:
        mixed = mixed + p[...]
    high = mixed.astype(bf16)
    low = (mixed - high.astype(f32)).astype(bf16)
    lhs = jnp.concatenate([high, low], 0)
    rank = lax.axis_index("tp")
    for k, target in enumerate((keep, send)):
        for m in range(groups):
            owner = rank ^ (2 * m + k)
            cols = pl.ds(pl.multiple_of(owner * feat, feat), feat)
            y = jnp.dot(lhs, w_out[:, cols], preferred_element_type=f32)
            target[m, :seg_total, :] = y[:seg_total] + y[seg_total:]
            target[m, seg_total:, :] = norms[...]


def mix(parts, norms, w_out, feat, groups):
    seg_total = parts[0].shape[0]
    whole = pl.BlockSpec(memory_space=pltpu.VMEM)
    out = jax.ShapeDtypeStruct((groups, seg_total + 8, feat), f32)

    def body(*refs):
        mix_body(len(parts), *refs)

    return pl.pallas_call(
        body,
        in_specs=[whole] * (len(parts) + 2),
        out_specs=[whole, whole],
        out_shape=[out, out],
        compiler_params=pltpu.CompilerParams(vmem_limit_bytes=16 * MIB),
        name="mix",
    )(*parts, norms, w_out)


def fold_body(groups, keep, received, own, *sends):
    rows = keep.shape[-1]
    own[...] = keep[0] + received[0]
    for m in range(1, groups):
        total = keep[m] + received[m]
        target = sends[m - 1]
        if target.dtype == f32:
            target[...] = total
        else:
            last = total[:, rows - LANES :]
            high = last.astype(bf16)
            target[:, : rows - LANES] = total[:, : rows - LANES].astype(bf16)
            target[:, rows - LANES : rows] = high
            target[:, rows:] = (last - high.astype(f32)).astype(bf16)


def fold(keep, received, kind):
    groups, rows, cols = keep.shape
    whole = pl.BlockSpec(memory_space=pltpu.VMEM)
    sent = jax.ShapeDtypeStruct((rows, cols if kind == f32 else cols + LANES), kind)

    def body(*refs):
        fold_body(groups, *refs)

    result = pl.pallas_call(
        body,
        in_specs=[whole, whole],
        out_specs=[whole] * groups,
        out_shape=[jax.ShapeDtypeStruct((rows, cols), f32)] + [sent] * (groups - 1),
        compiler_params=pltpu.CompilerParams(vmem_limit_bytes=12 * MIB),
        name="fold",
    )(keep, received)
    return [result[0]] + [swapped(result[m], "tp", 2 * m) for m in range(1, groups)]


def owner_span(owner_counts, owner):
    start = jnp.int32(0)
    for o in range(owner_counts.shape[0]):
        start = start + jnp.where(o < owner, owner_counts[o], 0)
    return start, owner_counts[owner]


def cross_body(groups, chunks, model_width, *refs):
    mixed = refs[:groups]
    token_sums, counts, gain, chosen, cent = refs[groups : groups + 5]
    keep, send, emb, norms, lhs = refs[groups + 5 :]
    seg_total, feat = emb.shape
    rows = cent.shape[0]
    slots = keep.shape[1]
    per_side = groups * slots

    total = mixed[0][...]
    for p in mixed[1:]:
        total = total + p[...]
    norms[...] = total[seg_total:]
    pooled = (total[:seg_total] + token_sums[...]) / counts[:, :1]
    square = jnp.sum(pooled * pooled, axis=1, keepdims=True)
    row = lax.broadcasted_iota(i32, (seg_total, LANES), 0)
    lane = lax.broadcasted_iota(i32, (seg_total, LANES), 1)
    square = jnp.sum(jnp.where(row == lane, square, 0.0), axis=0, keepdims=True)
    square = jnp.broadcast_to(square, (slots, LANES))
    scaled = pooled * gain[...]
    emb[...] = scaled
    high = scaled.astype(bf16)
    low = (scaled - high.astype(f32)).astype(bf16)
    picks = chosen[...].astype(bf16)
    factor = -2.0 / model_width**0.5
    lhs[: 2 * per_side] = (jnp.dot(picks, high, preferred_element_type=f32) * factor).astype(bf16)
    lhs[2 * per_side :] = (jnp.dot(picks, low, preferred_element_type=f32) * factor).astype(bf16)
    for target in (keep, send):
        for m in range(groups):
            target[m, :, rows:] = square

    size = rows // chunks
    for i in range(chunks):
        at = slice(i * size, (i + 1) * size)
        y = lax.dot_general(
            cent[at, :], lhs[...], (((1,), (1,)), ((), ())), preferred_element_type=f32
        ).T
        y = y[: 2 * per_side] + y[2 * per_side :]
        for k, target in enumerate((keep, send)):
            for m in range(groups):
                first = k * per_side + m * slots
                target[m, :, at] = y[first : first + slots]


def cross(mixed, token_sums, counts, gain, chosen, centroids, slots, model_width):
    rows, feat = centroids.shape
    groups = len(mixed)
    seg_total = counts.shape[0]
    whole = pl.BlockSpec(memory_space=pltpu.VMEM)
    side = jax.ShapeDtypeStruct((groups, slots, rows + LANES), f32)

    def body(*refs):
        cross_body(groups, 4, model_width, *refs)

    return pl.pallas_call(
        body,
        in_specs=[whole] * (groups + 5),
        out_specs=[whole] * 4,
        out_shape=[
            side,
            side,
            jax.ShapeDtypeStruct((seg_total, feat), f32),
            jax.ShapeDtypeStruct((8, rows // 8), f32),
        ],
        scratch_shapes=[pltpu.VMEM((4 * groups * slots, feat), bf16)],
        compiler_params=pltpu.CompilerParams(vmem_limit_bytes=16 * MIB),
        name="cross",
    )(*mixed, token_sums, counts, gain, chosen, centroids)


def finish_body(groups, model_width, place, *refs):
    terms = refs[:groups]
    norms, emb, hit, match, picked, wide_in, dist, wide, moved, sems = refs[groups:]
    seg_total, feat = emb.shape
    block = norms.shape[1]
    rows = dist.shape[1]
    total = terms[0][:, rows:]
    for t in terms[1:]:
        total = total + t[:, rows : rows + LANES].astype(f32)
        total = total + t[:, rows + LANES :].astype(f32)
    scale = lax.rsqrt(total / model_width + norm_eps)

    spread = jnp.broadcast_to(scale[:1], (seg_total, LANES))
    r_row = lax.broadcasted_iota(i32, (seg_total, LANES), 0)
    r_lane = lax.broadcasted_iota(i32, (seg_total, LANES), 1)
    row_scale = jnp.sum(jnp.where(r_row == r_lane, spread, 0.0), axis=1, keepdims=True)
    value = emb[...] * row_scale
    high = value.astype(bf16)
    rest = value - high.astype(f32)
    middle = rest.astype(bf16)
    low = (rest - middle.astype(f32)).astype(bf16)
    stacked = jnp.concatenate([high, middle, low], 0)
    once = lax.broadcasted_iota(i32, (3 * seg_total, LANES), 0) < seg_total
    stacked = jnp.concatenate([stacked, jnp.where(once, 1.0, 0.0).astype(bf16)], 1)
    added = jnp.dot(match[...], stacked, preferred_element_type=f32)
    shrink = 1.0 / (1.0 + added[:, feat:])
    for g in range(feat // LANES):
        at = slice(g * LANES, (g + 1) * LANES)
        moved[:, at] = (picked[:, at].astype(f32) + added[:, at]) * shrink

    def write(r):
        first = pl.multiple_of(place[0, r], GROUP)
        return pltpu.make_async_copy(
            moved.at[pl.ds(r * GROUP, GROUP), :], wide.at[pl.ds(first, GROUP), :], sems.at[r]
        )

    for r in range(seg_total):
        pl.when(place[2, r] == 1)(lambda r=r: write(r).start())

    own_scale = jnp.sum(hit[...] * scale, axis=1, keepdims=True)
    valid = jnp.sum(hit[...], axis=1, keepdims=True) > 0.0
    for g in range(rows // block):
        at = slice(g * block, (g + 1) * block)
        y = terms[0][:, at]
        for t in terms[1:]:
            y = y + t[:, at].astype(f32)
        y = norms[g : g + 1, :] * (1.0 / model_width**0.5) + y * own_scale
        dist[:, at] = jnp.where(valid, y, 0.0)

    for r in range(seg_total):
        pl.when(place[2, r] == 1)(lambda r=r: write(r).wait())


def finish(place, terms, norms, emb, hit, match, picked, wide, model_width):
    groups = len(terms)
    seg_total = emb.shape[0]
    slots, rows = terms[0].shape
    rows = rows - LANES
    whole = pl.BlockSpec(memory_space=pltpu.VMEM)
    in_hbm = pl.BlockSpec(memory_space=pltpu.HBM)
    scalar = pl.BlockSpec(memory_space=pltpu.SMEM)

    def body(*refs):
        finish_body(groups, model_width, *refs)

    return pl.pallas_call(
        body,
        in_specs=[scalar] + [whole] * (groups + 5) + [in_hbm],
        out_specs=[whole, in_hbm],
        out_shape=[
            jax.ShapeDtypeStruct((slots, rows), f32),
            jax.ShapeDtypeStruct(wide.shape, f32),
        ],
        scratch_shapes=[
            pltpu.VMEM((seg_total * GROUP, emb.shape[1]), f32),
            pltpu.SemaphoreType.DMA((seg_total,)),
        ],
        input_output_aliases={1 + groups + 5: 1},
        compiler_params=pltpu.CompilerParams(vmem_limit_bytes=16 * MIB),
        name="finish",
    )(place, *terms, norms, emb, hit, match, picked, wide)


def shards(
    tokens, w_query, w_key, w_value, w_out, seg_ids, owner_counts, centroids, pool_gain, assign
):
    tok_rows, model_width = tokens.shape
    seq_len = seg_ids.shape[0]
    seg_total = assign.shape[0]
    rank_seq = lax.axis_index("seq")
    seq_total = lax.axis_size("seq")
    tp_total = lax.axis_size("tp")
    groups = tp_total // 2
    feat = model_width // tp_total
    cent_rows = centroids.shape[0]
    slots = 2 * seg_total // owner_counts.shape[0]
    fine_np, coarse_np = angle_tables(seq_len)
    fine = jnp.asarray(fine_np)
    coarse = jnp.asarray(coarse_np)

    ids = seg_ids.reshape(seq_len // LANES, LANES)
    masks = range(1, seq_total)

    own, pooled, tables = project_kv(
        tokens, w_key, w_value, fine, coarse, ids, seg_total, model_width // tp_total
    )
    own = [own] + [swapped(own, "seq", m) for m in masks]
    other = [swapped(x, "tp", 1) for x in own]

    queries = list(project_q(tokens, w_query, tables))
    balanced = seq_total == 4 and seq_len <= WINDOW and tok_rows == 4 * QB
    if balanced:
        queries = queries + [lax.ppermute(queries[0], "seq", [(3, 0), (2, 1)])]

    local = assign - rank_seq * cent_rows
    mine = (local >= 0) & (local < cent_rows)
    first_row = jnp.where(mine, local // GROUP * GROUP, 0)
    line = assign // GROUP
    order = jnp.arange(seg_total, dtype=i32)
    repeat = jnp.any((line[:, None] == line[None, :]) & (order[None, :] < order[:, None]), axis=1)
    place = jnp.stack([first_row, line * GROUP, (mine & ~repeat).astype(i32), assign])
    wide, norms, picked, gain, chosen, hit, match = widen_centroids(
        place, owner_counts, pool_gain.reshape(1, feat), centroids, groups, slots
    )

    pooled_tokens = [pooled] + [swapped(pooled, "seq", m) for m in masks]

    queries, wide, norms, picked, gain, chosen, hit, match, pooled_tokens = lax.optimization_barrier(
        (queries, wide, norms, picked, gain, chosen, hit, match, pooled_tokens)
    )
    attended, counts, token_sums = attend(
        seg_ids, ids, queries, own, other, pooled_tokens, seg_total, balanced
    )
    attended = [attended] + [swapped(attended, "seq", m) for m in masks]

    keep, send = mix(attended, norms, w_out, feat, groups)
    mixed = fold(keep, swapped(send, "tp", 1), f32)

    keep, send, emb, norms = cross(
        mixed, token_sums, counts, gain, chosen, centroids, slots, model_width
    )
    terms = fold(keep, swapped(send, "tp", 1), bf16)
    distances, updated = finish(
        place, terms, norms, emb, hit, match, picked, wide, model_width
    )
    return (distances, updated)


def solution(mesh):
    in_specs = (
        P("seq", None),
        P(None, "tp"),
        P(None, "tp"),
        P(None, "tp"),
        P("tp", None),
        P(),
        P(),
        P("seq", "tp"),
        P("tp"),
        P(),
    )
    out_specs = (P("tp", "seq"), P("seq", "tp"))
    return jax.shard_map(shards, mesh=mesh, in_specs=in_specs, out_specs=out_specs, check_vma=False)
```

time: 117 us -> 91.6 us (0.78)
  Pallas kernels: 62.5 us -> 38.3 us
  waiting for transfers between devices: 20.5 us -> 24.8 us
  other arithmetic: 3.49 us -> 0.93 us
  matrix products: 1.69 us -> 0 us
  local copies, waits for them, and re-layouts: 4.86 us -> 3.41 us
    pallas_call x5 -> x7, Pallas kernels: 37.5 us -> 19.8 us  [the longest x1 7.14 us: project_kv(): pl.pallas_call(body, in_specs=[pl.BlockSpec(memory_space=pltpu.HBM)] * 6,...]
    pallas_call x1, Pallas kernels: 22.1 us -> 18 us  [attend(): pl.pallas_call(body, in_specs=[pl.BlockSpec(memory_space=pltpu.SMEM), who...]
    ppermute x21, waiting for transfers between devices: 20.5 us -> 23 us  [swapped(): return lax.ppermute(x, axis, [(i, i ^ mask) for i in range(count)])]
    pallas_call x1, Pallas kernels: 2.9 us -> 0.48 us  [mix(): pl.pallas_call(body, in_specs=[whole] * (len(parts) + 2), out_specs=[whol...]
    add x2 -> x0, other arithmetic: 2.12 us -> none  [shards(): both = keep + swapped(send, 'tp', 1)]
    ppermute x1, waiting for transfers between devices: 0.01 us -> 1.85 us  [shards(): queries = queries + [lax.ppermute(queries[0], 'seq', [(3, 0), (2, 1)])]]
    dot_general x1 -> x0, matrix products: 1.69 us -> none  [shards(): lax.dot_general(member, token_cols, (((0,), (0,)), ((), ())), preferred_e...]
    squeeze x2 -> x0, local copies, waits for them, and re-layouts: 1.35 us -> none  [shards(): both[m]]
  transfers between devices with their start and end apart: 22 -> 22, of which waited for: 11 -> 9; matrix products, arithmetic and copies ran while one was open for 5% -> 1% of each run, Pallas kernels for 16% -> 9%
where the time goes in v3:
time: 91.6 us; the launch traced here: 91.3 us
  Pallas kernels  38.3 us (42%)
  waiting for transfers between devices  24.8 us (27%)
  starting transfers between devices  22.9 us (25%)
  local copies, waits for them, and re-layouts  3.41 us (4%)
  between operations  1 us (1%)
  other arithmetic  0.93 us (1%)
    ppermute x21, waiting for transfers between devices, swapped(): return lax.ppermute(x, axis, [(i, i ^ mask) for i in range(count)])  23 us
    ppermute x21, starting transfers between devices, swapped(): return lax.ppermute(x, axis, [(i, i ^ mask) for i in range(count)])  21.4 us
    pallas_call x1, Pallas kernels, attend(): pl.pallas_call(body, in_specs=[pl.BlockSpec(memory_space=pltpu.SMEM), who...  18 us
    pallas_call x1, Pallas kernels, project_kv(): pl.pallas_call(body, in_specs=[pl.BlockSpec(memory_space=pltpu.HBM)] * 6,...  7.14 us
    pallas_call x1, Pallas kernels, widen_centroids(): pl.pallas_call(body, in_specs=[scalar, scalar, whole, in_hbm], out_specs=...  5.47 us
    unnamed x16, local copies, waits for them, and re-layouts  3.41 us
    pallas_call x1, Pallas kernels, project_q(): pl.pallas_call(q_body, in_specs=[whole] * 3, out_specs=[whole, whole], ou...  2.86 us
    pallas_call x1, Pallas kernels, finish(): pl.pallas_call(body, in_specs=[scalar] + [whole] * (groups + 5) + [in_hbm...  2.66 us
  transfers between devices with their start and end apart: 22, of which 9 were waited for; matrix products, arithmetic and copies ran while one was open for 1% of the time, Pallas kernels for 9%

profile of v3, /device:TPU:0, one launch (start us, length us, event | category | flops | bytes accessed | tf_op | source)
XLA Modules:
  0.0 91.3 jit_solution(11656471331484293627)
XLA Ops:
  0.6 0.0 copy-start.3
  0.6 7.1 %project_kv.1 = (bf16[1024,128]{1,0:T(8,128)(2,1)S(1)}, f32[32,512]{1,0:T(8,128)S(1)}, f32[2,1024,128]{2,1,0:T(8,128)S(1)}) custom-call(s32[32,128]{1,0:T(8,128)} %bitcast.11, bf16[64,4096]{1,0:T(8,128)(2,1)} %bitcast.14, bf16[64,4096]{1,0:T(8,128)(2,1)} %bitcast.15, f32[2,128,128]{2,1,0:T(8,128)} %constant.41.clone.refs_3_, ...), custom_call_target="tpu_custom_call" | custom-call | tf_op jit(solution)/shard_map/project_kv/pallas_call | solution.py:143
  7.8 0.0 copy-start.4
  7.8 4.0 %collective-permute-start.3 = (f32[32,512]{1,0:T(8,128)S(1)}, f32[32,512]{1,0:T(8,128)S(1)}, u32[]{:S(2)}, u32[]{:S(2)}) collective-permute-start(f32[32,512]{1,0:T(8,128)S(1)} %get-tuple-element.60.refs_13_), channel_id=1, source_target_pairs={{0,24},{8,16},{16,8},{24,0},{1,25},{9,17},{17,9},{25,1},{2,26},{10... | collective-permute-start | bytes 196616 | tf_op jit(solution)/shard_map/ppermute | solution.py:32
  11.8 0.5 collective-permute-start.2
  12.3 1.5 %collective-permute-start.6 = (bf16[1024,128]{1,0:T(8,128)(2,1)S(1)}, bf16[1024,128]{1,0:T(8,128)(2,1)}, u32[]{:S(2)}, u32[]{:S(2)}) collective-permute-start(bf16[1024,128]{1,0:T(8,128)(2,1)S(1)} %get-tuple-element.59.refs_5_), channel_id=1, source_target_pairs={{0,24},{8,16},{16,8},{24,0},{1,25},{9,17},{17,9},{25,1},{2,26},{10... | collective-permute-start | bytes 786440 | tf_op jit(solution)/shard_map/ppermute | solution.py:32
  13.8 0.1 collective-permute-start.5
  13.9 1.9 %collective-permute-start.4 = (bf16[1024,128]{1,0:T(8,128)(2,1)S(1)}, bf16[1024,128]{1,0:T(8,128)(2,1)}, u32[]{:S(2)}, u32[]{:S(2)}) collective-permute-start(bf16[1024,128]{1,0:T(8,128)(2,1)S(1)} %get-tuple-element.59.refs_5_), channel_id=1, source_target_pairs={{0,8},{8,0},{16,24},{24,16},{1,9},{9,1},{17,25},{25,17},{2,10},{10... | collective-permute-start | bytes 786440 | tf_op jit(solution)/shard_map/ppermute | solution.py:32
  15.8 0.7 multiply_bitcast_fusion
  16.5 0.0 copy-done.3
  16.5 0.0 copy-start
  16.5 3.4 %copy-done = bf16[1024,4096]{1,0:T(8,128)(2,1)S(1)} copy-done((bf16[1024,4096]{1,0:T(8,128)(2,1)S(1)}, bf16[1024,4096]{1,0:T(8,128)(2,1)}, u32[]{:S(2)}) %copy-start) | copy-done | bytes 8388632
  19.9 2.9 %project_q.1 = (bf16[512,256]{1,0:T(8,128)(2,1)S(1)}, bf16[512,256]{1,0:T(8,128)(2,1)S(1)}) custom-call(bf16[1024,4096]{1,0:T(8,128)(2,1)S(1)} %copy-done, bf16[4096,256]{1,0:T(8,128)(2,1)S(1)} %copy-done.3, f32[2,1024,128]{2,1,0:T(8,128)S(1)} %get-tuple-element.45.tables), custom_call_target="tpu_custom_call" | custom-call | tf_op jit(solution)/shard_map/project_q/pallas_call | solution.py:197
  22.8 0.0 collective-permute-done.3.refs_16_
  22.8 0.2 collective-permute-start.1
  23.0 0.2 fusion.1
  23.1 0.0 collective-permute-done.2.refs_15_
  23.2 0.1 collective-permute-start.7
  23.2 4.6 %collective-permute-done.1.refs_14_ = f32[32,512]{1,0:T(8,128)S(1)} collective-permute-done((f32[32,512]{1,0:T(8,128)S(1)}, f32[32,512]{1,0:T(8,128)S(1)}, u32[]{:S(2)}, u32[]{:S(2)}) %collective-permute-start.1) | collective-permute-done | bytes 65568 | tf_op jit(solution)/shard_map/ppermute | solution.py:32
  27.8 1.5 %collective-permute-start = (bf16[512,256]{1,0:T(8,128)(2,1)S(1)}, bf16[512,256]{1,0:T(8,128)(2,1)S(1)}, u32[]{:S(2)}, u32[]{:S(2)}) collective-permute-start(bf16[512,256]{1,0:T(8,128)(2,1)S(1)} %get-tuple-element.56.refs_2_), channel_id=1, source_target_pairs={{24,0},{16,8},{25,1},{17,9},{26,2},{18,10},{27,3},{19,11},{28,4},{... | collective-permute-start | bytes 786440 | tf_op jit(solution)/shard_map/ppermute | solution.py:787
  29.3 0.0 collective-permute-done.6.refs_8_
  29.3 0.1 collective-permute-start.10
  29.4 0.0 collective-permute-done.5.refs_7_
  29.4 0.5 collective-permute-start.9
  29.9 0.0 collective-permute-done.4.refs_6_
  29.9 0.1 collective-permute-start.8
  29.9 0.0 copy-done.7
  30.0 0.0 copy-done.6
  30.0 0.0 copy-done.5
  30.0 5.5 %widen_centroids.1 = (f32[4096,512]{1,0:T(8,128)}, f32[8,512]{1,0:T(8,128)S(1)}, bf16[512,512]{1,0:T(8,128)(2,1)S(1)}, f32[1,512]{1,0:T(1,128)S(1)}, f32[64,32]{...) custom-call(s32[4,32]{1,0:T(4,128)S(1)} %pad_add_fusion.refs_0_, s32[8]{0:T(128)S(1)} %copy-done.6, ...), custom_call_target="tpu_custom_call" | custom-call | tf_op jit(solution)/shard_map/widen_centroids/pallas_call | solution.py:280
  35.5 1.9 %collective-permute-done.refs_4_ = bf16[512,256]{1,0:T(8,128)(2,1)S(1)} collective-permute-done((bf16[512,256]{1,0:T(8,128)(2,1)S(1)}, bf16[512,256]{1,0:T(8,128)(2,1)S(1)}, u32[]{:S(2)}, u32[]{:S(2)}) %collective-permute-start) | collective-permute-done | bytes 262176 | tf_op jit(solution)/shard_map/ppermute | solution.py:787
  37.3 0.0 collective-permute-done.7.refs_9_
  37.3 0.0 collective-permute-done.10.refs_12_
  37.3 0.0 collective-permute-done.9.refs_11_
  37.3 0.0 collective-permute-done.8.refs_10_
  37.3 0.0 copy-done.4
  37.4 18.0 %attend.1 = (f32[32,256]{1,0:T(8,128)S(1)}, f32[32,128]{1,0:T(8,128)S(1)}, f32[32,512]{1,0:T(8,128)S(1)}) custom-call(s32[4096]{0:T(1024)S(1)} %copy-done.4, s32[32,128]{1,0:T(8,128)S(1)} %bitcast.12, bf16[512,256]{1,0:T(8,128)(2,1)S(1)} %get-tuple-element.56.refs_2_, bf16[512,256]{1,0:T(8,128)(2,1)S(1)} %get-tuple-element.57.refs_3_, ...), custom_call_target="tpu_custom_call" | custom-call | tf_op jit(solution)/shard_map/attend/pallas_call | solution.py:498
  55.3 0.1 collective-permute-start.13
  55.4 2.1 %collective-permute-start.12 = (f32[32,256]{1,0:T(8,128)S(1)}, f32[32,256]{1,0:T(8,128)S(1)}, u32[]{:S(2)}, u32[]{:S(2)}) collective-permute-start(f32[32,256]{1,0:T(8,128)S(1)} %get-tuple-element.64.refs_0_), channel_id=1, source_target_pairs={{0,16},{8,24},{16,0},{24,8},{1,17},{9,25},{17,1},{25,9},{2,18},{10... | collective-permute-start | bytes 98312 | tf_op jit(solution)/shard_map/ppermute | solution.py:32
  57.5 1.4 %collective-permute-start.11 = (f32[32,256]{1,0:T(8,128)S(1)}, f32[32,256]{1,0:T(8,128)S(1)}, u32[]{:S(2)}, u32[]{:S(2)}) collective-permute-start(f32[32,256]{1,0:T(8,128)S(1)} %get-tuple-element.64.refs_0_), channel_id=1, source_target_pairs={{0,8},{8,0},{16,24},{24,16},{1,9},{9,1},{17,25},{25,17},{2,10},{10... | collective-permute-start | bytes 98312 | tf_op jit(solution)/shard_map/ppermute | solution.py:32
  58.9 1.3 %collective-permute-done.13.refs_3_ = f32[32,256]{1,0:T(8,128)S(1)} collective-permute-done((f32[32,256]{1,0:T(8,128)S(1)}, f32[32,256]{1,0:T(8,128)S(1)}, u32[]{:S(2)}, u32[]{:S(2)}) %collective-permute-start.13) | collective-permute-done | bytes 32800 | tf_op jit(solution)/shard_map/ppermute | solution.py:32
  60.2 0.0 collective-permute-done.12.refs_2_
  60.2 1.2 %collective-permute-done.11.refs_1_ = f32[32,256]{1,0:T(8,128)S(1)} collective-permute-done((f32[32,256]{1,0:T(8,128)S(1)}, f32[32,256]{1,0:T(8,128)S(1)}, u32[]{:S(2)}, u32[]{:S(2)}) %collective-permute-start.11) | collective-permute-done | bytes 32800 | tf_op jit(solution)/shard_map/ppermute | solution.py:32
  61.4 0.5 mix.1
  61.9 0.0 collective-permute-start.14
  61.9 1.6 %collective-permute-done.14.refs_1_ = f32[4,40,512]{2,1,0:T(8,128)S(1)} collective-permute-done((f32[4,40,512]{2,1,0:T(8,128)S(1)}, f32[4,40,512]{2,1,0:T(8,128)S(1)}, u32[]{:S(2)}, u32[]{:S(2)}) %collective-permute-start.14) | collective-permute-done | bytes 327712 | tf_op jit(solution)/shard_map/ppermute | solution.py:32
  63.6 1.6 %collective-permute-start.15 = (f32[40,512]{1,0:T(8,128)S(1)}, f32[40,512]{1,0:T(8,128)S(1)}, u32[]{:S(2)}, u32[]{:S(2)}) collective-permute-start(f32[40,512]{1,0:T(8,128)S(1)} %get-tuple-element.69), channel_id=1, source_target_pairs={{0,2},{1,3},{2,0},{3,1},{4,6},{5,7},{6,4},{7,5},{8,10},{9,11},{10,... | collective-permute-start | bytes 245768 | tf_op jit(solution)/shard_map/ppermute | solution.py:32
  65.2 2.7 %collective-permute-start.16 = (f32[40,512]{1,0:T(8,128)S(1)}, f32[40,512]{1,0:T(8,128)S(1)}, u32[]{:S(2)}, u32[]{:S(2)}) collective-permute-start(f32[40,512]{1,0:T(8,128)S(1)} %get-tuple-element.70), channel_id=1, source_target_pairs={{0,4},{1,5},{2,6},{3,7},{4,0},{5,1},{6,2},{7,3},{8,12},{9,13},{10,... | collective-permute-start | bytes 245768 | tf_op jit(solution)/shard_map/ppermute | solution.py:32
  67.9 0.1 collective-permute-start.17
  68.0 0.1 collective-permute-done.15.refs_1_
  68.1 6.5 %collective-permute-done.16.refs_2_ = f32[40,512]{1,0:T(8,128)S(1)} collective-permute-done((f32[40,512]{1,0:T(8,128)S(1)}, f32[40,512]{1,0:T(8,128)S(1)}, u32[]{:S(2)}, u32[]{:S(2)}) %collective-permute-start.16) | collective-permute-done | bytes 81952 | tf_op jit(solution)/shard_map/ppermute | solution.py:32
  74.7 0.0 collective-permute-done.17.refs_3_
  74.7 0.0 copy-done.1
  74.7 1.6 %cross.1 = (f32[4,8,4224]{2,1,0:T(8,128)S(1)}, f32[4,8,4224]{2,1,0:T(8,128)S(1)}, f32[32,512]{1,0:T(8,128)S(1)}, f32[8,512]{1,0:T(8,128)S(1)}) custom-call(f32[40,512]{1,0:T(8,128)S(1)} %get-tuple-element.68.refs_0_, f32[40,512]{1,0:T(8,128)S(1)} %collective-permute-done.15.refs_1_, f32[40,512]{1,0:T(8,128)S(1)} %collective-permute-done.16.refs_2_, ...), custom_call_target="tpu_custom_call" | custom-call | tf_op jit(solution)/shard_map/cross/pallas_call | solution.py:659
  76.3 0.1 collective-permute-start.18
  76.3 1.9 %collective-permute-done.18.refs_1_ = f32[4,8,4224]{2,1,0:T(8,128)S(1)} collective-permute-done((f32[4,8,4224]{2,1,0:T(8,128)S(1)}, f32[4,8,4224]{2,1,0:T(8,128)S(1)}, u32[]{:S(2)}, u32[]{:S(2)}) %collective-permute-start.18) | collective-permute-done | bytes 540704 | tf_op jit(solution)/shard_map/ppermute | solution.py:32
  78.3 0.1 fold.3
  78.4 1.6 %collective-permute-start.19 = (bf16[8,4352]{1,0:T(8,128)(2,1)S(1)}, bf16[8,4352]{1,0:T(8,128)(2,1)S(1)}, u32[]{:S(2)}, u32[]{:S(2)}) collective-permute-start(bf16[8,4352]{1,0:T(8,128)(2,1)S(1)} %get-tuple-element.79), channel_id=1, source_target_pairs={{0,2},{1,3},{2,0},{3,1},{4,6},{5,7},{6,4},{7,5},{8,10},{9,11},{10,... | collective-permute-start | bytes 208904 | tf_op jit(solution)/shard_map/ppermute | solution.py:32
  80.0 1.5 %collective-permute-start.20 = (bf16[8,4352]{1,0:T(8,128)(2,1)S(1)}, bf16[8,4352]{1,0:T(8,128)(2,1)S(1)}, u32[]{:S(2)}, u32[]{:S(2)}) collective-permute-start(bf16[8,4352]{1,0:T(8,128)(2,1)S(1)} %get-tuple-element.80), channel_id=1, source_target_pairs={{0,4},{1,5},{2,6},{3,7},{4,0},{5,1},{6,2},{7,3},{8,12},{9,13},{10,... | collective-permute-start | bytes 208904 | tf_op jit(solution)/shard_map/ppermute | solution.py:32
  81.5 1.3 %collective-permute-start.21 = (bf16[8,4352]{1,0:T(8,128)(2,1)S(1)}, bf16[8,4352]{1,0:T(8,128)(2,1)S(1)}, u32[]{:S(2)}, u32[]{:S(2)}) collective-permute-start(bf16[8,4352]{1,0:T(8,128)(2,1)S(1)} %get-tuple-element.81), channel_id=1, source_target_pairs={{0,6},{1,7},{2,4},{3,5},{4,2},{5,3},{6,0},{7,1},{8,14},{9,15},{10,... | collective-permute-start | bytes 208904 | tf_op jit(solution)/shard_map/ppermute | solution.py:32
  82.8 0.0 collective-permute-done.19.refs_2_
  82.8 5.7 %collective-permute-done.20.refs_3_ = bf16[8,4352]{1,0:T(8,128)(2,1)S(1)} collective-permute-done((bf16[8,4352]{1,0:T(8,128)(2,1)S(1)}, bf16[8,4352]{1,0:T(8,128)(2,1)S(1)}, u32[]{:S(2)}, u32[]{:S(2)}) %collective-permute-start.20) | collective-permute-done | bytes 69664 | tf_op jit(solution)/shard_map/ppermute | solution.py:32
  88.5 0.0 collective-permute-done.21.refs_4_
  88.5 2.7 %finish.1 = (f32[8,4096]{1,0:T(8,128)}, f32[4096,512]{1,0:T(8,128)}) custom-call(s32[4,32]{1,0:T(4,128)S(1)} %pad_add_fusion.refs_0_, f32[8,4224]{1,0:T(8,128)S(1)} %get-tuple-element.78.refs_1_, bf16[8,4352]{1,0:T(8,128)(2,1)S(1)} %collective-permute-done.19.refs_2_, ...), custom_call_target="tpu_custom_call", output_to_operand_aliasing={{1}: (10, {})} | custom-call | tf_op jit(solution)/shard_map/finish/pallas_call | solution.py:740
  (9 shorter events, 0.1 us)
Async XLA Ops:
  0.6 15.9 %copy-start.3 = (bf16[4096,256]{1,0:T(8,128)(2,1)S(1)}, bf16[4096,256]{1,0:T(8,128)(2,1)}, u32[]{:S(2)}) copy-start(bf16[4096,256]{1,0:T(8,128)(2,1)} %weight.1) | copy-start | bytes 6291460
  7.8 29.6 %copy-start.4 = (s32[4096]{0:T(1024)S(1)}, s32[4096]{0:T(1024)}, u32[]{:S(2)}) copy-start(s32[4096]{0:T(1024)} %refs_0_.1) | copy-start | bytes 49156
  7.8 15.0 %collective-permute-start.3 = (f32[32,512]{1,0:T(8,128)S(1)}, f32[32,512]{1,0:T(8,128)S(1)}, u32[]{:S(2)}, u32[]{:S(2)}) collective-permute-start(f32[32,512]{1,0:T(8,128)S(1)} %get-tuple-element.60.refs_13_), channel_id=1, source_target_pairs={{0,24},{8,16},{16,8},{24,0},{1,25},{9,17},{17,9},{25,1},{2,26},{10... | collective-permute-start | bytes 196616 | tf_op jit(solution)/shard_map/ppermute | solution.py:32
  11.8 11.4 %collective-permute-start.2 = (f32[32,512]{1,0:T(8,128)S(1)}, f32[32,512]{1,0:T(8,128)}, u32[]{:S(2)}, u32[]{:S(2)}) collective-permute-start(f32[32,512]{1,0:T(8,128)S(1)} %get-tuple-element.60.refs_13_), channel_id=1, source_target_pairs={{0,16},{8,24},{16,0},{24,8},{1,17},{9,25},{17,1},{25,9},{2,18},{10... | collective-permute-start | bytes 196616 | tf_op jit(solution)/shard_map/ppermute | solution.py:32
  12.3 17.0 %collective-permute-start.6 = (bf16[1024,128]{1,0:T(8,128)(2,1)S(1)}, bf16[1024,128]{1,0:T(8,128)(2,1)}, u32[]{:S(2)}, u32[]{:S(2)}) collective-permute-start(bf16[1024,128]{1,0:T(8,128)(2,1)S(1)} %get-tuple-element.59.refs_5_), channel_id=1, source_target_pairs={{0,24},{8,16},{16,8},{24,0},{1,25},{9,17},{17,9},{25,1},{2,26},{10... | collective-permute-start | bytes 786440 | tf_op jit(solution)/shard_map/ppermute | solution.py:32
  13.8 15.6 %collective-permute-start.5 = (bf16[1024,128]{1,0:T(8,128)(2,1)S(1)}, bf16[1024,128]{1,0:T(8,128)(2,1)}, u32[]{:S(2)}, u32[]{:S(2)}) collective-permute-start(bf16[1024,128]{1,0:T(8,128)(2,1)S(1)} %get-tuple-element.59.refs_5_), channel_id=1, source_target_pairs={{0,16},{8,24},{16,0},{24,8},{1,17},{9,25},{17,1},{25,9},{2,18},{10... | collective-permute-start | bytes 786440 | tf_op jit(solution)/shard_map/ppermute | solution.py:32
  13.9 16.0 %collective-permute-start.4 = (bf16[1024,128]{1,0:T(8,128)(2,1)S(1)}, bf16[1024,128]{1,0:T(8,128)(2,1)}, u32[]{:S(2)}, u32[]{:S(2)}) collective-permute-start(bf16[1024,128]{1,0:T(8,128)(2,1)S(1)} %get-tuple-element.59.refs_5_), channel_id=1, source_target_pairs={{0,8},{8,0},{16,24},{24,16},{1,9},{9,1},{17,25},{25,17},{2,10},{10... | collective-permute-start | bytes 786440 | tf_op jit(solution)/shard_map/ppermute | solution.py:32
  15.8 14.2 %copy-start.7 = (s32[32]{0:T(128)S(1)}, s32[32]{0:T(128)}, u32[]{:S(2)}) copy-start(s32[32]{0:T(128)} %param.21) | copy-start | bytes 388
  15.8 14.2 %copy-start.6 = (s32[8]{0:T(128)S(1)}, s32[8]{0:T(128)}, u32[]{:S(2)}) copy-start(s32[8]{0:T(128)} %refs_1_.1) | copy-start | bytes 100
  16.5 3.4 %copy-start = (bf16[1024,4096]{1,0:T(8,128)(2,1)S(1)}, bf16[1024,4096]{1,0:T(8,128)(2,1)}, u32[]{:S(2)}) copy-start(bf16[1024,4096]{1,0:T(8,128)(2,1)} %tok.1) | copy-start | bytes 25165828
  19.9 10.1 %copy-start.5 = (f32[512]{0:T(512)S(1)}, f32[512]{0:T(512)}, u32[]{:S(2)}) copy-start(f32[512]{0:T(512)} %param.20) | copy-start | bytes 6148
  19.9 41.5 %copy-start.2 = (bf16[256,4096]{1,0:T(8,128)(2,1)S(1)}, bf16[256,4096]{1,0:T(8,128)(2,1)}, u32[]{:S(2)}) copy-start(bf16[256,4096]{1,0:T(8,128)(2,1)} %refs_5_.3) | copy-start | bytes 6291460
  19.9 54.8 %copy-start.1 = (bf16[4096,512]{1,0:T(8,128)(2,1)S(1)}, bf16[4096,512]{1,0:T(8,128)(2,1)}, u32[]{:S(2)}) copy-start(bf16[4096,512]{1,0:T(8,128)(2,1)} %refs_8_.1) | copy-start | bytes 12582916
  22.8 5.0 %collective-permute-start.1 = (f32[32,512]{1,0:T(8,128)S(1)}, f32[32,512]{1,0:T(8,128)S(1)}, u32[]{:S(2)}, u32[]{:S(2)}) collective-permute-start(f32[32,512]{1,0:T(8,128)S(1)} %get-tuple-element.60.refs_13_), channel_id=1, source_target_pairs={{0,8},{8,0},{16,24},{24,16},{1,9},{9,1},{17,25},{25,17},{2,10},{10... | collective-permute-start | bytes 196616 | tf_op jit(solution)/shard_map/ppermute | solution.py:32
  23.2 14.2 %collective-permute-start.7 = (bf16[1024,128]{1,0:T(8,128)(2,1)S(1)}, bf16[1024,128]{1,0:T(8,128)(2,1)S(1)}, u32[]{:S(2)}, u32[]{:S(2)}) collective-permute-start(bf16[1024,128]{1,0:T(8,128)(2,1)S(1)} %get-tuple-element.59.refs_5_), channel_id=1, source_target_pairs={{0,1},{1,0},{2,3},{3,2},{4,5},{5,4},{6,7},{7,6},{8,9},{9,8},{10,11... | collective-permute-start | bytes 786440 | tf_op jit(solution)/shard_map/ppermute | solution.py:32
  27.8 9.5 %collective-permute-start = (bf16[512,256]{1,0:T(8,128)(2,1)S(1)}, bf16[512,256]{1,0:T(8,128)(2,1)S(1)}, u32[]{:S(2)}, u32[]{:S(2)}) collective-permute-start(bf16[512,256]{1,0:T(8,128)(2,1)S(1)} %get-tuple-element.56.refs_2_), channel_id=1, source_target_pairs={{24,0},{16,8},{25,1},{17,9},{26,2},{18,10},{27,3},{19,11},{28,4},{... | collective-permute-start | bytes 786440 | tf_op jit(solution)/shard_map/ppermute | solution.py:787
  29.3 8.1 %collective-permute-start.10 = (bf16[1024,128]{1,0:T(8,128)(2,1)}, bf16[1024,128]{1,0:T(8,128)(2,1)S(1)}, u32[]{:S(2)}, u32[]{:S(2)}) collective-permute-start(bf16[1024,128]{1,0:T(8,128)(2,1)} %collective-permute-done.6.refs_8_), channel_id=1, source_target_pairs={{0,1},{1,0},{2,3},{3,2},{4,5},{5,4},{6,7},{7,6},{8,9},{9,8},{10,11... | collective-permute-start | bytes 786440 | tf_op jit(solution)/shard_map/ppermute | solution.py:32
  29.4 8.0 %collective-permute-start.9 = (bf16[1024,128]{1,0:T(8,128)(2,1)}, bf16[1024,128]{1,0:T(8,128)(2,1)S(1)}, u32[]{:S(2)}, u32[]{:S(2)}) collective-permute-start(bf16[1024,128]{1,0:T(8,128)(2,1)} %collective-permute-done.5.refs_7_), channel_id=1, source_target_pairs={{0,1},{1,0},{2,3},{3,2},{4,5},{5,4},{6,7},{7,6},{8,9},{9,8},{10,11... | collective-permute-start | bytes 786440 | tf_op jit(solution)/shard_map/ppermute | solution.py:32
  29.9 7.5 %collective-permute-start.8 = (bf16[1024,128]{1,0:T(8,128)(2,1)}, bf16[1024,128]{1,0:T(8,128)(2,1)S(1)}, u32[]{:S(2)}, u32[]{:S(2)}) collective-permute-start(bf16[1024,128]{1,0:T(8,128)(2,1)} %collective-permute-done.4.refs_6_), channel_id=1, source_target_pairs={{0,1},{1,0},{2,3},{3,2},{4,5},{5,4},{6,7},{7,6},{8,9},{9,8},{10,11... | collective-permute-start | bytes 786440 | tf_op jit(solution)/shard_map/ppermute | solution.py:32
  55.3 4.9 %collective-permute-start.13 = (f32[32,256]{1,0:T(8,128)S(1)}, f32[32,256]{1,0:T(8,128)S(1)}, u32[]{:S(2)}, u32[]{:S(2)}) collective-permute-start(f32[32,256]{1,0:T(8,128)S(1)} %get-tuple-element.64.refs_0_), channel_id=1, source_target_pairs={{0,24},{8,16},{16,8},{24,0},{1,25},{9,17},{17,9},{25,1},{2,26},{10... | collective-permute-start | bytes 98312 | tf_op jit(solution)/shard_map/ppermute | solution.py:32
  55.4 4.8 %collective-permute-start.12 = (f32[32,256]{1,0:T(8,128)S(1)}, f32[32,256]{1,0:T(8,128)S(1)}, u32[]{:S(2)}, u32[]{:S(2)}) collective-permute-start(f32[32,256]{1,0:T(8,128)S(1)} %get-tuple-element.64.refs_0_), channel_id=1, source_target_pairs={{0,16},{8,24},{16,0},{24,8},{1,17},{9,25},{17,1},{25,9},{2,18},{10... | collective-permute-start | bytes 98312 | tf_op jit(solution)/shard_map/ppermute | solution.py:32
  57.5 3.9 %collective-permute-start.11 = (f32[32,256]{1,0:T(8,128)S(1)}, f32[32,256]{1,0:T(8,128)S(1)}, u32[]{:S(2)}, u32[]{:S(2)}) collective-permute-start(f32[32,256]{1,0:T(8,128)S(1)} %get-tuple-element.64.refs_0_), channel_id=1, source_target_pairs={{0,8},{8,0},{16,24},{24,16},{1,9},{9,1},{17,25},{25,17},{2,10},{10... | collective-permute-start | bytes 98312 | tf_op jit(solution)/shard_map/ppermute | solution.py:32
  61.9 1.7 %collective-permute-start.14 = (f32[4,40,512]{2,1,0:T(8,128)S(1)}, f32[4,40,512]{2,1,0:T(8,128)S(1)}, u32[]{:S(2)}, u32[]{:S(2)}) collective-permute-start(f32[4,40,512]{2,1,0:T(8,128)S(1)} %get-tuple-element.67), channel_id=1, source_target_pairs={{0,1},{1,0},{2,3},{3,2},{4,5},{5,4},{6,7},{7,6},{8,9},{9,8},{10,11... | collective-permute-start | bytes 983048 | tf_op jit(solution)/shard_map/ppermute | solution.py:32
  63.6 4.6 %collective-permute-start.15 = (f32[40,512]{1,0:T(8,128)S(1)}, f32[40,512]{1,0:T(8,128)S(1)}, u32[]{:S(2)}, u32[]{:S(2)}) collective-permute-start(f32[40,512]{1,0:T(8,128)S(1)} %get-tuple-element.69), channel_id=1, source_target_pairs={{0,2},{1,3},{2,0},{3,1},{4,6},{5,7},{6,4},{7,5},{8,10},{9,11},{10,... | collective-permute-start | bytes 245768 | tf_op jit(solution)/shard_map/ppermute | solution.py:32
  65.2 9.5 %collective-permute-start.16 = (f32[40,512]{1,0:T(8,128)S(1)}, f32[40,512]{1,0:T(8,128)S(1)}, u32[]{:S(2)}, u32[]{:S(2)}) collective-permute-start(f32[40,512]{1,0:T(8,128)S(1)} %get-tuple-element.70), channel_id=1, source_target_pairs={{0,4},{1,5},{2,6},{3,7},{4,0},{5,1},{6,2},{7,3},{8,12},{9,13},{10,... | collective-permute-start | bytes 245768 | tf_op jit(solution)/shard_map/ppermute | solution.py:32
  67.9 6.8 %collective-permute-start.17 = (f32[40,512]{1,0:T(8,128)S(1)}, f32[40,512]{1,0:T(8,128)S(1)}, u32[]{:S(2)}, u32[]{:S(2)}) collective-permute-start(f32[40,512]{1,0:T(8,128)S(1)} %get-tuple-element.71), channel_id=1, source_target_pairs={{0,6},{1,7},{2,4},{3,5},{4,2},{5,3},{6,0},{7,1},{8,14},{9,15},{10,... | collective-permute-start | bytes 245768 | tf_op jit(solution)/shard_map/ppermute | solution.py:32
  76.3 2.0 %collective-permute-start.18 = (f32[4,8,4224]{2,1,0:T(8,128)S(1)}, f32[4,8,4224]{2,1,0:T(8,128)S(1)}, u32[]{:S(2)}, u32[]{:S(2)}) collective-permute-start(f32[4,8,4224]{2,1,0:T(8,128)S(1)} %get-tuple-element.77), channel_id=1, source_target_pairs={{0,1},{1,0},{2,3},{3,2},{4,5},{5,4},{6,7},{7,6},{8,9},{9,8},{10,11... | collective-permute-start | bytes 1622024 | tf_op jit(solution)/shard_map/ppermute | solution.py:32
  78.4 4.5 %collective-permute-start.19 = (bf16[8,4352]{1,0:T(8,128)(2,1)S(1)}, bf16[8,4352]{1,0:T(8,128)(2,1)S(1)}, u32[]{:S(2)}, u32[]{:S(2)}) collective-permute-start(bf16[8,4352]{1,0:T(8,128)(2,1)S(1)} %get-tuple-element.79), channel_id=1, source_target_pairs={{0,2},{1,3},{2,0},{3,1},{4,6},{5,7},{6,4},{7,5},{8,10},{9,11},{10,... | collective-permute-start | bytes 208904 | tf_op jit(solution)/shard_map/ppermute | solution.py:32
  80.0 8.5 %collective-permute-start.20 = (bf16[8,4352]{1,0:T(8,128)(2,1)S(1)}, bf16[8,4352]{1,0:T(8,128)(2,1)S(1)}, u32[]{:S(2)}, u32[]{:S(2)}) collective-permute-start(bf16[8,4352]{1,0:T(8,128)(2,1)S(1)} %get-tuple-element.80), channel_id=1, source_target_pairs={{0,4},{1,5},{2,6},{3,7},{4,0},{5,1},{6,2},{7,3},{8,12},{9,13},{10,... | collective-permute-start | bytes 208904 | tf_op jit(solution)/shard_map/ppermute | solution.py:32
  81.5 7.0 %collective-permute-start.21 = (bf16[8,4352]{1,0:T(8,128)(2,1)S(1)}, bf16[8,4352]{1,0:T(8,128)(2,1)S(1)}, u32[]{:S(2)}, u32[]{:S(2)}) collective-permute-start(bf16[8,4352]{1,0:T(8,128)(2,1)S(1)} %get-tuple-element.81), channel_id=1, source_target_pairs={{0,6},{1,7},{2,4},{3,5},{4,2},{5,3},{6,0},{7,1},{8,14},{9,15},{10,... | collective-permute-start | bytes 208904 | tf_op jit(solution)/shard_map/ppermute | solution.py:32

commit v4 on v3

--- a/solution.py
+++ b/solution.py
@@ -76,7 +76,7 @@
 
 def kv_body(chunks, seg_total, *refs):
     ids_in, wk_in, wv_in, fine_in, coarse_in, tok_in = refs[:6]
-    out, pooled, tables, tok, key_tables, weight, ids, fine, coarse, acc, small, sems = refs[6:]
+    out, tables, tok, key_tables, weight, ids, fine, coarse, acc, small, sems = refs[6:]
     rows, width = tok.shape
     half = wk_in.shape[0]
     subs = rows // LANES
@@ -126,10 +126,17 @@
         x = acc[at]
         x = x * key_tables[0, at, :] + pair_swap(x, even) * key_tables[1, at, :]
         out[at, :] = x.astype(bf16)
-    feat = pooled.shape[1]
+    feat = (out.shape[0] - rows) // 2 // seg_total * LANES
     cols = pl.ds(pl.multiple_of(lax.axis_index("tp") * feat, feat), feat)
     member = jnp.concatenate(members, 1).astype(bf16)
-    pooled[...] = jnp.dot(member, tok[:, cols], preferred_element_type=f32)
+    pooled = jnp.dot(member, tok[:, cols], preferred_element_type=f32)
+    high = pooled.astype(bf16)
+    low = (pooled - high.astype(f32)).astype(bf16)
+    row = rows
+    for part in (high, low):
+        for g in range(feat // LANES):
+            out[row : row + seg_total, :] = part[:, g * LANES : (g + 1) * LANES]
+            row = row + seg_total
 
 
 def project_kv(tokens, w_key, w_value, fine, coarse, ids, seg_total, feat):
@@ -143,10 +150,9 @@
     return pl.pallas_call(
         body,
         in_specs=[pl.BlockSpec(memory_space=pltpu.HBM)] * 6,
-        out_specs=[whole] * 3,
+        out_specs=[whole] * 2,
         out_shape=[
-            jax.ShapeDtypeStruct((rows, 2 * half), bf16),
-            jax.ShapeDtypeStruct((seg_total, feat), f32),
+            jax.ShapeDtypeStruct((rows + 2 * seg_total * feat // LANES, 2 * half), bf16),
             jax.ShapeDtypeStruct((2, rows, LANES), f32),
         ],
         scratch_shapes=[
@@ -161,6 +167,7 @@
             pltpu.SemaphoreType.DMA((TOKEN_CHUNKS,)),
         ],
         compiler_params=pltpu.CompilerParams(vmem_limit_bytes=20 * MIB),
+        cost_estimate=pl.CostEstimate(flops=2 * rows * width * 2 * half, bytes_accessed=2 * rows * width, transcendentals=0),
         name="project_kv",
     )(*[far(x) for x in (ids, w_key.T, w_value.T, fine, coarse, tokens)])
 
@@ -190,7 +197,7 @@
 
 
 def project_q(tokens, w_query, tables):
-    rows = tokens.shape[0]
+    rows, width = tokens.shape
     cols = w_query.shape[1]
     whole = pl.BlockSpec(memory_space=pltpu.VMEM)
     out = jax.ShapeDtypeStruct((rows // 2, cols), bf16)
@@ -201,6 +208,7 @@
         out_shape=[out, out],
         scratch_shapes=[pltpu.VMEM((rows, cols), f32)],
         compiler_params=pltpu.CompilerParams(vmem_limit_bytes=20 * MIB),
+        cost_estimate=pl.CostEstimate(flops=2 * rows * width * cols, bytes_accessed=2 * rows * width + 2 * width * cols, transcendentals=0),
         name="project_q",
     )(near(tokens), near(w_query), near(tables))
 
@@ -297,6 +305,7 @@
             pltpu.SemaphoreType.DMA((chunks,)),
         ],
         compiler_params=pltpu.CompilerParams(vmem_limit_bytes=24 * MIB),
+        cost_estimate=pl.CostEstimate(flops=4 * rows * feat, bytes_accessed=6 * rows * feat, transcendentals=0),
         name="widen_centroids",
     )(place, owner_counts, gain, far(centroids))
 
@@ -327,12 +336,11 @@
     refs = refs[len(queries) :]
     own_in = refs[:pieces]
     other_in = refs[pieces : 2 * pieces]
-    token_sums = refs[2 * pieces : 3 * pieces]
-    out, counts, tokens_out, q_all, kv, starts, weights, tops, col, lhs, sems = refs[
-        3 * pieces :
+    out, counts, tokens_out, tails, q_all, kv, starts, weights, tops, col, lhs, sems = refs[
+        2 * pieces :
     ]
     q_rows, q_cols = queries[0].shape
-    rows = own_in[0].shape[0]
+    rows = own_in[0].shape[0] - tails.shape[1]
     heads = q_cols // HD
     half = HD // 2
     seq_len = kv.shape[0]
@@ -349,7 +357,11 @@
         for m in range(pieces):
             row0 = pl.multiple_of((rank ^ m) * rows, rows)
             place = kv.at[pl.ds(row0, rows), pl.ds(k * HD, HD)]
-            copies.append(pltpu.make_async_copy(sources[m], place, sems.at[len(copies)]))
+            source = sources[m].at[pl.ds(0, rows), :]
+            copies.append(pltpu.make_async_copy(source, place, sems.at[len(copies)]))
+    for m in range(pieces):
+        source = own_in[m].at[pl.ds(rows, tails.shape[1]), :]
+        copies.append(pltpu.make_async_copy(source, tails.at[m], sems.at[len(copies)]))
     for c in copies:
         c.start()
     col[...] = jnp.zeros(col.shape, f32)
@@ -469,10 +481,13 @@
             lhs[h * seg_total : (h + 1) * seg_total, at] = high
             rest = (w - high.astype(f32)).astype(bf16)
             lhs[(heads + h) * seg_total : (heads + h + 1) * seg_total, at] = rest
-    sums = token_sums[0][...]
-    for t in token_sums[1:]:
-        sums = sums + t[...]
-    tokens_out[...] = sums
+    parts = tokens_out.shape[1] // LANES
+    for g in range(parts):
+        sums = jnp.zeros((seg_total, LANES), f32)
+        for m in range(pieces):
+            for first in (g * seg_total, (parts + g) * seg_total):
+                sums = sums + tails[m, first : first + seg_total, :].astype(f32)
+        tokens_out[:, g * LANES : (g + 1) * LANES] = sums
     counts[...] = jnp.broadcast_to(jnp.sum(number, axis=1, keepdims=True), counts.shape)
     pooled = jnp.dot(lhs[...], kv[...], preferred_element_type=f32)
     pooled = jnp.concatenate([pooled[:, half:HD], pooled[:, HD + half :]], 1)
@@ -482,9 +497,9 @@
         out[:, h * HD : (h + 1) * HD] = jnp.where(upper, pltpu.roll(x, half, 1), x)
 
 
-def attend(seg_ids, ids, queries, own, other, token_sums, seg_total, balanced):
+def attend(seg_ids, ids, queries, own, other, feat, seg_total, balanced):
     q_rows, cols = queries[0].shape
-    rows = own[0].shape[0]
+    tail = 2 * seg_total * feat // LANES
     seq_len = seg_ids.shape[0]
     pieces = len(own)
     heads = cols // HD
@@ -498,15 +513,15 @@
     return pl.pallas_call(
         body,
         in_specs=[pl.BlockSpec(memory_space=pltpu.SMEM), whole]
-        + [anywhere] * inputs
-        + [whole] * pieces,
+        + [anywhere] * inputs,
         out_specs=[whole, whole, whole],
         out_shape=[
             jax.ShapeDtypeStruct((seg_total, cols), f32),
             jax.ShapeDtypeStruct((seg_total, LANES), f32),
-            jax.ShapeDtypeStruct(token_sums[0].shape, f32),
+            jax.ShapeDtypeStruct((seg_total, feat), f32),
         ],
         scratch_shapes=[
+            pltpu.VMEM((pieces, tail, HD), bf16),
             pltpu.VMEM((len(queries) * q_rows, cols), bf16),
             pltpu.VMEM((seq_len, 2 * HD), bf16),
             pltpu.VMEM((seq_len // LANES, LANES), i32),
@@ -514,11 +529,12 @@
             pltpu.VMEM((max(8, seq_len // KB), heads * QB), f32),
             pltpu.VMEM((16, seq_len) if COLUMNS_AS_ROWS else (seq_len, LANES), f32),
             pltpu.VMEM((2 * heads * seg_total, seq_len), bf16),
-            pltpu.SemaphoreType.DMA((inputs,)),
+            pltpu.SemaphoreType.DMA((inputs + pieces,)),
         ],
         compiler_params=pltpu.CompilerParams(vmem_limit_bytes=24 * MIB),
+        cost_estimate=pl.CostEstimate(flops=8 * q_rows * cols * seq_len, bytes_accessed=4 * seq_len * HD, transcendentals=0),
         name="attend",
-    )(seg_ids, ids, *queries, *own, *other, *token_sums)
+    )(seg_ids, ids, *queries, *own, *other)
 
 
 def mix_body(pieces, *refs):
@@ -560,35 +576,41 @@
     )(*parts, norms, w_out)
 
 
-def fold_body(groups, keep, received, own, *sends):
-    rows = keep.shape[-1]
+def fold_body(groups, edge, keep, received, own, *sends):
+    _, rows, cols = keep.shape
     own[...] = keep[0] + received[0]
     for m in range(1, groups):
         total = keep[m] + received[m]
         target = sends[m - 1]
-        if target.dtype == f32:
-            target[...] = total
+        if edge == "rows":
+            inner = rows - 8
+            last = total[inner:]
+            high = last.astype(bf16).astype(f32)
+            target[:inner, :] = total[:inner].astype(bf16)
+            target[inner:, :] = jnp.concatenate([high, last - high], 0).astype(bf16)
         else:
-            last = total[:, rows - LANES :]
+            inner = cols - LANES
+            last = total[:, inner:]
             high = last.astype(bf16)
-            target[:, : rows - LANES] = total[:, : rows - LANES].astype(bf16)
-            target[:, rows - LANES : rows] = high
-            target[:, rows:] = (last - high.astype(f32)).astype(bf16)
-
-
-def fold(keep, received, kind):
+            target[:, :inner] = total[:, :inner].astype(bf16)
+            target[:, inner:cols] = high
+            target[:, cols:] = (last - high.astype(f32)).astype(bf16)
+
+
+def fold(keep, received, edge):
     groups, rows, cols = keep.shape
     whole = pl.BlockSpec(memory_space=pltpu.VMEM)
-    sent = jax.ShapeDtypeStruct((rows, cols if kind == f32 else cols + LANES), kind)
+    shape = (rows + 8, cols) if edge == "rows" else (rows, cols + LANES)
 
     def body(*refs):
-        fold_body(groups, *refs)
+        fold_body(groups, edge, *refs)
 
     result = pl.pallas_call(
         body,
         in_specs=[whole, whole],
         out_specs=[whole] * groups,
-        out_shape=[jax.ShapeDtypeStruct((rows, cols), f32)] + [sent] * (groups - 1),
+        out_shape=[jax.ShapeDtypeStruct((rows, cols), f32)]
+        + [jax.ShapeDtypeStruct(shape, bf16)] * (groups - 1),
         compiler_params=pltpu.CompilerParams(vmem_limit_bytes=12 * MIB),
         name="fold",
     )(keep, received)
@@ -611,11 +633,14 @@
     slots = keep.shape[1]
     per_side = groups * slots
 
-    total = mixed[0][...]
+    total = mixed[0][:seg_total, :] + token_sums[...]
+    square = mixed[0][seg_total:, :]
     for p in mixed[1:]:
-        total = total + p[...]
-    norms[...] = total[seg_total:]
-    pooled = (total[:seg_total] + token_sums[...]) / counts[:, :1]
+        total = total + p[:seg_total, :].astype(f32)
+        terms = p[seg_total:, :].astype(f32)
+        square = square + (terms[:8] + terms[8:])
+    norms[...] = square
+    pooled = total / counts[:, :1]
     square = jnp.sum(pooled * pooled, axis=1, keepdims=True)
     row = lax.broadcasted_iota(i32, (seg_total, LANES), 0)
     lane = lax.broadcasted_iota(i32, (seg_total, LANES), 1)
@@ -775,7 +800,7 @@
     ids = seg_ids.reshape(seq_len // LANES, LANES)
     masks = range(1, seq_total)
 
-    own, pooled, tables = project_kv(
+    own, tables = project_kv(
         tokens, w_key, w_value, fine, coarse, ids, seg_total, model_width // tp_total
     )
     own = [own] + [swapped(own, "seq", m) for m in masks]
@@ -797,23 +822,21 @@
         place, owner_counts, pool_gain.reshape(1, feat), centroids, groups, slots
     )
 
-    pooled_tokens = [pooled] + [swapped(pooled, "seq", m) for m in masks]
-
-    queries, wide, norms, picked, gain, chosen, hit, match, pooled_tokens = lax.optimization_barrier(
-        (queries, wide, norms, picked, gain, chosen, hit, match, pooled_tokens)
+    queries, wide, norms, picked, gain, chosen, hit, match = lax.optimization_barrier(
+        (queries, wide, norms, picked, gain, chosen, hit, match)
     )
     attended, counts, token_sums = attend(
-        seg_ids, ids, queries, own, other, pooled_tokens, seg_total, balanced
+        seg_ids, ids, queries, own, other, feat, seg_total, balanced
     )
     attended = [attended] + [swapped(attended, "seq", m) for m in masks]
 
     keep, send = mix(attended, norms, w_out, feat, groups)
-    mixed = fold(keep, swapped(send, "tp", 1), f32)
+    mixed = fold(keep, swapped(send, "tp", 1), "rows")
 
     keep, send, emb, norms = cross(
         mixed, token_sums, counts, gain, chosen, centroids, slots, model_width
     )
-    terms = fold(keep, swapped(send, "tp", 1), bf16)
+    terms = fold(keep, swapped(send, "tp", 1), "columns")
     distances, updated = finish(
         place, terms, norms, emb, hit, match, picked, wide, model_width
     )

time: 91.6 us -> 87 us (0.950)
  starting transfers between devices: 22.9 us -> 19.1 us
  local copies, waits for them, and re-layouts: 3.41 us -> 1.62 us
  waiting for transfers between devices: 24.8 us -> 25.9 us
    ppermute x21 -> x18, starting transfers between devices: 21.4 us -> 17.7 us  [swapped(): return lax.ppermute(x, axis, [(i, i ^ mask) for i in range(count)])]
    ppermute x21 -> x18, waiting for transfers between devices: 23 us -> 25.8 us  [swapped(): return lax.ppermute(x, axis, [(i, i ^ mask) for i in range(count)])]
    ppermute x1, waiting for transfers between devices: 1.85 us -> 0.01 us  [shards(): queries = queries + [lax.ppermute(queries[0], 'seq', [(3, 0), (2, 1)])]]
    unnamed x16, local copies, waits for them, and re-layouts: 3.41 us -> 1.62 us
  transfers between devices with their start and end apart: 22 -> 19, of which waited for: 9 -> 11; matrix products, arithmetic and copies ran while one was open for 1% -> 0% of each run, Pallas kernels for 9% -> 10%
where the time goes in v4:
time: 87 us; the launch traced here: 86.8 us
  Pallas kernels  39 us (45%)
  waiting for transfers between devices  25.9 us (30%)
  starting transfers between devices  19.1 us (22%)
  local copies, waits for them, and re-layouts  1.62 us (2%)
  between operations  1.02 us (1%)
    ppermute x18, waiting for transfers between devices, swapped(): return lax.ppermute(x, axis, [(i, i ^ mask) for i in range(count)])  25.8 us
    pallas_call x1, Pallas kernels, attend(): pl.pallas_call(body, in_specs=[pl.BlockSpec(memory_space=pltpu.SMEM), who...  18.3 us
    ppermute x18, starting transfers between devices, swapped(): return lax.ppermute(x, axis, [(i, i ^ mask) for i in range(count)])  17.7 us
    pallas_call x1, Pallas kernels, project_kv(): pl.pallas_call(body, in_specs=[pl.BlockSpec(memory_space=pltpu.HBM)] * 6,...  7.53 us
    pallas_call x1, Pallas kernels, widen_centroids(): pl.pallas_call(body, in_specs=[scalar, scalar, whole, in_hbm], out_specs=...  5.47 us
    pallas_call x1, Pallas kernels, project_q(): pl.pallas_call(q_body, in_specs=[whole] * 3, out_specs=[whole, whole], ou...  2.85 us
    pallas_call x1, Pallas kernels, finish(): pl.pallas_call(body, in_specs=[scalar] + [whole] * (groups + 5) + [in_hbm...  2.73 us
  transfers between devices with their start and end apart: 19, of which 11 were waited for; matrix products, arithmetic and copies ran while one was open for 0% of the time, Pallas kernels for 10%

profile of v4, /device:TPU:0, one launch (start us, length us, event | category | flops | bytes accessed | tf_op | source)
XLA Modules:
  0.0 86.8 jit_solution(3240668671275202132)
XLA Ops:
  0.6 0.0 copy-start
  0.6 0.0 copy-start.7
  0.7 0.0 copy-start.5
  0.7 0.0 copy-start.6
  0.7 0.0 copy-start.4
  0.7 7.5 %project_kv.1 = (bf16[1280,128]{1,0:T(8,128)(2,1)S(1)}, f32[2,1024,128]{2,1,0:T(8,128)S(1)}) custom-call(s32[32,128]{1,0:T(8,128)} %bitcast.11, bf16[64,4096]{1,0:T(8,128)(2,1)} %bitcast.14, bf16[64,4096]{1,0:T(8,128)(2,1)} %bitcast.15, f32[2,128,128]{2,1,0:T(8,128)} %constant.41.clone.refs_3_, f32[2,32,128]{2,1,0:T(8,128)} %constant.42.clone.refs_4_, ...), custom_call_target="tpu_custom_call" | custom-call | flops 1073741824 | bytes 8388608 | tf_op jit(solution)/shard_map/project_kv/pallas_call | solution.py:150
  8.2 0.5 collective-permute-start.4
  8.8 3.5 %collective-permute-start.3 = (bf16[1280,128]{1,0:T(8,128)(2,1)S(1)}, bf16[1280,128]{1,0:T(8,128)(2,1)S(1)}, u32[]{:S(2)}, u32[]{:S(2)}) collective-permute-start(bf16[1280,128]{1,0:T(8,128)(2,1)S(1)} %get-tuple-element.53.refs_5_), channel_id=1, source_target_pairs={{0,24},{8,16},{16,8},{24,0},{1,25},{9,17},{17,9},{25,1},{2,26},{10... | collective-permute-start | bytes 983048 | tf_op jit(solution)/shard_map/ppermute | solution.py:32
  12.3 0.5 collective-permute-start.2
  12.8 0.1 collective-permute-start.1
  12.9 0.0 copy-done
  12.9 0.0 copy-start.3
  12.9 1.6 %copy-done.3 = bf16[4096,256]{1,0:T(8,128)(2,1)S(1)} copy-done((bf16[4096,256]{1,0:T(8,128)(2,1)S(1)}, bf16[4096,256]{1,0:T(8,128)(2,1)}, u32[]{:S(2)}) %copy-start.3) | copy-done | bytes 2097176
  14.5 2.8 %project_q.1 = (bf16[512,256]{1,0:T(8,128)(2,1)S(1)}, bf16[512,256]{1,0:T(8,128)(2,1)S(1)}) custom-call(bf16[1024,4096]{1,0:T(8,128)(2,1)S(1)} %copy-done, bf16[4096,256]{1,0:T(8,128)(2,1)S(1)} %copy-done.3, f32[2,1024,128]{2,1,0:T(8,128)S(1)} %get-tuple-element.40.tables), custom_call_target="tpu_custom_call" | custom-call | flops 2147483648 | bytes 10485760 | tf_op jit(solution)/shard_map/project_q/pallas_call | solution.py:204
  17.3 1.5 %collective-permute-start = (bf16[512,256]{1,0:T(8,128)(2,1)S(1)}, bf16[512,256]{1,0:T(8,128)(2,1)S(1)}, u32[]{:S(2)}, u32[]{:S(2)}) collective-permute-start(bf16[512,256]{1,0:T(8,128)(2,1)S(1)} %get-tuple-element.50.refs_2_), channel_id=1, source_target_pairs={{24,0},{16,8},{25,1},{17,9},{26,2},{18,10},{27,3},{19,11},{28,4},{... | collective-permute-start | bytes 786440 | tf_op jit(solution)/shard_map/ppermute | solution.py:812
  18.8 0.0 copy-done.7
  18.9 0.2 fusion.1
  19.0 1.8 %collective-permute-done.3.refs_8_ = bf16[1280,128]{1,0:T(8,128)(2,1)S(1)} collective-permute-done((bf16[1280,128]{1,0:T(8,128)(2,1)S(1)}, bf16[1280,128]{1,0:T(8,128)(2,1)S(1)}, u32[]{:S(2)}, u32[]{:S(2)}) %collective-permute-start.3) | collective-permute-done | bytes 327712 | tf_op jit(solution)/shard_map/ppermute | solution.py:32
  20.9 0.0 collective-permute-start.7
  20.9 6.9 %collective-permute-done.2.refs_7_ = bf16[1280,128]{1,0:T(8,128)(2,1)S(1)} collective-permute-done((bf16[1280,128]{1,0:T(8,128)(2,1)S(1)}, bf16[1280,128]{1,0:T(8,128)(2,1)S(1)}, u32[]{:S(2)}, u32[]{:S(2)}) %collective-permute-start.2) | collective-permute-done | bytes 327712 | tf_op jit(solution)/shard_map/ppermute | solution.py:32
  27.8 0.0 collective-permute-start.6
  27.8 0.1 collective-permute-done.1.refs_6_
  27.9 0.4 collective-permute-start.5
  28.3 0.0 copy-done.5
  28.3 0.0 copy-done.6
  28.4 5.5 %widen_centroids.1 = (f32[4096,512]{1,0:T(8,128)}, f32[8,512]{1,0:T(8,128)S(1)}, bf16[512,512]{1,0:T(8,128)(2,1)S(1)}, f32[1,512]{1,0:T(1,128)S(1)}, f32[64,32]{...) custom-call(s32[4,32]{1,0:T(4,128)S(1)} %pad_add_fusion.refs_0_, s32[8]{0:T(128)S(1)} %copy-done.6, ...), custom_call_target="tpu_custom_call" | custom-call | flops 8388608 | bytes 12582912 | tf_op jit(solution)/shard_map/widen_centroids/pallas_call | solution.py:288
  33.8 0.0 copy-start.2
  33.8 0.0 collective-permute-done.refs_4_
  33.9 0.0 copy-start.1
  33.9 0.0 collective-permute-done.4.refs_9_
  33.9 0.0 collective-permute-done.7.refs_12_
  33.9 0.0 collective-permute-done.6.refs_11_
  33.9 0.0 collective-permute-done.5.refs_10_
  33.9 0.0 copy-done.4
  33.9 18.3 %attend.1 = (f32[32,256]{1,0:T(8,128)S(1)}, f32[32,128]{1,0:T(8,128)S(1)}, f32[32,512]{1,0:T(8,128)S(1)}) custom-call(s32[4096]{0:T(1024)S(1)} %copy-done.4, s32[32,128]{1,0:T(8,128)S(1)} %bitcast.12, bf16[512,256]{1,0:T(8,128)(2,1)S(1)} %get-tuple-element.50.refs_2_, bf16[512,256]{1,0:T(8,128)(2,1)S(1)} %get-tuple-element.51.refs_3_, ...), custom_call_target="tpu_custom_call" | custom-call | flops 4294967296 | bytes 2097152 | tf_op jit(solution)/shard_map/attend/pallas_call | solution.py:513
  52.2 0.1 collective-permute-start.10
  52.3 2.8 %collective-permute-start.9 = (f32[32,256]{1,0:T(8,128)S(1)}, f32[32,256]{1,0:T(8,128)S(1)}, u32[]{:S(2)}, u32[]{:S(2)}) collective-permute-start(f32[32,256]{1,0:T(8,128)S(1)} %get-tuple-element.54.refs_0_), channel_id=1, source_target_pairs={{0,16},{8,24},{16,0},{24,8},{1,17},{9,25},{17,1},{25,9},{2,18},{10... | collective-permute-start | bytes 98312 | tf_op jit(solution)/shard_map/ppermute | solution.py:32
  55.1 0.7 collective-permute-start.8
  55.7 1.5 %collective-permute-done.10.refs_3_ = f32[32,256]{1,0:T(8,128)S(1)} collective-permute-done((f32[32,256]{1,0:T(8,128)S(1)}, f32[32,256]{1,0:T(8,128)S(1)}, u32[]{:S(2)}, u32[]{:S(2)}) %collective-permute-start.10) | collective-permute-done | bytes 32800 | tf_op jit(solution)/shard_map/ppermute | solution.py:32
  57.3 0.0 collective-permute-done.9.refs_2_
  57.3 1.7 %collective-permute-done.8.refs_1_ = f32[32,256]{1,0:T(8,128)S(1)} collective-permute-done((f32[32,256]{1,0:T(8,128)S(1)}, f32[32,256]{1,0:T(8,128)S(1)}, u32[]{:S(2)}, u32[]{:S(2)}) %collective-permute-start.8) | collective-permute-done | bytes 32800 | tf_op jit(solution)/shard_map/ppermute | solution.py:32
  59.0 0.0 copy-done.2
  59.0 0.5 mix.1
  59.5 0.0 collective-permute-start.11
  59.5 1.6 %collective-permute-done.11.refs_1_ = f32[4,40,512]{2,1,0:T(8,128)S(1)} collective-permute-done((f32[4,40,512]{2,1,0:T(8,128)S(1)}, f32[4,40,512]{2,1,0:T(8,128)S(1)}, u32[]{:S(2)}, u32[]{:S(2)}) %collective-permute-start.11) | collective-permute-done | bytes 327712 | tf_op jit(solution)/shard_map/ppermute | solution.py:32
  61.2 1.6 %collective-permute-start.12 = (bf16[48,512]{1,0:T(8,128)(2,1)S(1)}, bf16[48,512]{1,0:T(8,128)(2,1)S(1)}, u32[]{:S(2)}, u32[]{:S(2)}) collective-permute-start(bf16[48,512]{1,0:T(8,128)(2,1)S(1)} %get-tuple-element.59), channel_id=1, source_target_pairs={{0,2},{1,3},{2,0},{3,1},{4,6},{5,7},{6,4},{7,5},{8,10},{9,11},{10,... | collective-permute-start | bytes 147464 | tf_op jit(solution)/shard_map/ppermute | solution.py:32
  62.8 2.6 %collective-permute-start.13 = (bf16[48,512]{1,0:T(8,128)(2,1)S(1)}, bf16[48,512]{1,0:T(8,128)(2,1)S(1)}, u32[]{:S(2)}, u32[]{:S(2)}) collective-permute-start(bf16[48,512]{1,0:T(8,128)(2,1)S(1)} %get-tuple-element.60), channel_id=1, source_target_pairs={{0,4},{1,5},{2,6},{3,7},{4,0},{5,1},{6,2},{7,3},{8,12},{9,13},{10,... | collective-permute-start | bytes 147464 | tf_op jit(solution)/shard_map/ppermute | solution.py:32
  65.4 0.2 collective-permute-start.14
  65.6 0.0 collective-permute-done.12.refs_1_
  65.6 3.1 %collective-permute-done.13.refs_2_ = bf16[48,512]{1,0:T(8,128)(2,1)S(1)} collective-permute-done((bf16[48,512]{1,0:T(8,128)(2,1)S(1)}, bf16[48,512]{1,0:T(8,128)(2,1)S(1)}, u32[]{:S(2)}, u32[]{:S(2)}) %collective-permute-start.13) | collective-permute-done | bytes 49184 | tf_op jit(solution)/shard_map/ppermute | solution.py:32
  68.7 2.6 %collective-permute-done.14.refs_3_ = bf16[48,512]{1,0:T(8,128)(2,1)S(1)} collective-permute-done((bf16[48,512]{1,0:T(8,128)(2,1)S(1)}, bf16[48,512]{1,0:T(8,128)(2,1)S(1)}, u32[]{:S(2)}, u32[]{:S(2)}) %collective-permute-start.14) | collective-permute-done | bytes 49184 | tf_op jit(solution)/shard_map/ppermute | solution.py:32
  71.3 0.0 copy-done.1
  71.3 1.6 %cross.1 = (f32[4,8,4224]{2,1,0:T(8,128)S(1)}, f32[4,8,4224]{2,1,0:T(8,128)S(1)}, f32[32,512]{1,0:T(8,128)S(1)}, f32[8,512]{1,0:T(8,128)S(1)}) custom-call(f32[40,512]{1,0:T(8,128)S(1)} %get-tuple-element.58.refs_0_, bf16[48,512]{1,0:T(8,128)(2,1)S(1)} %collective-permute-done.12.refs_1_, bf16[48,512]{1,0:T(8,128)(2,1)S(1)} %collective-permute-done.13.refs_2_, ...), custom_call_target="tpu_custom_call" | custom-call | tf_op jit(solution)/shard_map/cross/pallas_call | solution.py:684
  72.9 0.1 collective-permute-start.15
  72.9 1.9 %collective-permute-done.15.refs_1_ = f32[4,8,4224]{2,1,0:T(8,128)S(1)} collective-permute-done((f32[4,8,4224]{2,1,0:T(8,128)S(1)}, f32[4,8,4224]{2,1,0:T(8,128)S(1)}, u32[]{:S(2)}, u32[]{:S(2)}) %collective-permute-start.15) | collective-permute-done | bytes 540704 | tf_op jit(solution)/shard_map/ppermute | solution.py:32
  74.9 0.1 fold.3
  74.9 0.1 collective-permute-start.16
  75.0 1.6 %collective-permute-start.17 = (bf16[8,4352]{1,0:T(8,128)(2,1)S(1)}, bf16[8,4352]{1,0:T(8,128)(2,1)S(1)}, u32[]{:S(2)}, u32[]{:S(2)}) collective-permute-start(bf16[8,4352]{1,0:T(8,128)(2,1)S(1)} %get-tuple-element.70), channel_id=1, source_target_pairs={{0,4},{1,5},{2,6},{3,7},{4,0},{5,1},{6,2},{7,3},{8,12},{9,13},{10,... | collective-permute-start | bytes 208904 | tf_op jit(solution)/shard_map/ppermute | solution.py:32
  76.6 2.8 %collective-permute-start.18 = (bf16[8,4352]{1,0:T(8,128)(2,1)S(1)}, bf16[8,4352]{1,0:T(8,128)(2,1)S(1)}, u32[]{:S(2)}, u32[]{:S(2)}) collective-permute-start(bf16[8,4352]{1,0:T(8,128)(2,1)S(1)} %get-tuple-element.71), channel_id=1, source_target_pairs={{0,6},{1,7},{2,4},{3,5},{4,2},{5,3},{6,0},{7,1},{8,14},{9,15},{10,... | collective-permute-start | bytes 208904 | tf_op jit(solution)/shard_map/ppermute | solution.py:32
  79.4 0.9 %collective-permute-done.16.refs_2_ = bf16[8,4352]{1,0:T(8,128)(2,1)S(1)} collective-permute-done((bf16[8,4352]{1,0:T(8,128)(2,1)S(1)}, bf16[8,4352]{1,0:T(8,128)(2,1)S(1)}, u32[]{:S(2)}, u32[]{:S(2)}) %collective-permute-start.16) | collective-permute-done | bytes 69664 | tf_op jit(solution)/shard_map/ppermute | solution.py:32
  80.2 3.7 %collective-permute-done.17.refs_3_ = bf16[8,4352]{1,0:T(8,128)(2,1)S(1)} collective-permute-done((bf16[8,4352]{1,0:T(8,128)(2,1)S(1)}, bf16[8,4352]{1,0:T(8,128)(2,1)S(1)}, u32[]{:S(2)}, u32[]{:S(2)}) %collective-permute-start.17) | collective-permute-done | bytes 69664 | tf_op jit(solution)/shard_map/ppermute | solution.py:32
  83.9 0.0 collective-permute-done.18.refs_4_
  83.9 2.7 %finish.1 = (f32[8,4096]{1,0:T(8,128)}, f32[4096,512]{1,0:T(8,128)}) custom-call(s32[4,32]{1,0:T(4,128)S(1)} %pad_add_fusion.refs_0_, f32[8,4224]{1,0:T(8,128)S(1)} %get-tuple-element.68.refs_1_, bf16[8,4352]{1,0:T(8,128)(2,1)S(1)} %collective-permute-done.16.refs_2_, ...), custom_call_target="tpu_custom_call", output_to_operand_aliasing={{1}: (10, {})} | custom-call | tf_op jit(solution)/shard_map/finish/pallas_call | solution.py:765
  (4 shorter events, 0.1 us)
Async XLA Ops:
  0.6 12.3 %copy-start = (bf16[1024,4096]{1,0:T(8,128)(2,1)S(1)}, bf16[1024,4096]{1,0:T(8,128)(2,1)}, u32[]{:S(2)}) copy-start(bf16[1024,4096]{1,0:T(8,128)(2,1)} %tok.1) | copy-start | bytes 25165828
  0.6 18.2 %copy-start.7 = (s32[32]{0:T(128)S(1)}, s32[32]{0:T(128)}, u32[]{:S(2)}) copy-start(s32[32]{0:T(128)} %param.21) | copy-start | bytes 388
  0.7 27.7 %copy-start.5 = (f32[512]{0:T(512)S(1)}, f32[512]{0:T(512)}, u32[]{:S(2)}) copy-start(f32[512]{0:T(512)} %param.20) | copy-start | bytes 6148
  0.7 27.7 %copy-start.6 = (s32[8]{0:T(128)S(1)}, s32[8]{0:T(128)}, u32[]{:S(2)}) copy-start(s32[8]{0:T(128)} %refs_1_.1) | copy-start | bytes 100
  0.7 33.2 %copy-start.4 = (s32[4096]{0:T(1024)S(1)}, s32[4096]{0:T(1024)}, u32[]{:S(2)}) copy-start(s32[4096]{0:T(1024)} %refs_0_.1) | copy-start | bytes 49156
  8.2 25.6 %collective-permute-start.4 = (bf16[1280,128]{1,0:T(8,128)(2,1)S(1)}, bf16[1280,128]{1,0:T(8,128)(2,1)S(1)}, u32[]{:S(2)}, u32[]{:S(2)}) collective-permute-start(bf16[1280,128]{1,0:T(8,128)(2,1)S(1)} %get-tuple-element.53.refs_5_), channel_id=1, source_target_pairs={{0,1},{1,0},{2,3},{3,2},{4,5},{5,4},{6,7},{7,6},{8,9},{9,8},{10,11... | collective-permute-start | bytes 983048 | tf_op jit(solution)/shard_map/ppermute | solution.py:32
  8.8 12.1 %collective-permute-start.3 = (bf16[1280,128]{1,0:T(8,128)(2,1)S(1)}, bf16[1280,128]{1,0:T(8,128)(2,1)S(1)}, u32[]{:S(2)}, u32[]{:S(2)}) collective-permute-start(bf16[1280,128]{1,0:T(8,128)(2,1)S(1)} %get-tuple-element.53.refs_5_), channel_id=1, source_target_pairs={{0,24},{8,16},{16,8},{24,0},{1,25},{9,17},{17,9},{25,1},{2,26},{10... | collective-permute-start | bytes 983048 | tf_op jit(solution)/shard_map/ppermute | solution.py:32
  12.3 15.5 %collective-permute-start.2 = (bf16[1280,128]{1,0:T(8,128)(2,1)S(1)}, bf16[1280,128]{1,0:T(8,128)(2,1)S(1)}, u32[]{:S(2)}, u32[]{:S(2)}) collective-permute-start(bf16[1280,128]{1,0:T(8,128)(2,1)S(1)} %get-tuple-element.53.refs_5_), channel_id=1, source_target_pairs={{0,16},{8,24},{16,0},{24,8},{1,17},{9,25},{17,1},{25,9},{2,18},{10... | collective-permute-start | bytes 983048 | tf_op jit(solution)/shard_map/ppermute | solution.py:32
  12.8 15.1 %collective-permute-start.1 = (bf16[1280,128]{1,0:T(8,128)(2,1)S(1)}, bf16[1280,128]{1,0:T(8,128)(2,1)S(1)}, u32[]{:S(2)}, u32[]{:S(2)}) collective-permute-start(bf16[1280,128]{1,0:T(8,128)(2,1)S(1)} %get-tuple-element.53.refs_5_), channel_id=1, source_target_pairs={{0,8},{8,0},{16,24},{24,16},{1,9},{9,1},{17,25},{25,17},{2,10},{10... | collective-permute-start | bytes 983048 | tf_op jit(solution)/shard_map/ppermute | solution.py:32
  12.9 1.6 %copy-start.3 = (bf16[4096,256]{1,0:T(8,128)(2,1)S(1)}, bf16[4096,256]{1,0:T(8,128)(2,1)}, u32[]{:S(2)}) copy-start(bf16[4096,256]{1,0:T(8,128)(2,1)} %weight.1) | copy-start | bytes 6291460
  17.3 16.5 %collective-permute-start = (bf16[512,256]{1,0:T(8,128)(2,1)S(1)}, bf16[512,256]{1,0:T(8,128)(2,1)S(1)}, u32[]{:S(2)}, u32[]{:S(2)}) collective-permute-start(bf16[512,256]{1,0:T(8,128)(2,1)S(1)} %get-tuple-element.50.refs_2_), channel_id=1, source_target_pairs={{24,0},{16,8},{25,1},{17,9},{26,2},{18,10},{27,3},{19,11},{28,4},{... | collective-permute-start | bytes 786440 | tf_op jit(solution)/shard_map/ppermute | solution.py:812
  20.9 13.0 %collective-permute-start.7 = (bf16[1280,128]{1,0:T(8,128)(2,1)S(1)}, bf16[1280,128]{1,0:T(8,128)(2,1)S(1)}, u32[]{:S(2)}, u32[]{:S(2)}) collective-permute-start(bf16[1280,128]{1,0:T(8,128)(2,1)S(1)} %collective-permute-done.3.refs_8_), channel_id=1, source_target_pairs={{0,1},{1,0},{2,3},{3,2},{4,5},{5,4},{6,7},{7,6},{8,9},{9,8},{10,11... | collective-permute-start | bytes 983048 | tf_op jit(solution)/shard_map/ppermute | solution.py:32
  27.8 6.1 %collective-permute-start.6 = (bf16[1280,128]{1,0:T(8,128)(2,1)S(1)}, bf16[1280,128]{1,0:T(8,128)(2,1)S(1)}, u32[]{:S(2)}, u32[]{:S(2)}) collective-permute-start(bf16[1280,128]{1,0:T(8,128)(2,1)S(1)} %collective-permute-done.2.refs_7_), channel_id=1, source_target_pairs={{0,1},{1,0},{2,3},{3,2},{4,5},{5,4},{6,7},{7,6},{8,9},{9,8},{10,11... | collective-permute-start | bytes 983048 | tf_op jit(solution)/shard_map/ppermute | solution.py:32
  27.9 6.0 %collective-permute-start.5 = (bf16[1280,128]{1,0:T(8,128)(2,1)S(1)}, bf16[1280,128]{1,0:T(8,128)(2,1)S(1)}, u32[]{:S(2)}, u32[]{:S(2)}) collective-permute-start(bf16[1280,128]{1,0:T(8,128)(2,1)S(1)} %collective-permute-done.1.refs_6_), channel_id=1, source_target_pairs={{0,1},{1,0},{2,3},{3,2},{4,5},{5,4},{6,7},{7,6},{8,9},{9,8},{10,11... | collective-permute-start | bytes 983048 | tf_op jit(solution)/shard_map/ppermute | solution.py:32
  33.8 25.1 %copy-start.2 = (bf16[256,4096]{1,0:T(8,128)(2,1)S(1)}, bf16[256,4096]{1,0:T(8,128)(2,1)}, u32[]{:S(2)}) copy-start(bf16[256,4096]{1,0:T(8,128)(2,1)} %refs_5_.3) | copy-start | bytes 6291460
  33.9 37.4 %copy-start.1 = (bf16[4096,512]{1,0:T(8,128)(2,1)S(1)}, bf16[4096,512]{1,0:T(8,128)(2,1)}, u32[]{:S(2)}) copy-start(bf16[4096,512]{1,0:T(8,128)(2,1)} %refs_8_.1) | copy-start | bytes 12582916
  52.2 5.1 %collective-permute-start.10 = (f32[32,256]{1,0:T(8,128)S(1)}, f32[32,256]{1,0:T(8,128)S(1)}, u32[]{:S(2)}, u32[]{:S(2)}) collective-permute-start(f32[32,256]{1,0:T(8,128)S(1)} %get-tuple-element.54.refs_0_), channel_id=1, source_target_pairs={{0,24},{8,16},{16,8},{24,0},{1,25},{9,17},{17,9},{25,1},{2,26},{10... | collective-permute-start | bytes 98312 | tf_op jit(solution)/shard_map/ppermute | solution.py:32
  52.3 5.0 %collective-permute-start.9 = (f32[32,256]{1,0:T(8,128)S(1)}, f32[32,256]{1,0:T(8,128)S(1)}, u32[]{:S(2)}, u32[]{:S(2)}) collective-permute-start(f32[32,256]{1,0:T(8,128)S(1)} %get-tuple-element.54.refs_0_), channel_id=1, source_target_pairs={{0,16},{8,24},{16,0},{24,8},{1,17},{9,25},{17,1},{25,9},{2,18},{10... | collective-permute-start | bytes 98312 | tf_op jit(solution)/shard_map/ppermute | solution.py:32
  55.1 3.9 %collective-permute-start.8 = (f32[32,256]{1,0:T(8,128)S(1)}, f32[32,256]{1,0:T(8,128)S(1)}, u32[]{:S(2)}, u32[]{:S(2)}) collective-permute-start(f32[32,256]{1,0:T(8,128)S(1)} %get-tuple-element.54.refs_0_), channel_id=1, source_target_pairs={{0,8},{8,0},{16,24},{24,16},{1,9},{9,1},{17,25},{25,17},{2,10},{10... | collective-permute-start | bytes 98312 | tf_op jit(solution)/shard_map/ppermute | solution.py:32
  59.5 1.7 %collective-permute-start.11 = (f32[4,40,512]{2,1,0:T(8,128)S(1)}, f32[4,40,512]{2,1,0:T(8,128)S(1)}, u32[]{:S(2)}, u32[]{:S(2)}) collective-permute-start(f32[4,40,512]{2,1,0:T(8,128)S(1)} %get-tuple-element.57), channel_id=1, source_target_pairs={{0,1},{1,0},{2,3},{3,2},{4,5},{5,4},{6,7},{7,6},{8,9},{9,8},{10,11... | collective-permute-start | bytes 983048 | tf_op jit(solution)/shard_map/ppermute | solution.py:32
  61.2 4.5 %collective-permute-start.12 = (bf16[48,512]{1,0:T(8,128)(2,1)S(1)}, bf16[48,512]{1,0:T(8,128)(2,1)S(1)}, u32[]{:S(2)}, u32[]{:S(2)}) collective-permute-start(bf16[48,512]{1,0:T(8,128)(2,1)S(1)} %get-tuple-element.59), channel_id=1, source_target_pairs={{0,2},{1,3},{2,0},{3,1},{4,6},{5,7},{6,4},{7,5},{8,10},{9,11},{10,... | collective-permute-start | bytes 147464 | tf_op jit(solution)/shard_map/ppermute | solution.py:32
  62.8 5.9 %collective-permute-start.13 = (bf16[48,512]{1,0:T(8,128)(2,1)S(1)}, bf16[48,512]{1,0:T(8,128)(2,1)S(1)}, u32[]{:S(2)}, u32[]{:S(2)}) collective-permute-start(bf16[48,512]{1,0:T(8,128)(2,1)S(1)} %get-tuple-element.60), channel_id=1, source_target_pairs={{0,4},{1,5},{2,6},{3,7},{4,0},{5,1},{6,2},{7,3},{8,12},{9,13},{10,... | collective-permute-start | bytes 147464 | tf_op jit(solution)/shard_map/ppermute | solution.py:32
  65.4 5.9 %collective-permute-start.14 = (bf16[48,512]{1,0:T(8,128)(2,1)S(1)}, bf16[48,512]{1,0:T(8,128)(2,1)S(1)}, u32[]{:S(2)}, u32[]{:S(2)}) collective-permute-start(bf16[48,512]{1,0:T(8,128)(2,1)S(1)} %get-tuple-element.61), channel_id=1, source_target_pairs={{0,6},{1,7},{2,4},{3,5},{4,2},{5,3},{6,0},{7,1},{8,14},{9,15},{10,... | collective-permute-start | bytes 147464 | tf_op jit(solution)/shard_map/ppermute | solution.py:32
  72.9 2.0 %collective-permute-start.15 = (f32[4,8,4224]{2,1,0:T(8,128)S(1)}, f32[4,8,4224]{2,1,0:T(8,128)S(1)}, u32[]{:S(2)}, u32[]{:S(2)}) collective-permute-start(f32[4,8,4224]{2,1,0:T(8,128)S(1)} %get-tuple-element.67), channel_id=1, source_target_pairs={{0,1},{1,0},{2,3},{3,2},{4,5},{5,4},{6,7},{7,6},{8,9},{9,8},{10,11... | collective-permute-start | bytes 1622024 | tf_op jit(solution)/shard_map/ppermute | solution.py:32
  74.9 5.3 %collective-permute-start.16 = (bf16[8,4352]{1,0:T(8,128)(2,1)S(1)}, bf16[8,4352]{1,0:T(8,128)(2,1)S(1)}, u32[]{:S(2)}, u32[]{:S(2)}) collective-permute-start(bf16[8,4352]{1,0:T(8,128)(2,1)S(1)} %get-tuple-element.69), channel_id=1, source_target_pairs={{0,2},{1,3},{2,0},{3,1},{4,6},{5,7},{6,4},{7,5},{8,10},{9,11},{10,... | collective-permute-start | bytes 208904 | tf_op jit(solution)/shard_map/ppermute | solution.py:32
  75.0 8.9 %collective-permute-start.17 = (bf16[8,4352]{1,0:T(8,128)(2,1)S(1)}, bf16[8,4352]{1,0:T(8,128)(2,1)S(1)}, u32[]{:S(2)}, u32[]{:S(2)}) collective-permute-start(bf16[8,4352]{1,0:T(8,128)(2,1)S(1)} %get-tuple-element.70), channel_id=1, source_target_pairs={{0,4},{1,5},{2,6},{3,7},{4,0},{5,1},{6,2},{7,3},{8,12},{9,13},{10,... | collective-permute-start | bytes 208904 | tf_op jit(solution)/shard_map/ppermute | solution.py:32
  76.6 7.3 %collective-permute-start.18 = (bf16[8,4352]{1,0:T(8,128)(2,1)S(1)}, bf16[8,4352]{1,0:T(8,128)(2,1)S(1)}, u32[]{:S(2)}, u32[]{:S(2)}) collective-permute-start(bf16[8,4352]{1,0:T(8,128)(2,1)S(1)} %get-tuple-element.71), channel_id=1, source_target_pairs={{0,6},{1,7},{2,4},{3,5},{4,2},{5,3},{6,0},{7,1},{8,14},{9,15},{10,... | collective-permute-start | bytes 208904 | tf_op jit(solution)/shard_map/ppermute | solution.py:32

commit v5 on v4

--- a/solution.py
+++ b/solution.py
@@ -14,8 +14,6 @@
 KB = 512
 LANES = 128
 GROUP = 16
-TOKEN_CHUNKS = 8
-AHEAD = 3
 COLUMNS_AS_ROWS = True
 
 rope_theta = 10000.0
@@ -74,13 +72,12 @@
     return result
 
 
-def kv_body(chunks, seg_total, *refs):
-    ids_in, wk_in, wv_in, fine_in, coarse_in, tok_in = refs[:6]
-    out, tables, tok, key_tables, weight, ids, fine, coarse, acc, small, sems = refs[6:]
-    rows, width = tok.shape
+def kv_body(seg_total, *refs):
+    ids_in, wk_in, wv_in, fine_in, coarse_in, tok = refs[:6]
+    out, tables, key_tables, weight, ids, fine, coarse, acc, small = refs[6:]
+    rows, _ = tok.shape
     half = wk_in.shape[0]
     subs = rows // LANES
-    size = width // chunks
     rest = [
         pltpu.make_async_copy(wk_in, weight.at[pl.ds(0, half), :], small.at[0]),
         pltpu.make_async_copy(wv_in, weight.at[pl.ds(half, half), :], small.at[1]),
@@ -89,9 +86,6 @@
         pltpu.make_async_copy(ids_in, ids, small.at[4]),
     ]
     for c in rest:
-        c.start()
-    copies = stream(tok_in, tok, sems, chunks, 1)
-    for c in copies[:AHEAD]:
         c.start()
     for c in rest:
         c.wait()
@@ -112,15 +106,9 @@
         key_tables[1, at, :] = jnp.where(lane < half, sin, 0.0)
         member = ids[pl.ds(first + sub, 1), :] == lax.broadcasted_iota(i32, (seg_total, LANES), 0)
         members.append(jnp.where(member, 1.0, 0.0))
-    for i in range(chunks):
-        at = slice(i * size, (i + 1) * size)
-        copies[i].wait()
-        if i + AHEAD < chunks:
-            copies[i + AHEAD].start()
-        part = lax.dot_general(
-            tok[:, at], weight[:, at], (((1,), (1,)), ((), ())), preferred_element_type=f32
-        )
-        acc[...] = part if i == 0 else acc[...] + part
+    acc[...] = lax.dot_general(
+        tok[...], weight[...], (((1,), (1,)), ((), ())), preferred_element_type=f32
+    )
     for sub in range(subs):
         at = slice(sub * LANES, (sub + 1) * LANES)
         x = acc[at]
@@ -145,18 +133,17 @@
     whole = pl.BlockSpec(memory_space=pltpu.VMEM)
 
     def body(*refs):
-        kv_body(TOKEN_CHUNKS, seg_total, *refs)
+        kv_body(seg_total, *refs)
 
     return pl.pallas_call(
         body,
-        in_specs=[pl.BlockSpec(memory_space=pltpu.HBM)] * 6,
+        in_specs=[pl.BlockSpec(memory_space=pltpu.HBM)] * 5 + [whole],
         out_specs=[whole] * 2,
         out_shape=[
             jax.ShapeDtypeStruct((rows + 2 * seg_total * feat // LANES, 2 * half), bf16),
             jax.ShapeDtypeStruct((2, rows, LANES), f32),
         ],
         scratch_shapes=[
-            pltpu.VMEM((rows, width), bf16),
             pltpu.VMEM((2, rows, LANES), f32),
             pltpu.VMEM((2 * half, width), bf16),
             pltpu.VMEM(ids.shape, i32),
@@ -164,12 +151,11 @@
             pltpu.VMEM(coarse.shape, f32),
             pltpu.VMEM((rows, 2 * half), f32),
             pltpu.SemaphoreType.DMA((5,)),
-            pltpu.SemaphoreType.DMA((TOKEN_CHUNKS,)),
         ],
         compiler_params=pltpu.CompilerParams(vmem_limit_bytes=20 * MIB),
         cost_estimate=pl.CostEstimate(flops=2 * rows * width * 2 * half, bytes_accessed=2 * rows * width, transcendentals=0),
         name="project_kv",
-    )(*[far(x) for x in (ids, w_key.T, w_value.T, fine, coarse, tokens)])
+    )(*[far(x) for x in (ids, w_key.T, w_value.T, fine, coarse)], near(tokens))
 
 
 def q_body(tok, weight, tables, *refs):
@@ -375,8 +361,8 @@
         base = pl.multiple_of(base, QB)
         last_seg = seg[base + QB - 1]
         first_seg = seg[base]
-        end = (base + QB - 1) // KB + 1
         clear_end = base // KB
+        short = (base % KB + QB <= QB).astype(i32)
         begin = jnp.int32(0)
         clear = jnp.int32(0)
         for t in range(seq_len // KB):
@@ -431,7 +417,8 @@
             0, pairs, lambda t, c: score(False, 2 * KB, clear + 2 * t, c), state
         )
         state = lax.fori_loop(single, clear_end, lambda kb, c: score(False, KB, kb, c), state)
-        state = lax.fori_loop(clear_end, end, lambda kb, c: score(True, KB, kb, c), state)
+        state = lax.fori_loop(0, short, lambda t, c: score(True, QB, clear_end, c), state)
+        state = lax.fori_loop(short, 1, lambda t, c: score(True, KB, clear_end, c), state)
         top = jnp.concatenate([t for t, _ in state], 1)
         total = jnp.concatenate([t for _, t in state], 1)
         share = 1.0 / jnp.sum(total, axis=0, keepdims=True)
@@ -457,7 +444,9 @@
 
         lax.fori_loop(begin, clear, lambda kb, c: gather(KB, kb, c), 0)
         lax.fori_loop(0, pairs, lambda t, c: gather(2 * KB, clear + 2 * t, c), 0)
-        lax.fori_loop(single, end, lambda kb, c: gather(KB, kb, c), 0)
+        lax.fori_loop(single, clear_end, lambda kb, c: gather(KB, kb, c), 0)
+        lax.fori_loop(0, short, lambda t, c: gather(QB, clear_end, c), 0)
+        lax.fori_loop(short, 1, lambda t, c: gather(KB, clear_end, c), 0)
         return carry
 
     if balanced:

time: 87 us -> 86 us (0.989)
  Pallas kernels: 39 us -> 34.7 us
  local copies, waits for them, and re-layouts: 1.62 us -> 3.41 us
  waiting for transfers between devices: 25.9 us -> 27.4 us
    pallas_call x1, Pallas kernels: 7.53 us -> 3.94 us  [project_kv(): pl.pallas_call(body, in_specs=[pl.BlockSpec(memory_space=pltpu.HBM)] * 5...]
    unnamed x16, local copies, waits for them, and re-layouts: 1.62 us -> 3.41 us
    ppermute x18, waiting for transfers between devices: 25.8 us -> 27.4 us  [swapped(): return lax.ppermute(x, axis, [(i, i ^ mask) for i in range(count)])]
where the time goes in v5:
time: 86 us; the launch traced here: 85.8 us
  Pallas kernels  34.7 us (40%)
  waiting for transfers between devices  27.4 us (32%)
  starting transfers between devices  19.1 us (22%)
  local copies, waits for them, and re-layouts  3.41 us (4%)
  between operations  1 us (1%)
    ppermute x18, waiting for transfers between devices, swapped(): return lax.ppermute(x, axis, [(i, i ^ mask) for i in range(count)])  27.4 us
    ppermute x18, starting transfers between devices, swapped(): return lax.ppermute(x, axis, [(i, i ^ mask) for i in range(count)])  17.7 us
    pallas_call x1, Pallas kernels, attend(): pl.pallas_call(body, in_specs=[pl.BlockSpec(memory_space=pltpu.SMEM), who...  17.6 us
    pallas_call x1, Pallas kernels, widen_centroids(): pl.pallas_call(body, in_specs=[scalar, scalar, whole, in_hbm], out_specs=...  5.47 us
    pallas_call x1, Pallas kernels, project_kv(): pl.pallas_call(body, in_specs=[pl.BlockSpec(memory_space=pltpu.HBM)] * 5...  3.94 us
    unnamed x16, local copies, waits for them, and re-layouts  3.41 us
    pallas_call x1, Pallas kernels, project_q(): pl.pallas_call(q_body, in_specs=[whole] * 3, out_specs=[whole, whole], ou...  2.85 us
    pallas_call x1, Pallas kernels, finish(): pl.pallas_call(body, in_specs=[scalar] + [whole] * (groups + 5) + [in_hbm...  2.67 us
  transfers between devices with their start and end apart: 19, of which 11 were waited for; matrix products, arithmetic and copies ran while one was open for 0% of the time, Pallas kernels for 10%

profile of v5, /device:TPU:0, one launch (start us, length us, event | category | flops | bytes accessed | tf_op | source)
XLA Modules:
  0.0 85.8 jit_solution(10134979037864212615)
XLA Ops:
  0.6 0.0 copy-start
  0.6 3.4 %copy-done = bf16[1024,4096]{1,0:T(8,128)(2,1)S(1)} copy-done((bf16[1024,4096]{1,0:T(8,128)(2,1)S(1)}, bf16[1024,4096]{1,0:T(8,128)(2,1)}, u32[]{:S(2)}) %copy-start) | copy-done | bytes 8388632
  4.0 0.0 copy-start.3
  4.0 0.0 copy-start.7
  4.0 0.0 copy-start.5
  4.0 0.0 copy-start.6
  4.0 3.9 %project_kv.1 = (bf16[1280,128]{1,0:T(8,128)(2,1)S(1)}, f32[2,1024,128]{2,1,0:T(8,128)S(1)}) custom-call(s32[32,128]{1,0:T(8,128)} %bitcast.11, bf16[64,4096]{1,0:T(8,128)(2,1)} %bitcast.14, bf16[64,4096]{1,0:T(8,128)(2,1)} %bitcast.15, f32[2,128,128]{2,1,0:T(8,128)} %constant.41.clone.refs_3_, f32[2,32,128]{2,1,0:T(8,128)} %constant.42.clone.refs_4_, ...), custom_call_target="tpu_custom_call" | custom-call | flops 1073741824 | bytes 8388608 | tf_op jit(solution)/shard_map/project_kv/pallas_call | solution.py:138
  8.0 0.0 copy-start.4
  8.0 0.6 collective-permute-start.4
  8.5 3.5 %collective-permute-start.3 = (bf16[1280,128]{1,0:T(8,128)(2,1)S(1)}, bf16[1280,128]{1,0:T(8,128)(2,1)S(1)}, u32[]{:S(2)}, u32[]{:S(2)}) collective-permute-start(bf16[1280,128]{1,0:T(8,128)(2,1)S(1)} %get-tuple-element.53.refs_5_), channel_id=1, source_target_pairs={{0,24},{8,16},{16,8},{24,0},{1,25},{9,17},{17,9},{25,1},{2,26},{10... | collective-permute-start | bytes 983048 | tf_op jit(solution)/shard_map/ppermute | solution.py:30
  12.0 0.5 collective-permute-start.2
  12.5 0.1 collective-permute-start.1
  12.7 0.0 copy-done.3
  12.7 2.8 %project_q.1 = (bf16[512,256]{1,0:T(8,128)(2,1)S(1)}, bf16[512,256]{1,0:T(8,128)(2,1)S(1)}) custom-call(bf16[1024,4096]{1,0:T(8,128)(2,1)S(1)} %copy-done, bf16[4096,256]{1,0:T(8,128)(2,1)S(1)} %copy-done.3, f32[2,1024,128]{2,1,0:T(8,128)S(1)} %get-tuple-element.40.tables), custom_call_target="tpu_custom_call" | custom-call | flops 2147483648 | bytes 10485760 | tf_op jit(solution)/shard_map/project_q/pallas_call | solution.py:190
  15.5 1.5 %collective-permute-start = (bf16[512,256]{1,0:T(8,128)(2,1)S(1)}, bf16[512,256]{1,0:T(8,128)(2,1)S(1)}, u32[]{:S(2)}, u32[]{:S(2)}) collective-permute-start(bf16[512,256]{1,0:T(8,128)(2,1)S(1)} %get-tuple-element.50.refs_2_), channel_id=1, source_target_pairs={{24,0},{16,8},{25,1},{17,9},{26,2},{18,10},{27,3},{19,11},{28,4},{... | collective-permute-start | bytes 786440 | tf_op jit(solution)/shard_map/ppermute | solution.py:801
  17.0 0.0 copy-done.7
  17.0 0.2 fusion.1
  17.2 3.4 %collective-permute-done.3.refs_8_ = bf16[1280,128]{1,0:T(8,128)(2,1)S(1)} collective-permute-done((bf16[1280,128]{1,0:T(8,128)(2,1)S(1)}, bf16[1280,128]{1,0:T(8,128)(2,1)S(1)}, u32[]{:S(2)}, u32[]{:S(2)}) %collective-permute-start.3) | collective-permute-done | bytes 327712 | tf_op jit(solution)/shard_map/ppermute | solution.py:30
  20.6 0.0 collective-permute-start.7
  20.6 6.9 %collective-permute-done.2.refs_7_ = bf16[1280,128]{1,0:T(8,128)(2,1)S(1)} collective-permute-done((bf16[1280,128]{1,0:T(8,128)(2,1)S(1)}, bf16[1280,128]{1,0:T(8,128)(2,1)S(1)}, u32[]{:S(2)}, u32[]{:S(2)}) %collective-permute-start.2) | collective-permute-done | bytes 327712 | tf_op jit(solution)/shard_map/ppermute | solution.py:30
  27.6 0.0 collective-permute-start.6
  27.6 0.1 collective-permute-done.1.refs_6_
  27.7 0.4 collective-permute-start.5
  28.1 0.0 copy-done.5
  28.1 0.0 copy-done.6
  28.1 5.5 %widen_centroids.1 = (f32[4096,512]{1,0:T(8,128)}, f32[8,512]{1,0:T(8,128)S(1)}, bf16[512,512]{1,0:T(8,128)(2,1)S(1)}, f32[1,512]{1,0:T(1,128)S(1)}, f32[64,32]{...) custom-call(s32[4,32]{1,0:T(4,128)S(1)} %pad_add_fusion.refs_0_, s32[8]{0:T(128)S(1)} %copy-done.6, ...), custom_call_target="tpu_custom_call" | custom-call | flops 8388608 | bytes 12582912 | tf_op jit(solution)/shard_map/widen_centroids/pallas_call | solution.py:274
  33.6 0.0 copy-start.2
  33.6 0.0 collective-permute-done.refs_4_
  33.6 0.0 copy-start.1
  33.6 0.0 collective-permute-done.4.refs_9_
  33.6 0.0 collective-permute-done.7.refs_12_
  33.6 0.0 collective-permute-done.6.refs_11_
  33.7 0.0 collective-permute-done.5.refs_10_
  33.7 0.0 copy-done.4
  33.7 17.6 %attend.1 = (f32[32,256]{1,0:T(8,128)S(1)}, f32[32,128]{1,0:T(8,128)S(1)}, f32[32,512]{1,0:T(8,128)S(1)}) custom-call(s32[4096]{0:T(1024)S(1)} %copy-done.4, s32[32,128]{1,0:T(8,128)S(1)} %bitcast.12, bf16[512,256]{1,0:T(8,128)(2,1)S(1)} %get-tuple-element.50.refs_2_, bf16[512,256]{1,0:T(8,128)(2,1)S(1)} %get-tuple-element.51.refs_3_, ...), custom_call_target="tpu_custom_call" | custom-call | flops 4294967296 | bytes 2097152 | tf_op jit(solution)/shard_map/attend/pallas_call | solution.py:502
  51.3 0.1 collective-permute-start.10
  51.4 2.8 %collective-permute-start.9 = (f32[32,256]{1,0:T(8,128)S(1)}, f32[32,256]{1,0:T(8,128)S(1)}, u32[]{:S(2)}, u32[]{:S(2)}) collective-permute-start(f32[32,256]{1,0:T(8,128)S(1)} %get-tuple-element.54.refs_0_), channel_id=1, source_target_pairs={{0,16},{8,24},{16,0},{24,8},{1,17},{9,25},{17,1},{25,9},{2,18},{10... | collective-permute-start | bytes 98312 | tf_op jit(solution)/shard_map/ppermute | solution.py:30
  54.1 0.7 collective-permute-start.8
  54.8 1.6 %collective-permute-done.10.refs_3_ = f32[32,256]{1,0:T(8,128)S(1)} collective-permute-done((f32[32,256]{1,0:T(8,128)S(1)}, f32[32,256]{1,0:T(8,128)S(1)}, u32[]{:S(2)}, u32[]{:S(2)}) %collective-permute-start.10) | collective-permute-done | bytes 32800 | tf_op jit(solution)/shard_map/ppermute | solution.py:30
  56.4 0.0 collective-permute-done.9.refs_2_
  56.4 1.6 %collective-permute-done.8.refs_1_ = f32[32,256]{1,0:T(8,128)S(1)} collective-permute-done((f32[32,256]{1,0:T(8,128)S(1)}, f32[32,256]{1,0:T(8,128)S(1)}, u32[]{:S(2)}, u32[]{:S(2)}) %collective-permute-start.8) | collective-permute-done | bytes 32800 | tf_op jit(solution)/shard_map/ppermute | solution.py:30
  58.0 0.0 copy-done.2
  58.0 0.5 mix.1
  58.5 0.0 collective-permute-start.11
  58.6 1.6 %collective-permute-done.11.refs_1_ = f32[4,40,512]{2,1,0:T(8,128)S(1)} collective-permute-done((f32[4,40,512]{2,1,0:T(8,128)S(1)}, f32[4,40,512]{2,1,0:T(8,128)S(1)}, u32[]{:S(2)}, u32[]{:S(2)}) %collective-permute-start.11) | collective-permute-done | bytes 327712 | tf_op jit(solution)/shard_map/ppermute | solution.py:30
  60.2 1.7 %collective-permute-start.12 = (bf16[48,512]{1,0:T(8,128)(2,1)S(1)}, bf16[48,512]{1,0:T(8,128)(2,1)S(1)}, u32[]{:S(2)}, u32[]{:S(2)}) collective-permute-start(bf16[48,512]{1,0:T(8,128)(2,1)S(1)} %get-tuple-element.59), channel_id=1, source_target_pairs={{0,2},{1,3},{2,0},{3,1},{4,6},{5,7},{6,4},{7,5},{8,10},{9,11},{10,... | collective-permute-start | bytes 147464 | tf_op jit(solution)/shard_map/ppermute | solution.py:30
  61.9 2.6 %collective-permute-start.13 = (bf16[48,512]{1,0:T(8,128)(2,1)S(1)}, bf16[48,512]{1,0:T(8,128)(2,1)S(1)}, u32[]{:S(2)}, u32[]{:S(2)}) collective-permute-start(bf16[48,512]{1,0:T(8,128)(2,1)S(1)} %get-tuple-element.60), channel_id=1, source_target_pairs={{0,4},{1,5},{2,6},{3,7},{4,0},{5,1},{6,2},{7,3},{8,12},{9,13},{10,... | collective-permute-start | bytes 147464 | tf_op jit(solution)/shard_map/ppermute | solution.py:30
  64.5 0.2 collective-permute-start.14
  64.7 0.0 collective-permute-done.12.refs_1_
  64.7 3.1 %collective-permute-done.13.refs_2_ = bf16[48,512]{1,0:T(8,128)(2,1)S(1)} collective-permute-done((bf16[48,512]{1,0:T(8,128)(2,1)S(1)}, bf16[48,512]{1,0:T(8,128)(2,1)S(1)}, u32[]{:S(2)}, u32[]{:S(2)}) %collective-permute-start.13) | collective-permute-done | bytes 49184 | tf_op jit(solution)/shard_map/ppermute | solution.py:30
  67.8 2.6 %collective-permute-done.14.refs_3_ = bf16[48,512]{1,0:T(8,128)(2,1)S(1)} collective-permute-done((bf16[48,512]{1,0:T(8,128)(2,1)S(1)}, bf16[48,512]{1,0:T(8,128)(2,1)S(1)}, u32[]{:S(2)}, u32[]{:S(2)}) %collective-permute-start.14) | collective-permute-done | bytes 49184 | tf_op jit(solution)/shard_map/ppermute | solution.py:30
  70.3 0.0 copy-done.1
  70.3 1.6 %cross.1 = (f32[4,8,4224]{2,1,0:T(8,128)S(1)}, f32[4,8,4224]{2,1,0:T(8,128)S(1)}, f32[32,512]{1,0:T(8,128)S(1)}, f32[8,512]{1,0:T(8,128)S(1)}) custom-call(f32[40,512]{1,0:T(8,128)S(1)} %get-tuple-element.58.refs_0_, bf16[48,512]{1,0:T(8,128)(2,1)S(1)} %collective-permute-done.12.refs_1_, bf16[48,512]{1,0:T(8,128)(2,1)S(1)} %collective-permute-done.13.refs_2_, ...), custom_call_target="tpu_custom_call" | custom-call | tf_op jit(solution)/shard_map/cross/pallas_call | solution.py:673
  71.9 0.1 collective-permute-start.15
  72.0 1.9 %collective-permute-done.15.refs_1_ = f32[4,8,4224]{2,1,0:T(8,128)S(1)} collective-permute-done((f32[4,8,4224]{2,1,0:T(8,128)S(1)}, f32[4,8,4224]{2,1,0:T(8,128)S(1)}, u32[]{:S(2)}, u32[]{:S(2)}) %collective-permute-start.15) | collective-permute-done | bytes 540704 | tf_op jit(solution)/shard_map/ppermute | solution.py:30
  73.9 0.1 fold.3
  74.0 0.1 collective-permute-start.16
  74.0 1.6 %collective-permute-start.17 = (bf16[8,4352]{1,0:T(8,128)(2,1)S(1)}, bf16[8,4352]{1,0:T(8,128)(2,1)S(1)}, u32[]{:S(2)}, u32[]{:S(2)}) collective-permute-start(bf16[8,4352]{1,0:T(8,128)(2,1)S(1)} %get-tuple-element.70), channel_id=1, source_target_pairs={{0,4},{1,5},{2,6},{3,7},{4,0},{5,1},{6,2},{7,3},{8,12},{9,13},{10,... | collective-permute-start | bytes 208904 | tf_op jit(solution)/shard_map/ppermute | solution.py:30
  75.6 2.8 %collective-permute-start.18 = (bf16[8,4352]{1,0:T(8,128)(2,1)S(1)}, bf16[8,4352]{1,0:T(8,128)(2,1)S(1)}, u32[]{:S(2)}, u32[]{:S(2)}) collective-permute-start(bf16[8,4352]{1,0:T(8,128)(2,1)S(1)} %get-tuple-element.71), channel_id=1, source_target_pairs={{0,6},{1,7},{2,4},{3,5},{4,2},{5,3},{6,0},{7,1},{8,14},{9,15},{10,... | collective-permute-start | bytes 208904 | tf_op jit(solution)/shard_map/ppermute | solution.py:30
  78.4 0.9 %collective-permute-done.16.refs_2_ = bf16[8,4352]{1,0:T(8,128)(2,1)S(1)} collective-permute-done((bf16[8,4352]{1,0:T(8,128)(2,1)S(1)}, bf16[8,4352]{1,0:T(8,128)(2,1)S(1)}, u32[]{:S(2)}, u32[]{:S(2)}) %collective-permute-start.16) | collective-permute-done | bytes 69664 | tf_op jit(solution)/shard_map/ppermute | solution.py:30
  79.3 3.7 %collective-permute-done.17.refs_3_ = bf16[8,4352]{1,0:T(8,128)(2,1)S(1)} collective-permute-done((bf16[8,4352]{1,0:T(8,128)(2,1)S(1)}, bf16[8,4352]{1,0:T(8,128)(2,1)S(1)}, u32[]{:S(2)}, u32[]{:S(2)}) %collective-permute-start.17) | collective-permute-done | bytes 69664 | tf_op jit(solution)/shard_map/ppermute | solution.py:30
  83.0 0.0 collective-permute-done.18.refs_4_
  83.0 2.7 %finish.1 = (f32[8,4096]{1,0:T(8,128)}, f32[4096,512]{1,0:T(8,128)}) custom-call(s32[4,32]{1,0:T(4,128)S(1)} %pad_add_fusion.refs_0_, f32[8,4224]{1,0:T(8,128)S(1)} %get-tuple-element.68.refs_1_, bf16[8,4352]{1,0:T(8,128)(2,1)S(1)} %collective-permute-done.16.refs_2_, ...), custom_call_target="tpu_custom_call", output_to_operand_aliasing={{1}: (10, {})} | custom-call | tf_op jit(solution)/shard_map/finish/pallas_call | solution.py:754
  (4 shorter events, 0.1 us)
Async XLA Ops:
  0.6 3.4 %copy-start = (bf16[1024,4096]{1,0:T(8,128)(2,1)S(1)}, bf16[1024,4096]{1,0:T(8,128)(2,1)}, u32[]{:S(2)}) copy-start(bf16[1024,4096]{1,0:T(8,128)(2,1)} %tok.1) | copy-start | bytes 25165828
  4.0 8.7 %copy-start.3 = (bf16[4096,256]{1,0:T(8,128)(2,1)S(1)}, bf16[4096,256]{1,0:T(8,128)(2,1)}, u32[]{:S(2)}) copy-start(bf16[4096,256]{1,0:T(8,128)(2,1)} %weight.1) | copy-start | bytes 6291460
  4.0 13.0 %copy-start.7 = (s32[32]{0:T(128)S(1)}, s32[32]{0:T(128)}, u32[]{:S(2)}) copy-start(s32[32]{0:T(128)} %param.21) | copy-start | bytes 388
  4.0 24.1 %copy-start.5 = (f32[512]{0:T(512)S(1)}, f32[512]{0:T(512)}, u32[]{:S(2)}) copy-start(f32[512]{0:T(512)} %param.20) | copy-start | bytes 6148
  4.0 24.1 %copy-start.6 = (s32[8]{0:T(128)S(1)}, s32[8]{0:T(128)}, u32[]{:S(2)}) copy-start(s32[8]{0:T(128)} %refs_1_.1) | copy-start | bytes 100
  8.0 25.7 %copy-start.4 = (s32[4096]{0:T(1024)S(1)}, s32[4096]{0:T(1024)}, u32[]{:S(2)}) copy-start(s32[4096]{0:T(1024)} %refs_0_.1) | copy-start | bytes 49156
  8.0 25.6 %collective-permute-start.4 = (bf16[1280,128]{1,0:T(8,128)(2,1)S(1)}, bf16[1280,128]{1,0:T(8,128)(2,1)S(1)}, u32[]{:S(2)}, u32[]{:S(2)}) collective-permute-start(bf16[1280,128]{1,0:T(8,128)(2,1)S(1)} %get-tuple-element.53.refs_5_), channel_id=1, source_target_pairs={{0,1},{1,0},{2,3},{3,2},{4,5},{5,4},{6,7},{7,6},{8,9},{9,8},{10,11... | collective-permute-start | bytes 983048 | tf_op jit(solution)/shard_map/ppermute | solution.py:30
  8.5 12.1 %collective-permute-start.3 = (bf16[1280,128]{1,0:T(8,128)(2,1)S(1)}, bf16[1280,128]{1,0:T(8,128)(2,1)S(1)}, u32[]{:S(2)}, u32[]{:S(2)}) collective-permute-start(bf16[1280,128]{1,0:T(8,128)(2,1)S(1)} %get-tuple-element.53.refs_5_), channel_id=1, source_target_pairs={{0,24},{8,16},{16,8},{24,0},{1,25},{9,17},{17,9},{25,1},{2,26},{10... | collective-permute-start | bytes 983048 | tf_op jit(solution)/shard_map/ppermute | solution.py:30
  12.0 15.5 %collective-permute-start.2 = (bf16[1280,128]{1,0:T(8,128)(2,1)S(1)}, bf16[1280,128]{1,0:T(8,128)(2,1)S(1)}, u32[]{:S(2)}, u32[]{:S(2)}) collective-permute-start(bf16[1280,128]{1,0:T(8,128)(2,1)S(1)} %get-tuple-element.53.refs_5_), channel_id=1, source_target_pairs={{0,16},{8,24},{16,0},{24,8},{1,17},{9,25},{17,1},{25,9},{2,18},{10... | collective-permute-start | bytes 983048 | tf_op jit(solution)/shard_map/ppermute | solution.py:30
  12.5 15.1 %collective-permute-start.1 = (bf16[1280,128]{1,0:T(8,128)(2,1)S(1)}, bf16[1280,128]{1,0:T(8,128)(2,1)S(1)}, u32[]{:S(2)}, u32[]{:S(2)}) collective-permute-start(bf16[1280,128]{1,0:T(8,128)(2,1)S(1)} %get-tuple-element.53.refs_5_), channel_id=1, source_target_pairs={{0,8},{8,0},{16,24},{24,16},{1,9},{9,1},{17,25},{25,17},{2,10},{10... | collective-permute-start | bytes 983048 | tf_op jit(solution)/shard_map/ppermute | solution.py:30
  15.5 18.1 %collective-permute-start = (bf16[512,256]{1,0:T(8,128)(2,1)S(1)}, bf16[512,256]{1,0:T(8,128)(2,1)S(1)}, u32[]{:S(2)}, u32[]{:S(2)}) collective-permute-start(bf16[512,256]{1,0:T(8,128)(2,1)S(1)} %get-tuple-element.50.refs_2_), channel_id=1, source_target_pairs={{24,0},{16,8},{25,1},{17,9},{26,2},{18,10},{27,3},{19,11},{28,4},{... | collective-permute-start | bytes 786440 | tf_op jit(solution)/shard_map/ppermute | solution.py:801
  20.6 13.0 %collective-permute-start.7 = (bf16[1280,128]{1,0:T(8,128)(2,1)S(1)}, bf16[1280,128]{1,0:T(8,128)(2,1)S(1)}, u32[]{:S(2)}, u32[]{:S(2)}) collective-permute-start(bf16[1280,128]{1,0:T(8,128)(2,1)S(1)} %collective-permute-done.3.refs_8_), channel_id=1, source_target_pairs={{0,1},{1,0},{2,3},{3,2},{4,5},{5,4},{6,7},{7,6},{8,9},{9,8},{10,11... | collective-permute-start | bytes 983048 | tf_op jit(solution)/shard_map/ppermute | solution.py:30
  27.6 6.1 %collective-permute-start.6 = (bf16[1280,128]{1,0:T(8,128)(2,1)S(1)}, bf16[1280,128]{1,0:T(8,128)(2,1)S(1)}, u32[]{:S(2)}, u32[]{:S(2)}) collective-permute-start(bf16[1280,128]{1,0:T(8,128)(2,1)S(1)} %collective-permute-done.2.refs_7_), channel_id=1, source_target_pairs={{0,1},{1,0},{2,3},{3,2},{4,5},{5,4},{6,7},{7,6},{8,9},{9,8},{10,11... | collective-permute-start | bytes 983048 | tf_op jit(solution)/shard_map/ppermute | solution.py:30
  27.7 6.0 %collective-permute-start.5 = (bf16[1280,128]{1,0:T(8,128)(2,1)S(1)}, bf16[1280,128]{1,0:T(8,128)(2,1)S(1)}, u32[]{:S(2)}, u32[]{:S(2)}) collective-permute-start(bf16[1280,128]{1,0:T(8,128)(2,1)S(1)} %collective-permute-done.1.refs_6_), channel_id=1, source_target_pairs={{0,1},{1,0},{2,3},{3,2},{4,5},{5,4},{6,7},{7,6},{8,9},{9,8},{10,11... | collective-permute-start | bytes 983048 | tf_op jit(solution)/shard_map/ppermute | solution.py:30
  33.6 24.4 %copy-start.2 = (bf16[256,4096]{1,0:T(8,128)(2,1)S(1)}, bf16[256,4096]{1,0:T(8,128)(2,1)}, u32[]{:S(2)}) copy-start(bf16[256,4096]{1,0:T(8,128)(2,1)} %refs_5_.3) | copy-start | bytes 6291460
  33.6 36.7 %copy-start.1 = (bf16[4096,512]{1,0:T(8,128)(2,1)S(1)}, bf16[4096,512]{1,0:T(8,128)(2,1)}, u32[]{:S(2)}) copy-start(bf16[4096,512]{1,0:T(8,128)(2,1)} %refs_8_.1) | copy-start | bytes 12582916
  51.3 5.1 %collective-permute-start.10 = (f32[32,256]{1,0:T(8,128)S(1)}, f32[32,256]{1,0:T(8,128)S(1)}, u32[]{:S(2)}, u32[]{:S(2)}) collective-permute-start(f32[32,256]{1,0:T(8,128)S(1)} %get-tuple-element.54.refs_0_), channel_id=1, source_target_pairs={{0,24},{8,16},{16,8},{24,0},{1,25},{9,17},{17,9},{25,1},{2,26},{10... | collective-permute-start | bytes 98312 | tf_op jit(solution)/shard_map/ppermute | solution.py:30
  51.4 5.1 %collective-permute-start.9 = (f32[32,256]{1,0:T(8,128)S(1)}, f32[32,256]{1,0:T(8,128)S(1)}, u32[]{:S(2)}, u32[]{:S(2)}) collective-permute-start(f32[32,256]{1,0:T(8,128)S(1)} %get-tuple-element.54.refs_0_), channel_id=1, source_target_pairs={{0,16},{8,24},{16,0},{24,8},{1,17},{9,25},{17,1},{25,9},{2,18},{10... | collective-permute-start | bytes 98312 | tf_op jit(solution)/shard_map/ppermute | solution.py:30
  54.1 3.9 %collective-permute-start.8 = (f32[32,256]{1,0:T(8,128)S(1)}, f32[32,256]{1,0:T(8,128)S(1)}, u32[]{:S(2)}, u32[]{:S(2)}) collective-permute-start(f32[32,256]{1,0:T(8,128)S(1)} %get-tuple-element.54.refs_0_), channel_id=1, source_target_pairs={{0,8},{8,0},{16,24},{24,16},{1,9},{9,1},{17,25},{25,17},{2,10},{10... | collective-permute-start | bytes 98312 | tf_op jit(solution)/shard_map/ppermute | solution.py:30
  58.5 1.7 %collective-permute-start.11 = (f32[4,40,512]{2,1,0:T(8,128)S(1)}, f32[4,40,512]{2,1,0:T(8,128)S(1)}, u32[]{:S(2)}, u32[]{:S(2)}) collective-permute-start(f32[4,40,512]{2,1,0:T(8,128)S(1)} %get-tuple-element.57), channel_id=1, source_target_pairs={{0,1},{1,0},{2,3},{3,2},{4,5},{5,4},{6,7},{7,6},{8,9},{9,8},{10,11... | collective-permute-start | bytes 983048 | tf_op jit(solution)/shard_map/ppermute | solution.py:30
  60.2 4.5 %collective-permute-start.12 = (bf16[48,512]{1,0:T(8,128)(2,1)S(1)}, bf16[48,512]{1,0:T(8,128)(2,1)S(1)}, u32[]{:S(2)}, u32[]{:S(2)}) collective-permute-start(bf16[48,512]{1,0:T(8,128)(2,1)S(1)} %get-tuple-element.59), channel_id=1, source_target_pairs={{0,2},{1,3},{2,0},{3,1},{4,6},{5,7},{6,4},{7,5},{8,10},{9,11},{10,... | collective-permute-start | bytes 147464 | tf_op jit(solution)/shard_map/ppermute | solution.py:30
  61.9 5.9 %collective-permute-start.13 = (bf16[48,512]{1,0:T(8,128)(2,1)S(1)}, bf16[48,512]{1,0:T(8,128)(2,1)S(1)}, u32[]{:S(2)}, u32[]{:S(2)}) collective-permute-start(bf16[48,512]{1,0:T(8,128)(2,1)S(1)} %get-tuple-element.60), channel_id=1, source_target_pairs={{0,4},{1,5},{2,6},{3,7},{4,0},{5,1},{6,2},{7,3},{8,12},{9,13},{10,... | collective-permute-start | bytes 147464 | tf_op jit(solution)/shard_map/ppermute | solution.py:30
  64.5 5.9 %collective-permute-start.14 = (bf16[48,512]{1,0:T(8,128)(2,1)S(1)}, bf16[48,512]{1,0:T(8,128)(2,1)S(1)}, u32[]{:S(2)}, u32[]{:S(2)}) collective-permute-start(bf16[48,512]{1,0:T(8,128)(2,1)S(1)} %get-tuple-element.61), channel_id=1, source_target_pairs={{0,6},{1,7},{2,4},{3,5},{4,2},{5,3},{6,0},{7,1},{8,14},{9,15},{10,... | collective-permute-start | bytes 147464 | tf_op jit(solution)/shard_map/ppermute | solution.py:30
  71.9 2.0 %collective-permute-start.15 = (f32[4,8,4224]{2,1,0:T(8,128)S(1)}, f32[4,8,4224]{2,1,0:T(8,128)S(1)}, u32[]{:S(2)}, u32[]{:S(2)}) collective-permute-start(f32[4,8,4224]{2,1,0:T(8,128)S(1)} %get-tuple-element.67), channel_id=1, source_target_pairs={{0,1},{1,0},{2,3},{3,2},{4,5},{5,4},{6,7},{7,6},{8,9},{9,8},{10,11... | collective-permute-start | bytes 1622024 | tf_op jit(solution)/shard_map/ppermute | solution.py:30
  74.0 5.3 %collective-permute-start.16 = (bf16[8,4352]{1,0:T(8,128)(2,1)S(1)}, bf16[8,4352]{1,0:T(8,128)(2,1)S(1)}, u32[]{:S(2)}, u32[]{:S(2)}) collective-permute-start(bf16[8,4352]{1,0:T(8,128)(2,1)S(1)} %get-tuple-element.69), channel_id=1, source_target_pairs={{0,2},{1,3},{2,0},{3,1},{4,6},{5,7},{6,4},{7,5},{8,10},{9,11},{10,... | collective-permute-start | bytes 208904 | tf_op jit(solution)/shard_map/ppermute | solution.py:30
  74.0 8.9 %collective-permute-start.17 = (bf16[8,4352]{1,0:T(8,128)(2,1)S(1)}, bf16[8,4352]{1,0:T(8,128)(2,1)S(1)}, u32[]{:S(2)}, u32[]{:S(2)}) collective-permute-start(bf16[8,4352]{1,0:T(8,128)(2,1)S(1)} %get-tuple-element.70), channel_id=1, source_target_pairs={{0,4},{1,5},{2,6},{3,7},{4,0},{5,1},{6,2},{7,3},{8,12},{9,13},{10,... | collective-permute-start | bytes 208904 | tf_op jit(solution)/shard_map/ppermute | solution.py:30
  75.6 7.3 %collective-permute-start.18 = (bf16[8,4352]{1,0:T(8,128)(2,1)S(1)}, bf16[8,4352]{1,0:T(8,128)(2,1)S(1)}, u32[]{:S(2)}, u32[]{:S(2)}) collective-permute-start(bf16[8,4352]{1,0:T(8,128)(2,1)S(1)} %get-tuple-element.71), channel_id=1, source_target_pairs={{0,6},{1,7},{2,4},{3,5},{4,2},{5,3},{6,0},{7,1},{8,14},{9,15},{10,... | collective-permute-start | bytes 208904 | tf_op jit(solution)/shard_map/ppermute | solution.py:30

commit v6 on v5

--- a/solution.py
+++ b/solution.py
@@ -263,7 +263,7 @@
 def widen_centroids(place, owner_counts, gain, centroids, groups, slots):
     rows, feat = centroids.shape
     count = place.shape[1]
-    chunks = 4
+    chunks = 8
     whole = pl.BlockSpec(memory_space=pltpu.VMEM)
     scalar = pl.BlockSpec(memory_space=pltpu.SMEM)
     in_hbm = pl.BlockSpec(memory_space=pltpu.HBM)

time: 86 us -> 85.7 us (level)
  transfers between devices with their start and end apart: 19 -> 19, of which waited for: 11 -> 11; matrix products, arithmetic and copies ran while one was open for 0% -> 0% of each run, Pallas kernels for 10% -> 9%
where the time goes in v6:
time: 85.7 us; the launch traced here: 85.5 us
  Pallas kernels  34.4 us (40%)
  waiting for transfers between devices  27.4 us (32%)
  starting transfers between devices  19.1 us (22%)
  local copies, waits for them, and re-layouts  3.41 us (4%)
  between operations  1 us (1%)
    ppermute x18, waiting for transfers between devices, swapped(): return lax.ppermute(x, axis, [(i, i ^ mask) for i in range(count)])  27.4 us
    ppermute x18, starting transfers between devices, swapped(): return lax.ppermute(x, axis, [(i, i ^ mask) for i in range(count)])  17.7 us
    pallas_call x1, Pallas kernels, attend(): pl.pallas_call(body, in_specs=[pl.BlockSpec(memory_space=pltpu.SMEM), who...  17.6 us
    pallas_call x1, Pallas kernels, widen_centroids(): pl.pallas_call(body, in_specs=[scalar, scalar, whole, in_hbm], out_specs=...  5.15 us
    pallas_call x1, Pallas kernels, project_kv(): pl.pallas_call(body, in_specs=[pl.BlockSpec(memory_space=pltpu.HBM)] * 5...  3.94 us
    unnamed x16, local copies, waits for them, and re-layouts  3.41 us
    pallas_call x1, Pallas kernels, project_q(): pl.pallas_call(q_body, in_specs=[whole] * 3, out_specs=[whole, whole], ou...  2.85 us
    pallas_call x1, Pallas kernels, finish(): pl.pallas_call(body, in_specs=[scalar] + [whole] * (groups + 5) + [in_hbm...  2.7 us
  transfers between devices with their start and end apart: 19, of which 11 were waited for; matrix products, arithmetic and copies ran while one was open for 0% of the time, Pallas kernels for 9%

profile of v6, /device:TPU:0, one launch (start us, length us, event | category | flops | bytes accessed | tf_op | source)
XLA Modules:
  0.0 85.5 jit_solution(7360926365897372879)
XLA Ops:
  0.6 0.0 copy-start
  0.6 3.4 %copy-done = bf16[1024,4096]{1,0:T(8,128)(2,1)S(1)} copy-done((bf16[1024,4096]{1,0:T(8,128)(2,1)S(1)}, bf16[1024,4096]{1,0:T(8,128)(2,1)}, u32[]{:S(2)}) %copy-start) | copy-done | bytes 8388632
  4.0 0.0 copy-start.3
  4.0 0.0 copy-start.7
  4.0 0.0 copy-start.5
  4.0 0.0 copy-start.6
  4.0 3.9 %project_kv.1 = (bf16[1280,128]{1,0:T(8,128)(2,1)S(1)}, f32[2,1024,128]{2,1,0:T(8,128)S(1)}) custom-call(s32[32,128]{1,0:T(8,128)} %bitcast.11, bf16[64,4096]{1,0:T(8,128)(2,1)} %bitcast.14, bf16[64,4096]{1,0:T(8,128)(2,1)} %bitcast.15, f32[2,128,128]{2,1,0:T(8,128)} %constant.41.clone.refs_3_, f32[2,32,128]{2,1,0:T(8,128)} %constant.42.clone.refs_4_, ...), custom_call_target="tpu_custom_call" | custom-call | flops 1073741824 | bytes 8388608 | tf_op jit(solution)/shard_map/project_kv/pallas_call | solution.py:138
  8.0 0.0 copy-start.4
  8.0 0.6 collective-permute-start.4
  8.5 3.5 %collective-permute-start.3 = (bf16[1280,128]{1,0:T(8,128)(2,1)S(1)}, bf16[1280,128]{1,0:T(8,128)(2,1)S(1)}, u32[]{:S(2)}, u32[]{:S(2)}) collective-permute-start(bf16[1280,128]{1,0:T(8,128)(2,1)S(1)} %get-tuple-element.53.refs_5_), channel_id=1, source_target_pairs={{0,24},{8,16},{16,8},{24,0},{1,25},{9,17},{17,9},{25,1},{2,26},{10... | collective-permute-start | bytes 983048 | tf_op jit(solution)/shard_map/ppermute | solution.py:30
  12.0 0.5 collective-permute-start.2
  12.5 0.1 collective-permute-start.1
  12.7 0.0 copy-done.3
  12.7 2.8 %project_q.1 = (bf16[512,256]{1,0:T(8,128)(2,1)S(1)}, bf16[512,256]{1,0:T(8,128)(2,1)S(1)}) custom-call(bf16[1024,4096]{1,0:T(8,128)(2,1)S(1)} %copy-done, bf16[4096,256]{1,0:T(8,128)(2,1)S(1)} %copy-done.3, f32[2,1024,128]{2,1,0:T(8,128)S(1)} %get-tuple-element.40.tables), custom_call_target="tpu_custom_call" | custom-call | flops 2147483648 | bytes 10485760 | tf_op jit(solution)/shard_map/project_q/pallas_call | solution.py:190
  15.5 1.5 %collective-permute-start = (bf16[512,256]{1,0:T(8,128)(2,1)S(1)}, bf16[512,256]{1,0:T(8,128)(2,1)S(1)}, u32[]{:S(2)}, u32[]{:S(2)}) collective-permute-start(bf16[512,256]{1,0:T(8,128)(2,1)S(1)} %get-tuple-element.50.refs_2_), channel_id=1, source_target_pairs={{24,0},{16,8},{25,1},{17,9},{26,2},{18,10},{27,3},{19,11},{28,4},{... | collective-permute-start | bytes 786440 | tf_op jit(solution)/shard_map/ppermute | solution.py:801
  17.0 0.0 copy-done.7
  17.0 0.2 fusion.1
  17.2 3.4 %collective-permute-done.3.refs_8_ = bf16[1280,128]{1,0:T(8,128)(2,1)S(1)} collective-permute-done((bf16[1280,128]{1,0:T(8,128)(2,1)S(1)}, bf16[1280,128]{1,0:T(8,128)(2,1)S(1)}, u32[]{:S(2)}, u32[]{:S(2)}) %collective-permute-start.3) | collective-permute-done | bytes 327712 | tf_op jit(solution)/shard_map/ppermute | solution.py:30
  20.6 0.0 collective-permute-start.7
  20.6 6.9 %collective-permute-done.2.refs_7_ = bf16[1280,128]{1,0:T(8,128)(2,1)S(1)} collective-permute-done((bf16[1280,128]{1,0:T(8,128)(2,1)S(1)}, bf16[1280,128]{1,0:T(8,128)(2,1)S(1)}, u32[]{:S(2)}, u32[]{:S(2)}) %collective-permute-start.2) | collective-permute-done | bytes 327712 | tf_op jit(solution)/shard_map/ppermute | solution.py:30
  27.6 0.0 collective-permute-start.6
  27.6 0.1 collective-permute-done.1.refs_6_
  27.7 0.4 collective-permute-start.5
  28.1 0.0 copy-done.5
  28.1 0.0 copy-done.6
  28.1 5.1 %widen_centroids.1 = (f32[4096,512]{1,0:T(8,128)}, f32[8,512]{1,0:T(8,128)S(1)}, bf16[512,512]{1,0:T(8,128)(2,1)S(1)}, f32[1,512]{1,0:T(1,128)S(1)}, f32[64,32]{...) custom-call(s32[4,32]{1,0:T(4,128)S(1)} %pad_add_fusion.refs_0_, s32[8]{0:T(128)S(1)} %copy-done.6, ...), custom_call_target="tpu_custom_call" | custom-call | flops 8388608 | bytes 12582912 | tf_op jit(solution)/shard_map/widen_centroids/pallas_call | solution.py:274
  33.3 0.0 copy-start.2
  33.3 0.0 collective-permute-done.refs_4_
  33.3 0.0 copy-start.1
  33.3 0.0 collective-permute-done.4.refs_9_
  33.3 0.0 collective-permute-done.7.refs_12_
  33.3 0.0 collective-permute-done.6.refs_11_
  33.3 0.0 collective-permute-done.5.refs_10_
  33.3 0.0 copy-done.4
  33.4 17.6 %attend.1 = (f32[32,256]{1,0:T(8,128)S(1)}, f32[32,128]{1,0:T(8,128)S(1)}, f32[32,512]{1,0:T(8,128)S(1)}) custom-call(s32[4096]{0:T(1024)S(1)} %copy-done.4, s32[32,128]{1,0:T(8,128)S(1)} %bitcast.12, bf16[512,256]{1,0:T(8,128)(2,1)S(1)} %get-tuple-element.50.refs_2_, bf16[512,256]{1,0:T(8,128)(2,1)S(1)} %get-tuple-element.51.refs_3_, ...), custom_call_target="tpu_custom_call" | custom-call | flops 4294967296 | bytes 2097152 | tf_op jit(solution)/shard_map/attend/pallas_call | solution.py:502
  51.0 0.1 collective-permute-start.10
  51.0 2.8 %collective-permute-start.9 = (f32[32,256]{1,0:T(8,128)S(1)}, f32[32,256]{1,0:T(8,128)S(1)}, u32[]{:S(2)}, u32[]{:S(2)}) collective-permute-start(f32[32,256]{1,0:T(8,128)S(1)} %get-tuple-element.54.refs_0_), channel_id=1, source_target_pairs={{0,16},{8,24},{16,0},{24,8},{1,17},{9,25},{17,1},{25,9},{2,18},{10... | collective-permute-start | bytes 98312 | tf_op jit(solution)/shard_map/ppermute | solution.py:30
  53.8 0.7 collective-permute-start.8
  54.5 1.6 %collective-permute-done.10.refs_3_ = f32[32,256]{1,0:T(8,128)S(1)} collective-permute-done((f32[32,256]{1,0:T(8,128)S(1)}, f32[32,256]{1,0:T(8,128)S(1)}, u32[]{:S(2)}, u32[]{:S(2)}) %collective-permute-start.10) | collective-permute-done | bytes 32800 | tf_op jit(solution)/shard_map/ppermute | solution.py:30
  56.1 0.0 collective-permute-done.9.refs_2_
  56.1 1.6 %collective-permute-done.8.refs_1_ = f32[32,256]{1,0:T(8,128)S(1)} collective-permute-done((f32[32,256]{1,0:T(8,128)S(1)}, f32[32,256]{1,0:T(8,128)S(1)}, u32[]{:S(2)}, u32[]{:S(2)}) %collective-permute-start.8) | collective-permute-done | bytes 32800 | tf_op jit(solution)/shard_map/ppermute | solution.py:30
  57.7 0.0 copy-done.2
  57.7 0.5 mix.1
  58.2 0.0 collective-permute-start.11
  58.2 1.6 %collective-permute-done.11.refs_1_ = f32[4,40,512]{2,1,0:T(8,128)S(1)} collective-permute-done((f32[4,40,512]{2,1,0:T(8,128)S(1)}, f32[4,40,512]{2,1,0:T(8,128)S(1)}, u32[]{:S(2)}, u32[]{:S(2)}) %collective-permute-start.11) | collective-permute-done | bytes 327712 | tf_op jit(solution)/shard_map/ppermute | solution.py:30
  59.9 1.6 %collective-permute-start.12 = (bf16[48,512]{1,0:T(8,128)(2,1)S(1)}, bf16[48,512]{1,0:T(8,128)(2,1)S(1)}, u32[]{:S(2)}, u32[]{:S(2)}) collective-permute-start(bf16[48,512]{1,0:T(8,128)(2,1)S(1)} %get-tuple-element.59), channel_id=1, source_target_pairs={{0,2},{1,3},{2,0},{3,1},{4,6},{5,7},{6,4},{7,5},{8,10},{9,11},{10,... | collective-permute-start | bytes 147464 | tf_op jit(solution)/shard_map/ppermute | solution.py:30
  61.5 2.6 %collective-permute-start.13 = (bf16[48,512]{1,0:T(8,128)(2,1)S(1)}, bf16[48,512]{1,0:T(8,128)(2,1)S(1)}, u32[]{:S(2)}, u32[]{:S(2)}) collective-permute-start(bf16[48,512]{1,0:T(8,128)(2,1)S(1)} %get-tuple-element.60), channel_id=1, source_target_pairs={{0,4},{1,5},{2,6},{3,7},{4,0},{5,1},{6,2},{7,3},{8,12},{9,13},{10,... | collective-permute-start | bytes 147464 | tf_op jit(solution)/shard_map/ppermute | solution.py:30
  64.1 0.2 collective-permute-start.14
  64.4 0.0 collective-permute-done.12.refs_1_
  64.4 3.1 %collective-permute-done.13.refs_2_ = bf16[48,512]{1,0:T(8,128)(2,1)S(1)} collective-permute-done((bf16[48,512]{1,0:T(8,128)(2,1)S(1)}, bf16[48,512]{1,0:T(8,128)(2,1)S(1)}, u32[]{:S(2)}, u32[]{:S(2)}) %collective-permute-start.13) | collective-permute-done | bytes 49184 | tf_op jit(solution)/shard_map/ppermute | solution.py:30
  67.4 2.6 %collective-permute-done.14.refs_3_ = bf16[48,512]{1,0:T(8,128)(2,1)S(1)} collective-permute-done((bf16[48,512]{1,0:T(8,128)(2,1)S(1)}, bf16[48,512]{1,0:T(8,128)(2,1)S(1)}, u32[]{:S(2)}, u32[]{:S(2)}) %collective-permute-start.14) | collective-permute-done | bytes 49184 | tf_op jit(solution)/shard_map/ppermute | solution.py:30
  70.0 0.0 copy-done.1
  70.0 1.6 %cross.1 = (f32[4,8,4224]{2,1,0:T(8,128)S(1)}, f32[4,8,4224]{2,1,0:T(8,128)S(1)}, f32[32,512]{1,0:T(8,128)S(1)}, f32[8,512]{1,0:T(8,128)S(1)}) custom-call(f32[40,512]{1,0:T(8,128)S(1)} %get-tuple-element.58.refs_0_, bf16[48,512]{1,0:T(8,128)(2,1)S(1)} %collective-permute-done.12.refs_1_, bf16[48,512]{1,0:T(8,128)(2,1)S(1)} %collective-permute-done.13.refs_2_, ...), custom_call_target="tpu_custom_call" | custom-call | tf_op jit(solution)/shard_map/cross/pallas_call | solution.py:673
  71.6 0.1 collective-permute-start.15
  71.7 1.9 %collective-permute-done.15.refs_1_ = f32[4,8,4224]{2,1,0:T(8,128)S(1)} collective-permute-done((f32[4,8,4224]{2,1,0:T(8,128)S(1)}, f32[4,8,4224]{2,1,0:T(8,128)S(1)}, u32[]{:S(2)}, u32[]{:S(2)}) %collective-permute-start.15) | collective-permute-done | bytes 540704 | tf_op jit(solution)/shard_map/ppermute | solution.py:30
  73.6 0.1 fold.3
  73.6 0.1 collective-permute-start.16
  73.7 1.6 %collective-permute-start.17 = (bf16[8,4352]{1,0:T(8,128)(2,1)S(1)}, bf16[8,4352]{1,0:T(8,128)(2,1)S(1)}, u32[]{:S(2)}, u32[]{:S(2)}) collective-permute-start(bf16[8,4352]{1,0:T(8,128)(2,1)S(1)} %get-tuple-element.70), channel_id=1, source_target_pairs={{0,4},{1,5},{2,6},{3,7},{4,0},{5,1},{6,2},{7,3},{8,12},{9,13},{10,... | collective-permute-start | bytes 208904 | tf_op jit(solution)/shard_map/ppermute | solution.py:30
  75.3 2.8 %collective-permute-start.18 = (bf16[8,4352]{1,0:T(8,128)(2,1)S(1)}, bf16[8,4352]{1,0:T(8,128)(2,1)S(1)}, u32[]{:S(2)}, u32[]{:S(2)}) collective-permute-start(bf16[8,4352]{1,0:T(8,128)(2,1)S(1)} %get-tuple-element.71), channel_id=1, source_target_pairs={{0,6},{1,7},{2,4},{3,5},{4,2},{5,3},{6,0},{7,1},{8,14},{9,15},{10,... | collective-permute-start | bytes 208904 | tf_op jit(solution)/shard_map/ppermute | solution.py:30
  78.1 0.9 %collective-permute-done.16.refs_2_ = bf16[8,4352]{1,0:T(8,128)(2,1)S(1)} collective-permute-done((bf16[8,4352]{1,0:T(8,128)(2,1)S(1)}, bf16[8,4352]{1,0:T(8,128)(2,1)S(1)}, u32[]{:S(2)}, u32[]{:S(2)}) %collective-permute-start.16) | collective-permute-done | bytes 69664 | tf_op jit(solution)/shard_map/ppermute | solution.py:30
  79.0 3.7 %collective-permute-done.17.refs_3_ = bf16[8,4352]{1,0:T(8,128)(2,1)S(1)} collective-permute-done((bf16[8,4352]{1,0:T(8,128)(2,1)S(1)}, bf16[8,4352]{1,0:T(8,128)(2,1)S(1)}, u32[]{:S(2)}, u32[]{:S(2)}) %collective-permute-start.17) | collective-permute-done | bytes 69664 | tf_op jit(solution)/shard_map/ppermute | solution.py:30
  82.6 0.0 collective-permute-done.18.refs_4_
  82.6 2.7 %finish.1 = (f32[8,4096]{1,0:T(8,128)}, f32[4096,512]{1,0:T(8,128)}) custom-call(s32[4,32]{1,0:T(4,128)S(1)} %pad_add_fusion.refs_0_, f32[8,4224]{1,0:T(8,128)S(1)} %get-tuple-element.68.refs_1_, bf16[8,4352]{1,0:T(8,128)(2,1)S(1)} %collective-permute-done.16.refs_2_, ...), custom_call_target="tpu_custom_call", output_to_operand_aliasing={{1}: (10, {})} | custom-call | tf_op jit(solution)/shard_map/finish/pallas_call | solution.py:754
  (4 shorter events, 0.1 us)
Async XLA Ops:
  0.6 3.4 %copy-start = (bf16[1024,4096]{1,0:T(8,128)(2,1)S(1)}, bf16[1024,4096]{1,0:T(8,128)(2,1)}, u32[]{:S(2)}) copy-start(bf16[1024,4096]{1,0:T(8,128)(2,1)} %tok.1) | copy-start | bytes 25165828
  4.0 8.7 %copy-start.3 = (bf16[4096,256]{1,0:T(8,128)(2,1)S(1)}, bf16[4096,256]{1,0:T(8,128)(2,1)}, u32[]{:S(2)}) copy-start(bf16[4096,256]{1,0:T(8,128)(2,1)} %weight.1) | copy-start | bytes 6291460
  4.0 13.0 %copy-start.7 = (s32[32]{0:T(128)S(1)}, s32[32]{0:T(128)}, u32[]{:S(2)}) copy-start(s32[32]{0:T(128)} %param.21) | copy-start | bytes 388
  4.0 24.1 %copy-start.5 = (f32[512]{0:T(512)S(1)}, f32[512]{0:T(512)}, u32[]{:S(2)}) copy-start(f32[512]{0:T(512)} %param.20) | copy-start | bytes 6148
  4.0 24.1 %copy-start.6 = (s32[8]{0:T(128)S(1)}, s32[8]{0:T(128)}, u32[]{:S(2)}) copy-start(s32[8]{0:T(128)} %refs_1_.1) | copy-start | bytes 100
  8.0 25.4 %copy-start.4 = (s32[4096]{0:T(1024)S(1)}, s32[4096]{0:T(1024)}, u32[]{:S(2)}) copy-start(s32[4096]{0:T(1024)} %refs_0_.1) | copy-start | bytes 49156
  8.0 25.3 %collective-permute-start.4 = (bf16[1280,128]{1,0:T(8,128)(2,1)S(1)}, bf16[1280,128]{1,0:T(8,128)(2,1)S(1)}, u32[]{:S(2)}, u32[]{:S(2)}) collective-permute-start(bf16[1280,128]{1,0:T(8,128)(2,1)S(1)} %get-tuple-element.53.refs_5_), channel_id=1, source_target_pairs={{0,1},{1,0},{2,3},{3,2},{4,5},{5,4},{6,7},{7,6},{8,9},{9,8},{10,11... | collective-permute-start | bytes 983048 | tf_op jit(solution)/shard_map/ppermute | solution.py:30
  8.5 12.1 %collective-permute-start.3 = (bf16[1280,128]{1,0:T(8,128)(2,1)S(1)}, bf16[1280,128]{1,0:T(8,128)(2,1)S(1)}, u32[]{:S(2)}, u32[]{:S(2)}) collective-permute-start(bf16[1280,128]{1,0:T(8,128)(2,1)S(1)} %get-tuple-element.53.refs_5_), channel_id=1, source_target_pairs={{0,24},{8,16},{16,8},{24,0},{1,25},{9,17},{17,9},{25,1},{2,26},{10... | collective-permute-start | bytes 983048 | tf_op jit(solution)/shard_map/ppermute | solution.py:30
  12.0 15.5 %collective-permute-start.2 = (bf16[1280,128]{1,0:T(8,128)(2,1)S(1)}, bf16[1280,128]{1,0:T(8,128)(2,1)S(1)}, u32[]{:S(2)}, u32[]{:S(2)}) collective-permute-start(bf16[1280,128]{1,0:T(8,128)(2,1)S(1)} %get-tuple-element.53.refs_5_), channel_id=1, source_target_pairs={{0,16},{8,24},{16,0},{24,8},{1,17},{9,25},{17,1},{25,9},{2,18},{10... | collective-permute-start | bytes 983048 | tf_op jit(solution)/shard_map/ppermute | solution.py:30
  12.5 15.1 %collective-permute-start.1 = (bf16[1280,128]{1,0:T(8,128)(2,1)S(1)}, bf16[1280,128]{1,0:T(8,128)(2,1)S(1)}, u32[]{:S(2)}, u32[]{:S(2)}) collective-permute-start(bf16[1280,128]{1,0:T(8,128)(2,1)S(1)} %get-tuple-element.53.refs_5_), channel_id=1, source_target_pairs={{0,8},{8,0},{16,24},{24,16},{1,9},{9,1},{17,25},{25,17},{2,10},{10... | collective-permute-start | bytes 983048 | tf_op jit(solution)/shard_map/ppermute | solution.py:30
  15.5 17.8 %collective-permute-start = (bf16[512,256]{1,0:T(8,128)(2,1)S(1)}, bf16[512,256]{1,0:T(8,128)(2,1)S(1)}, u32[]{:S(2)}, u32[]{:S(2)}) collective-permute-start(bf16[512,256]{1,0:T(8,128)(2,1)S(1)} %get-tuple-element.50.refs_2_), channel_id=1, source_target_pairs={{24,0},{16,8},{25,1},{17,9},{26,2},{18,10},{27,3},{19,11},{28,4},{... | collective-permute-start | bytes 786440 | tf_op jit(solution)/shard_map/ppermute | solution.py:801
  20.6 12.7 %collective-permute-start.7 = (bf16[1280,128]{1,0:T(8,128)(2,1)S(1)}, bf16[1280,128]{1,0:T(8,128)(2,1)S(1)}, u32[]{:S(2)}, u32[]{:S(2)}) collective-permute-start(bf16[1280,128]{1,0:T(8,128)(2,1)S(1)} %collective-permute-done.3.refs_8_), channel_id=1, source_target_pairs={{0,1},{1,0},{2,3},{3,2},{4,5},{5,4},{6,7},{7,6},{8,9},{9,8},{10,11... | collective-permute-start | bytes 983048 | tf_op jit(solution)/shard_map/ppermute | solution.py:30
  27.6 5.8 %collective-permute-start.6 = (bf16[1280,128]{1,0:T(8,128)(2,1)S(1)}, bf16[1280,128]{1,0:T(8,128)(2,1)S(1)}, u32[]{:S(2)}, u32[]{:S(2)}) collective-permute-start(bf16[1280,128]{1,0:T(8,128)(2,1)S(1)} %collective-permute-done.2.refs_7_), channel_id=1, source_target_pairs={{0,1},{1,0},{2,3},{3,2},{4,5},{5,4},{6,7},{7,6},{8,9},{9,8},{10,11... | collective-permute-start | bytes 983048 | tf_op jit(solution)/shard_map/ppermute | solution.py:30
  27.7 5.7 %collective-permute-start.5 = (bf16[1280,128]{1,0:T(8,128)(2,1)S(1)}, bf16[1280,128]{1,0:T(8,128)(2,1)S(1)}, u32[]{:S(2)}, u32[]{:S(2)}) collective-permute-start(bf16[1280,128]{1,0:T(8,128)(2,1)S(1)} %collective-permute-done.1.refs_6_), channel_id=1, source_target_pairs={{0,1},{1,0},{2,3},{3,2},{4,5},{5,4},{6,7},{7,6},{8,9},{9,8},{10,11... | collective-permute-start | bytes 983048 | tf_op jit(solution)/shard_map/ppermute | solution.py:30
  33.3 24.4 %copy-start.2 = (bf16[256,4096]{1,0:T(8,128)(2,1)S(1)}, bf16[256,4096]{1,0:T(8,128)(2,1)}, u32[]{:S(2)}) copy-start(bf16[256,4096]{1,0:T(8,128)(2,1)} %refs_5_.3) | copy-start | bytes 6291460
  33.3 36.7 %copy-start.1 = (bf16[4096,512]{1,0:T(8,128)(2,1)S(1)}, bf16[4096,512]{1,0:T(8,128)(2,1)}, u32[]{:S(2)}) copy-start(bf16[4096,512]{1,0:T(8,128)(2,1)} %refs_8_.1) | copy-start | bytes 12582916
  51.0 5.1 %collective-permute-start.10 = (f32[32,256]{1,0:T(8,128)S(1)}, f32[32,256]{1,0:T(8,128)S(1)}, u32[]{:S(2)}, u32[]{:S(2)}) collective-permute-start(f32[32,256]{1,0:T(8,128)S(1)} %get-tuple-element.54.refs_0_), channel_id=1, source_target_pairs={{0,24},{8,16},{16,8},{24,0},{1,25},{9,17},{17,9},{25,1},{2,26},{10... | collective-permute-start | bytes 98312 | tf_op jit(solution)/shard_map/ppermute | solution.py:30
  51.0 5.1 %collective-permute-start.9 = (f32[32,256]{1,0:T(8,128)S(1)}, f32[32,256]{1,0:T(8,128)S(1)}, u32[]{:S(2)}, u32[]{:S(2)}) collective-permute-start(f32[32,256]{1,0:T(8,128)S(1)} %get-tuple-element.54.refs_0_), channel_id=1, source_target_pairs={{0,16},{8,24},{16,0},{24,8},{1,17},{9,25},{17,1},{25,9},{2,18},{10... | collective-permute-start | bytes 98312 | tf_op jit(solution)/shard_map/ppermute | solution.py:30
  53.8 3.9 %collective-permute-start.8 = (f32[32,256]{1,0:T(8,128)S(1)}, f32[32,256]{1,0:T(8,128)S(1)}, u32[]{:S(2)}, u32[]{:S(2)}) collective-permute-start(f32[32,256]{1,0:T(8,128)S(1)} %get-tuple-element.54.refs_0_), channel_id=1, source_target_pairs={{0,8},{8,0},{16,24},{24,16},{1,9},{9,1},{17,25},{25,17},{2,10},{10... | collective-permute-start | bytes 98312 | tf_op jit(solution)/shard_map/ppermute | solution.py:30
  58.2 1.7 %collective-permute-start.11 = (f32[4,40,512]{2,1,0:T(8,128)S(1)}, f32[4,40,512]{2,1,0:T(8,128)S(1)}, u32[]{:S(2)}, u32[]{:S(2)}) collective-permute-start(f32[4,40,512]{2,1,0:T(8,128)S(1)} %get-tuple-element.57), channel_id=1, source_target_pairs={{0,1},{1,0},{2,3},{3,2},{4,5},{5,4},{6,7},{7,6},{8,9},{9,8},{10,11... | collective-permute-start | bytes 983048 | tf_op jit(solution)/shard_map/ppermute | solution.py:30
  59.9 4.5 %collective-permute-start.12 = (bf16[48,512]{1,0:T(8,128)(2,1)S(1)}, bf16[48,512]{1,0:T(8,128)(2,1)S(1)}, u32[]{:S(2)}, u32[]{:S(2)}) collective-permute-start(bf16[48,512]{1,0:T(8,128)(2,1)S(1)} %get-tuple-element.59), channel_id=1, source_target_pairs={{0,2},{1,3},{2,0},{3,1},{4,6},{5,7},{6,4},{7,5},{8,10},{9,11},{10,... | collective-permute-start | bytes 147464 | tf_op jit(solution)/shard_map/ppermute | solution.py:30
  61.5 5.9 %collective-permute-start.13 = (bf16[48,512]{1,0:T(8,128)(2,1)S(1)}, bf16[48,512]{1,0:T(8,128)(2,1)S(1)}, u32[]{:S(2)}, u32[]{:S(2)}) collective-permute-start(bf16[48,512]{1,0:T(8,128)(2,1)S(1)} %get-tuple-element.60), channel_id=1, source_target_pairs={{0,4},{1,5},{2,6},{3,7},{4,0},{5,1},{6,2},{7,3},{8,12},{9,13},{10,... | collective-permute-start | bytes 147464 | tf_op jit(solution)/shard_map/ppermute | solution.py:30
  64.1 5.9 %collective-permute-start.14 = (bf16[48,512]{1,0:T(8,128)(2,1)S(1)}, bf16[48,512]{1,0:T(8,128)(2,1)S(1)}, u32[]{:S(2)}, u32[]{:S(2)}) collective-permute-start(bf16[48,512]{1,0:T(8,128)(2,1)S(1)} %get-tuple-element.61), channel_id=1, source_target_pairs={{0,6},{1,7},{2,4},{3,5},{4,2},{5,3},{6,0},{7,1},{8,14},{9,15},{10,... | collective-permute-start | bytes 147464 | tf_op jit(solution)/shard_map/ppermute | solution.py:30
  71.6 2.0 %collective-permute-start.15 = (f32[4,8,4224]{2,1,0:T(8,128)S(1)}, f32[4,8,4224]{2,1,0:T(8,128)S(1)}, u32[]{:S(2)}, u32[]{:S(2)}) collective-permute-start(f32[4,8,4224]{2,1,0:T(8,128)S(1)} %get-tuple-element.67), channel_id=1, source_target_pairs={{0,1},{1,0},{2,3},{3,2},{4,5},{5,4},{6,7},{7,6},{8,9},{9,8},{10,11... | collective-permute-start | bytes 1622024 | tf_op jit(solution)/shard_map/ppermute | solution.py:30
  73.6 5.3 %collective-permute-start.16 = (bf16[8,4352]{1,0:T(8,128)(2,1)S(1)}, bf16[8,4352]{1,0:T(8,128)(2,1)S(1)}, u32[]{:S(2)}, u32[]{:S(2)}) collective-permute-start(bf16[8,4352]{1,0:T(8,128)(2,1)S(1)} %get-tuple-element.69), channel_id=1, source_target_pairs={{0,2},{1,3},{2,0},{3,1},{4,6},{5,7},{6,4},{7,5},{8,10},{9,11},{10,... | collective-permute-start | bytes 208904 | tf_op jit(solution)/shard_map/ppermute | solution.py:30
  73.7 8.9 %collective-permute-start.17 = (bf16[8,4352]{1,0:T(8,128)(2,1)S(1)}, bf16[8,4352]{1,0:T(8,128)(2,1)S(1)}, u32[]{:S(2)}, u32[]{:S(2)}) collective-permute-start(bf16[8,4352]{1,0:T(8,128)(2,1)S(1)} %get-tuple-element.70), channel_id=1, source_target_pairs={{0,4},{1,5},{2,6},{3,7},{4,0},{5,1},{6,2},{7,3},{8,12},{9,13},{10,... | collective-permute-start | bytes 208904 | tf_op jit(solution)/shard_map/ppermute | solution.py:30
  75.3 7.3 %collective-permute-start.18 = (bf16[8,4352]{1,0:T(8,128)(2,1)S(1)}, bf16[8,4352]{1,0:T(8,128)(2,1)S(1)}, u32[]{:S(2)}, u32[]{:S(2)}) collective-permute-start(bf16[8,4352]{1,0:T(8,128)(2,1)S(1)} %get-tuple-element.71), channel_id=1, source_target_pairs={{0,6},{1,7},{2,4},{3,5},{4,2},{5,3},{6,0},{7,1},{8,14},{9,15},{10,... | collective-permute-start | bytes 208904 | tf_op jit(solution)/shard_map/ppermute | solution.py:30
